TPU v7x, 32 devices: a whole 2x2x4 slice. The times are simulated.
32 devices in a mesh: groups: 2 (over y), wide: 4 (over z), narrow: 4 (over x, core).
Axes of the slice: x: 2, y: 2, z: 4, core: 2. Of those that a mesh axis runs over, the one named last changes fastest.
Arguments:
- generator: int32 [8192], P('narrow'), may hold values from 1 to 511
- lattice_shift: int32 [16384], P(('groups', 'narrow')), parts along dimension 0, may hold values from 0 to 1023
- loadings: bfloat16 [512, 4, 64, 128], P(('groups', 'wide')), parts along dimension 0, may hold values from -0.375 to 0.375
- load_pattern: int32 [512, 4], P(('groups', 'wide')), parts along dimension 0, may hold values from 0 to 127
- threshold: float32 [65536], P(('groups', 'wide')), parts along dimension 0, may hold values from -2.5 to -0.5
- exposure: float32 [65536], P(('groups', 'wide')), parts along dimension 0, may hold values from 0.1 to 2
- segment_map: int32 [65536], P(('groups', 'wide')), parts along dimension 0, may hold values from 0 to 4095, as said below
- net_tiles: bfloat16 [64, 8, 128, 128], P(('groups', 'wide')), parts along dimension 0, may hold values from -0.1875 to 0.1875
- net_pattern: int32 [64, 8], P(('groups', 'wide')), parts along dimension 0, may hold values from 0 to 7
Outputs:
- net_loss: float32 [512, 8192], P('narrow', ('groups', 'wide')), parts along dimension 1
- moments: float32 [2, 8192], P(None, ('groups', 'wide')), parts along dimension 1
There are 2 independent parts, one for each index of `groups`. A program takes and returns all parts, laid end to end along the dimension named above; an argument that names none is the same for every part. Nothing has to cross between parts.
Inputs may be any that keep to these rules, and one draw needn't show every extreme that they name: `segment_map`: in each aligned block of 8192 obligors at most 3072 map to the same group of 1024 consecutive segments; one group receives exactly 3072 obligors from every block.
All inputs are finite; a program needn't handle non-finite values.
Results may differ from a plain program's by a relative error of at most 0.0036.
Values may be sent and summed in bfloat16 or wider, within the bound.
No kernel may reach another device: no remote copies, remote signals or barrier semaphores. Data moves between devices by JAX's collectives and lax.ppermute only.
A program may use at most 64 MiB of HBM per device.

v0:
```python
import jax
import jax.numpy as jnp
from jax import lax
from jax.sharding import PartitionSpec as P

P_SIZE = 512
SEG_DEV = 1024


def normal_cdf(values):
    return 0.5 * lax.erfc(-values * 0.7071067811865476)


def normal_quantile(values):
    return 1.4142135623730951 * lax.erf_inv(2.0 * values - 1.0)


def normal_points(count, generator, lattice_shift):
    points = jnp.arange(count, dtype=jnp.int32)
    residue = points[:, None] * generator[None, :] % P_SIZE
    offset = (lattice_shift.astype(jnp.float32) + 0.5) / 1024.0
    uniform = (residue.astype(jnp.float32) + offset[None, :]) / P_SIZE
    return normal_quantile(uniform).astype(jnp.bfloat16)


def body(
    generator,
    lattice_shift,
    loadings,
    load_pattern,
    threshold,
    exposure,
    segment_map,
    net_tiles,
    net_pattern,
):
    narrow_size = lax.axis_size("narrow")
    local_points = P_SIZE // narrow_size
    panel = normal_points(P_SIZE, generator, lattice_shift)
    factors = lax.all_to_all(panel, "narrow", split_axis=0, concat_axis=1, tiled=True)
    factor_width = factors.shape[1]
    factor_tiles = factors.T.reshape(factor_width // 64, 64, local_points)
    picked = factor_tiles[load_pattern]
    latent = jnp.einsum("bkfp,bkfi->pbi", picked, loadings, preferred_element_type=jnp.float32)
    latent = latent.reshape(local_points, -1)
    default_prob = normal_cdf(threshold[None, :] - latent)
    weighted = (exposure[None, :] * default_prob).astype(jnp.bfloat16)
    by_row = weighted.T
    groups = lax.axis_size("wide")
    partial_sums = jax.ops.segment_sum(
        by_row.astype(jnp.float32), segment_map, num_segments=groups * SEG_DEV
    )
    seg_loss = lax.psum_scatter(partial_sums, "wide", scatter_dimension=0, tiled=True)
    loss_blocks = seg_loss.astype(jnp.bfloat16).reshape(-1, 128, local_points)
    gathered = loss_blocks[net_pattern]
    netted = jnp.einsum("bkjp,bkji->pbi", gathered, net_tiles, preferred_element_type=jnp.float32)
    netted = netted.reshape(local_points, -1)
    first_sum, second_sum = lax.psum(
        (jnp.sum(netted, axis=0), jnp.sum(netted * netted, axis=0)), "narrow"
    )
    moments = jnp.stack([first_sum, second_sum]) / P_SIZE
    return (netted, moments)


def solution(mesh):
    return jax.shard_map(
        body,
        mesh=mesh,
        in_specs=(
            P("narrow"),
            P(("groups", "narrow")),
            P(("groups", "wide"), None, None, None),
            P(("groups", "wide"), None),
            P(("groups", "wide")),
            P(("groups", "wide")),
            P(("groups", "wide")),
            P(("groups", "wide"), None, None, None),
            P(("groups", "wide"), None),
        ),
        out_specs=(P("narrow", ("groups", "wide")), P(None, ("groups", "wide"))),
        check_vma=False,
    )
```

profile of v0, /device:TPU:0, one launch (start us, length us, event | category | flops | bytes accessed | tf_op | source)
XLA Modules:
  0.0 184.4 jit_solution(4201307887410369890)
XLA Ops:
  7.2 0.0 copy-start
  7.2 0.0 copy-start.4
  7.2 0.0 copy-start.2
  7.2 0.8 add_multiply_fusion
  8.1 12.4 %multiply_convert_fusion = bf16[4,128,2048]{1,2,0:T(8,128)(2,1)} fusion(f32[2048]{0:T(1024)S(1)} %add_multiply_fusion, s32[2048]{0:T(1024)} %param.9, s32[4,128]{1,0:T(4,128)S(1)} %multiply_add_fusion), kind=kLoop, calls=%fused_computation.38 | loop fusion | flops 57671680 | bytes 2115584 | tf_op jit(solution)/shard_map/convert_element_type | solution.py:23
  20.4 4.4 %all-to-all-start = ((bf16[4,128,2048]{1,2,0:T(8,128)(2,1)}), bf16[4,128,2048]{1,2,0:T(8,128)(2,1)}, u32[]{:S(2)}, u32[]{:S(2)}) async-start(bf16[4,128,2048]{1,2,0:T(8,128)(2,1)} %multiply_convert_fusion), calls=%async_computation | async-start | bytes 4194304 | tf_op jit(solution)/shard_map/all_to_all | solution.py:40
  24.9 0.0 reduce-scatter.2.cloned.1.call-start
  24.9 0.0 copy-done.4
  25.0 0.1 copy.13
  25.1 0.1 reshape.52
  25.2 0.0 copy-done.2
  25.2 26.1 %all-to-all-done = bf16[4,128,2048]{1,2,0:T(8,128)(2,1)} async-done(((bf16[4,128,2048]{1,2,0:T(8,128)(2,1)}), bf16[4,128,2048]{1,2,0:T(8,128)(2,1)}, u32[]{:S(2)}, u32[]{:S(2)}) %all-to-all-start) | async-done | bytes 2097184 | tf_op jit(solution)/shard_map/all_to_all | solution.py:40
  51.3 4.6 %gather_fusion = bf16[256,64,128]{2,1,0:T(8,128)(2,1)} fusion(bf16[128,64,128]{2,1,0:T(8,128)(2,1)} %bitcast.3, s32[1024]{0:T(1024)S(1)} %pad_clamp_fusion.1), kind=kCustom, calls=%fused_computation | custom fusion | bytes 8389632 | tf_op jit(solution)/shard_map/gather | solution.py:43
  55.9 0.0 copy-start.1
  55.9 4.8 %fusion.24 = f32[64,128,128,1]{1,2,3,0:T(8,128)S(1)} fusion(bf16[64,4,64,128]{3,2,1,0:T(8,128)(2,1)} %bitcast.43, bf16[64,4,64,128]{3,2,1,0:T(8,128)(2,1)} %param.11), kind=kOutput, calls=%fused_computation.54 | convolution fusion | flops 536870912 | bytes 12582912 | tf_op jit(solution)/shard_map/bkfp,bkfi->pbi/dot_general | solution.py:44
  60.7 0.0 copy-done.1
  60.7 11.9 %fusion.8 = bf16[128,8192]{0,1:T(8,128)(2,1)} fusion(f32[64,128,128,1]{1,2,3,0:T(8,128)S(1)} %fusion.24, f32[8192]{0:T(1024)S(1)} %broadcast_multiply_fusion, f32[8192]{0:T(1024)S(1)} %copy-done.1), kind=kLoop, calls=%fused_computation.18 | loop fusion | flops 68157440 | bytes 6356992 | tf_op jit(solution)/shard_map/convert_element_type | solution.py:47
  72.6 0.0 copy-start.3
  72.6 46.0 %scatter_custom_fusion = f32[4096,128]{1,0:T(8,128)} fusion(s32[8192]{0:T(1024)} %param.15, bf16[128,8192]{0,1:T(8,128)(2,1)} %fusion.8, f32[]{:T(128)} %constant.62.clone.1), kind=kCustom, calls=%fused_computation.23 | custom fusion | flops 2097152 | bytes 4194816 | tf_op jit(solution)/shard_map/scatter-add | solution.py:50
  118.5 0.0 reduce-scatter.2.cloned.1.call-update
  118.6 0.0 copy-done.3
  118.6 0.1 reshape.60
  118.7 45.0 %reduce-scatter.2.cloned.1.call-done = f32[1024,128]{1,0:T(8,128)} async-done(((f32[4096,128]{1,0:T(8,128)}), f32[1024,128]{1,0:T(8,128)}) %reduce-scatter.2.cloned.1.call-update) | async-done | bytes 524304 | tf_op jit(solution)/shard_map/reduce_scatter | solution.py:53
  163.7 1.1 convert_element_type.29
  164.8 2.2 %gather_fusion.1 = bf16[64,128,128]{2,1,0:T(8,128)(2,1)} fusion(bf16[8,128,128]{2,1,0:T(8,128)(2,1)S(1)} %bitcast.42, s32[1024]{0:T(1024)S(1)} %pad_clamp_fusion), kind=kCustom, calls=%fused_computation.1 | custom fusion | bytes 4194560 | tf_op jit(solution)/shard_map/gather | solution.py:55
  167.0 0.0 copy-done
  167.0 2.5 %bitcast_reduce_fusion = (f32[8,128]{1,0:T(8,128)S(1)}, f32[8,128]{1,0:T(8,128)S(1)}, f32[8,128,128,1]{1,2,3,0:T(8,128)S(1)}) fusion(bf16[8,8,128,128]{3,2,1,0:T(8,128)(2,1)} %bitcast.44, bf16[8,8,128,128]{3,2,1,0:T(8,128)(2,1)S(1)} %copy-done), kind=kOutput, calls=%fused_computation.43 | convolution fusion | flops 268826624 | bytes 4726784 | tf_op jit(solution)/shard_map/bkjp,bkji->pbi/dot_general | solution.py:56
  169.5 1.0 copy.15
  170.5 6.5 %all-reduce = (f32[1,1024]{1,0:T(1,128)S(1)}, f32[1,1024]{1,0:T(1,128)S(1)}) all-reduce(f32[1,1024]{1,0:T(1,128)S(1)} %bitcast.47, f32[1,1024]{1,0:T(1,128)S(1)} %bitcast.46), channel_id=1, replica_groups=mesh['groups'=2,'wide'=4,'narrow'=4] {'narrow'}, use_global_device_ids=true, to_apply=%region_5.6 | all-reduce | flops 2048 | bytes 16384 | tf_op jit(solution)/shard_map/psum | solution.py:58
  177.0 0.6 maximum_multiply_fusion
  (6 shorter events, 0.0 us)
Async XLA Ops:
  7.2 159.8 %copy-start = (bf16[8,8,128,128]{3,2,1,0:T(8,128)(2,1)S(1)}, bf16[8,8,128,128]{3,2,1,0:T(8,128)(2,1)}, u32[]{:S(2)}) copy-start(bf16[8,8,128,128]{3,2,1,0:T(8,128)(2,1)} %param.16) | copy-start | bytes 6291460
  7.2 17.8 %copy-start.4 = (s32[64,4]{0,1:T(4,128)S(1)}, s32[64,4]{0,1:T(4,128)}, u32[]{:S(2)}) copy-start(s32[64,4]{0,1:T(4,128)} %param.12) | copy-start | bytes 3076
  7.2 18.0 %copy-start.2 = (f32[8192]{0:T(1024)S(1)}, f32[8192]{0:T(1024)}, u32[]{:S(2)}) copy-start(f32[8192]{0:T(1024)} %param.14) | copy-start | bytes 98308
  20.4 30.8 %all-to-all-start = ((bf16[4,128,2048]{1,2,0:T(8,128)(2,1)}), bf16[4,128,2048]{1,2,0:T(8,128)(2,1)}, u32[]{:S(2)}, u32[]{:S(2)}) async-start(bf16[4,128,2048]{1,2,0:T(8,128)(2,1)} %multiply_convert_fusion), calls=%async_computation | async-start | bytes 4194304 | tf_op jit(solution)/shard_map/all_to_all | solution.py:40
  24.9 138.8 %reduce-scatter.2.cloned.1.call-start = ((), (), s32[]{:S(2)}) async-start(), calls=%async_computation.2 | async-start | bytes 2621440 | tf_op jit(solution)/shard_map/reduce_scatter | solution.py:53
  55.9 4.8 %copy-start.1 = (f32[8192]{0:T(1024)S(1)}, f32[8192]{0:T(1024)}, u32[]{:S(2)}) copy-start(f32[8192]{0:T(1024)} %param.13) | copy-start | bytes 98308
  72.6 46.0 %copy-start.3 = (s32[8,8]{1,0:T(8,128)S(1)}, s32[8,8]{1,0:T(8,128)}, u32[]{:S(2)}) copy-start(s32[8,8]{1,0:T(8,128)} %param.17) | copy-start | bytes 772
Sparse Core Ops, SparseCore 0:
  118.7 44.9 reduce-scatter.1
where the time goes:
time: 185 us; the launch traced here: 184 us
  other arithmetic  72.8 us (39%)
  waiting for transfers between devices  71.1 us (38%)
  between operations  14.2 us (8%)
  local copies, waits for them, and re-layouts  8.08 us (4%)
  matrix products  7.29 us (4%)
  blocking collectives  6.49 us (4%)
  starting transfers between devices  4.48 us (2%)
    scatter-add x1, other arithmetic, body(): jax.ops.segment_sum(by_row.astype(jnp.float32), segment_map, num_segments...  46 us
    reduce_scatter x1, waiting for transfers between devices, body(): lax.psum_scatter(partial_sums, 'wide', scatter_dimension=0, tiled=True)  45 us
    all_to_all x1, waiting for transfers between devices, body(): lax.all_to_all(panel, 'narrow', split_axis=0, concat_axis=1, tiled=True)  26.1 us
    convert_element_type x1, other arithmetic, normal_points(): return normal_quantile(uniform).astype(jnp.bfloat16)  12.4 us
    convert_element_type x1, other arithmetic, body(): weighted = (exposure[None, :] * default_prob).astype(jnp.bfloat16)  11.9 us
    psum x1, blocking collectives, body(): lax.psum((jnp.sum(netted, axis=0), jnp.sum(netted * netted, axis=0)), 'na...  6.49 us
    dot_general x1, matrix products, body(): jnp.einsum('bkfp,bkfi->pbi', picked, loadings, preferred_element_type=jnp...  4.77 us
    gather x1, local copies, waits for them, and re-layouts, body(): picked = factor_tiles[load_pattern]  4.61 us
  transfers between devices with their start and end apart: 2, of which 2 were waited for; matrix products, arithmetic and copies ran while one was open for 0% of the time, Pallas kernels for 0%

commit v1 on v0

v1 whole, which is shorter than its diff:
```python
import functools

import jax
import jax.numpy as jnp
from jax import lax
from jax.experimental import pallas as pl
from jax.experimental.pallas import tpu as pltpu
from jax.sharding import PartitionSpec as P

P_SIZE = 512
LANES = 128
ROWS = 16
STEP_BLOCKS = 8
DEST_CHUNK = 4

QUANTILE_MID = 2.6095163822174072
QUANTILE = (
    2.883376121520996,
    1.5978178977966309,
    0.023873422294855118,
    -0.0908193290233612,
    0.0662941262125969,
    -0.010339167900383472,
    -0.019267892464995384,
    0.011844170279800892,
    0.003007495542988181,
    -0.004063245374709368,
    -0.00016578214126639068,
    0.0005968576297163963,
)
CDF_SHIFT = 3.0
CDF_MID = 0.1666666716337204
CDF = (
    0.729083776473999,
    3.0559914112091064,
    8.280515670776367,
    10.208822250366211,
    -13.521076202392578,
    -54.16969680786133,
    43.550254821777344,
    285.4417419433594,
    -214.20135498046875,
    -1204.82958984375,
)
HALF_LOG2E = 0.7213475204444817


def horner(coefs, x):
    total = coefs[-1]
    for coef in coefs[-2::-1]:
        total = total * x + coef
    return total


def quantile(scaled):
    x = scaled.astype(jnp.float32) * (2.0**-31)
    s = 2.0 - jnp.log(1.0 - x * x)
    y = s * lax.rsqrt(s)
    return x * horner(QUANTILE, y - QUANTILE_MID)


def weighted_prob(t, exposure):
    y = jnp.abs(t)
    r = lax.rsqrt(y + CDF_SHIFT)
    q = r * r
    tail = jnp.exp2(t * t * -HALF_LOG2E) * q * horner(CDF, q - CDF_MID)
    return exposure * jnp.where(t > 0.0, 1.0 - tail, tail)


def loss_kernel(n_parts, n_dest, split, meta, pattern, *refs):
    parts = refs[:n_parts]
    load_ref, thr_ref, expo_ref, seg_ref = refs[n_parts : n_parts + 4]
    outs = refs[n_parts + 4 : -5]
    panel, acc, weighted, masked, onehot = refs[-5:]
    points = acc.shape[1]
    seg_dev = acc.shape[2]
    step = pl.program_id(0)
    width = parts[0].shape[1]
    columns = width // LANES

    @pl.when(step == 0)
    def _():
        acc[...] = jnp.zeros_like(acc)
        row = lax.broadcasted_iota(jnp.int32, (ROWS, LANES), 0) + meta[0]

        for k in range(n_parts):
            first = meta[2 + k] * columns

            def fill(c, carry, k=k, first=first):
                at = pl.ds(pl.multiple_of(c * LANES, LANES), LANES)
                gen = parts[k][0:1, at]
                shift = parts[k][1:2, at]
                scaled = lax.shift_left(row * gen, 23) + (lax.shift_left(shift, 13) + (4096 - 2**31))
                jump = lax.shift_left(gen, 27)
                for r in range(points // ROWS):
                    value = quantile(scaled)
                    rows = pl.ds(r * ROWS, ROWS)
                    panel[0, first + c, rows, :] = value.astype(jnp.bfloat16)
                    panel[1, first + c, rows, :] = pltpu.roll(value, LANES // 2, 1).astype(jnp.bfloat16)
                    scaled = scaled + jump
                return carry

            lax.fori_loop(0, columns, fill, 0)

    low = lax.broadcasted_iota(jnp.int32, (points, LANES), 1) < LANES // 2
    seg_row = lax.broadcasted_iota(jnp.int32, (seg_dev, LANES), 0)

    def rel_dest(seg):
        dest = lax.shift_right_logical(seg, seg_dev.bit_length() - 1) - meta[1]
        return jnp.where(dest < 0, dest + n_dest, dest)

    for j in range(STEP_BLOCKS):
        b = step * STEP_BLOCKS + j
        here = slice(j * LANES, (j + 1) * LANES)
        halves = []
        for k in (0, 2):
            q0 = pattern[4 * b + k]
            q1 = pattern[4 * b + k + 1]
            left = panel[q0 & 1, lax.shift_right_logical(q0, 1)]
            right = panel[1 - (q1 & 1), lax.shift_right_logical(q1, 1)]
            halves.append(jnp.where(low, left, right))
        picked = jnp.concatenate(halves, axis=1)
        latent = jnp.dot(picked, load_ref[j], preferred_element_type=jnp.float32)
        one = pl.ds(b, 1)
        prob = weighted_prob(thr_ref[one, :] - latent, expo_ref[one, :])
        weighted[:, here] = prob.astype(jnp.bfloat16)
        local = seg_ref[one, :] & (seg_dev - 1)
        onehot[:, here] = jnp.where(seg_row == local, 1.0, 0.0).astype(jnp.bfloat16)

    def add_chunk(chunk):
        for j in range(STEP_BLOCKS):
            here = slice(j * LANES, (j + 1) * LANES)
            dest = rel_dest(seg_ref[pl.ds(step * STEP_BLOCKS + j, 1), :])
            for d in range(split):
                mine = jnp.where(dest == chunk * split + d, 1.0, 0.0).astype(jnp.bfloat16)
                masked[d * points : (d + 1) * points, here] = weighted[:, here] * mine
        sums = lax.dot_general(
            masked[...], onehot[...], (((1,), (1,)), ((), ())), preferred_element_type=jnp.float32
        )
        for d in range(split):
            acc[chunk * split + d] += sums[d * points : (d + 1) * points]

    if n_dest == split:
        add_chunk(0)
    else:
        lax.fori_loop(0, n_dest // split, lambda c, x: (add_chunk(c), x)[1], 0)

    @pl.when(step == pl.num_programs(0) - 1)
    def _():
        for d in range(n_dest):
            if len(outs) == 1:
                outs[0][d] = acc[d].astype(jnp.bfloat16)
            else:
                outs[d][...] = acc[d].astype(jnp.bfloat16)


def net_kernel(pattern, *refs):
    tiles_ref, net_ref, sums_ref, losses = refs[-4:]
    received = refs[:-4]
    blocks = tiles_ref.shape[0]
    slots = tiles_ref.shape[1] // LANES
    for q in range(blocks):
        at = slice(q * LANES, (q + 1) * LANES)
        if len(received) == 1:
            total = jnp.sum(received[0][:, :, at].astype(jnp.float32), axis=0)
        else:
            total = received[0][:, at].astype(jnp.float32)
            for ref in received[1:]:
                total = total + ref[:, at].astype(jnp.float32)
        losses[q] = total.astype(jnp.bfloat16)
    for b in range(blocks):
        at = slice(b * LANES, (b + 1) * LANES)
        picked = jnp.concatenate([losses[pattern[slots * b + k]] for k in range(slots)], axis=1)
        net = jnp.dot(picked, tiles_ref[b], preferred_element_type=jnp.float32)
        net_ref[:, at] = net
        sums_ref[0:1, at] = jnp.sum(net, axis=0, keepdims=True)
        sums_ref[1:2, at] = jnp.sum(net * net, axis=0, keepdims=True)


def shifted(x, axis, k):
    n = lax.axis_size(axis)
    return lax.ppermute(x, axis, [(i, (i + k) % n) for i in range(n)])


def swapped(x, axis, k):
    return lax.ppermute(x, axis, [(i, i ^ k) for i in range(lax.axis_size(axis))])


def pair_sum(terms):
    while len(terms) > 1:
        terms = [terms[i] + terms[i + 1] for i in range(0, len(terms), 2)]
    return terms[0]


def body(
    generator,
    lattice_shift,
    loadings,
    load_pattern,
    threshold,
    exposure,
    segment_map,
    net_tiles,
    net_pattern,
):
    n_narrow = lax.axis_size("narrow")
    n_dest = lax.axis_size("wide")
    me = lax.axis_index("narrow")
    points = P_SIZE // n_narrow
    blocks = loadings.shape[0]
    seg_blocks = net_tiles.shape[0]
    seg_dev = seg_blocks * LANES
    direct = n_dest <= 8
    split = min(n_dest, DEST_CHUNK)

    own = jnp.stack([generator, lattice_shift])
    parts = [own] + [swapped(own, "narrow", k) for k in range(1, n_narrow)]
    quarter = [me ^ k for k in range(n_narrow)]
    base = lax.axis_index("wide") if direct else 0
    meta = jnp.stack([me * points, jnp.int32(base)] + quarter).astype(jnp.int32)

    block = jax.ShapeDtypeStruct((points, seg_dev), jnp.bfloat16)
    whole = lambda *shape: pl.BlockSpec(shape, lambda s, *_: (0,) * len(shape))
    if direct:
        out_shape = [block] * n_dest
        out_specs = [whole(points, seg_dev)] * n_dest
    else:
        out_shape = [jax.ShapeDtypeStruct((n_dest, points, seg_dev), jnp.bfloat16)]
        out_specs = [whole(n_dest, points, seg_dev)]
    step_width = STEP_BLOCKS * LANES
    partial = pl.pallas_call(
        functools.partial(loss_kernel, n_narrow, n_dest, split),
        out_shape=out_shape,
        grid_spec=pltpu.PrefetchScalarGridSpec(
            num_scalar_prefetch=2,
            grid=(blocks // STEP_BLOCKS,),
            in_specs=[whole(*own.shape)] * n_narrow
            + [pl.BlockSpec((STEP_BLOCKS, 256, LANES), lambda s, *_: (s, 0, 0))]
            + [whole(blocks, LANES)] * 3,
            out_specs=out_specs,
            scratch_shapes=[
                pltpu.VMEM((2, own.shape[1] * n_narrow // LANES, points, LANES), jnp.bfloat16),
                pltpu.VMEM((n_dest, points, seg_dev), jnp.float32),
                pltpu.VMEM((points, step_width), jnp.bfloat16),
                pltpu.VMEM((split * points, step_width), jnp.bfloat16),
                pltpu.VMEM((seg_dev, step_width), jnp.bfloat16),
            ],
        ),
        compiler_params=pltpu.CompilerParams(vmem_limit_bytes=60 << 20),
        name="loss",
    )(
        meta,
        load_pattern.reshape(-1),
        *parts,
        loadings.reshape(blocks, 256, LANES),
        threshold.reshape(blocks, LANES),
        exposure.reshape(blocks, LANES),
        segment_map.reshape(blocks, LANES),
    )

    if direct:
        received = [partial[0]] + [shifted(partial[k], "wide", k) for k in range(1, n_dest)]
        received_specs = [pl.BlockSpec(memory_space=pltpu.VMEM)] * n_dest
    else:
        received = [lax.all_to_all(partial[0], "wide", split_axis=0, concat_axis=0, tiled=True)]
        received_specs = [pl.BlockSpec(memory_space=pltpu.VMEM)]
    slots = net_tiles.shape[1]
    net_loss, sums = pl.pallas_call(
        net_kernel,
        out_shape=[
            jax.ShapeDtypeStruct((points, seg_dev), jnp.float32),
            jax.ShapeDtypeStruct((2, seg_dev), jnp.float32),
        ],
        in_specs=[pl.BlockSpec(memory_space=pltpu.SMEM)]
        + received_specs
        + [pl.BlockSpec(memory_space=pltpu.VMEM)],
        out_specs=[pl.BlockSpec(memory_space=pltpu.VMEM)] * 2,
        scratch_shapes=[pltpu.VMEM((seg_blocks, points, LANES), jnp.bfloat16)],
        compiler_params=pltpu.CompilerParams(vmem_limit_bytes=40 << 20),
        name="net",
    )(net_pattern.reshape(-1), *received, net_tiles.reshape(seg_blocks, slots * LANES, LANES))

    total = pair_sum([sums] + [swapped(sums, "narrow", k) for k in range(1, n_narrow)])
    return (net_loss, total / P_SIZE)


def solution(mesh):
    return jax.shard_map(
        body,
        mesh=mesh,
        in_specs=(
            P("narrow"),
            P(("groups", "narrow")),
            P(("groups", "wide"), None, None, None),
            P(("groups", "wide"), None),
            P(("groups", "wide")),
            P(("groups", "wide")),
            P(("groups", "wide")),
            P(("groups", "wide"), None, None, None),
            P(("groups", "wide"), None),
        ),
        out_specs=(P("narrow", ("groups", "wide")), P(None, ("groups", "wide"))),
        check_vma=False,
    )
```

time: 185 us -> 74.6 us (0.40)
  the two profiles are of different devices: /device:TPU:0 before, /device:TPU:8 now
where the time goes in v1:
time: 74.6 us; the launch traced here: 74.4 us
  Pallas kernels  35.6 us (48%)
  waiting for transfers between devices  24.5 us (33%)
  starting transfers between devices  8.41 us (11%)
  local copies, waits for them, and re-layouts  3.74 us (5%)
  other arithmetic  1.49 us (2%)
    pallas_call x1, Pallas kernels, body(): pl.pallas_call(functools.partial(loss_kernel, n_narrow, n_dest, split), o...  33.4 us
    ppermute x3, waiting for transfers between devices, shifted(): return lax.ppermute(x, axis, [(i, (i + k) % n) for i in range(n)])  21 us
    ppermute x3, starting transfers between devices, shifted(): return lax.ppermute(x, axis, [(i, (i + k) % n) for i in range(n)])  4.63 us
    ppermute x6, starting transfers between devices, swapped(): lax.ppermute(x, axis, [(i, i ^ k) for i in range(lax.axis_size(axis))])  3.79 us
    ppermute x6, waiting for transfers between devices, swapped(): lax.ppermute(x, axis, [(i, i ^ k) for i in range(lax.axis_size(axis))])  3.5 us
    unnamed x15, local copies, waits for them, and re-layouts  2.33 us
    pallas_call x1, Pallas kernels, body(): pl.pallas_call(net_kernel, out_shape=[jax.ShapeDtypeStruct((points, seg_d...  2.2 us
  transfers between devices with their start and end apart: 9, of which 6 were waited for; matrix products, arithmetic and copies ran while one was open for 3% of the time, Pallas kernels for 0%

profile of v1, /device:TPU:8, one launch (start us, length us, event | category | flops | bytes accessed | tf_op | source)
XLA Modules:
  0.0 74.4 jit_solution(9179286977571022346)
XLA Ops:
  0.6 0.0 copy-start.6
  0.6 0.0 copy-start
  0.7 0.9 %pad_add_fusion.refs_0_ = s32[2,2048]{1,0:T(2,128)S(1)} fusion(s32[1,2048]{1,0:T(1,128)} %bitcast.18, s32[1,2048]{1,0:T(1,128)} %bitcast.19), kind=kLoop, calls=%fused_computation | loop fusion | flops 4096 | bytes 32768 | tf_op jit(solution)/shard_map/stack | solution.py:216
  1.5 0.0 copy-start.2
  1.5 1.0 %collective-permute-start.2 = (s32[2,2048]{1,0:T(2,128)S(1)}, s32[2,2048]{1,0:T(2,128)S(1)}, u32[]{:S(2)}, u32[]{:S(2)}) collective-permute-start(s32[2,2048]{1,0:T(2,128)S(1)} %pad_add_fusion.refs_0_), channel_id=1, source_target_pairs={{0,3},{1,2},{2,1},{3,0},{4,7},{5,6},{6,5},{7,4},{8,11},{9,10},{10,... | collective-permute-start | bytes 49160 | tf_op jit(solution)/shard_map/ppermute | solution.py:186
  2.5 0.6 collective-permute-start.1
  3.2 0.3 collective-permute-start
  3.5 0.8 %copy.11 = s32[64,4]{1,0:T(8,128)S(1)} copy(s32[64,4]{0,1:T(4,128)} %param.12) | data formatting | bytes 2048 | tf_op args[3]
  4.2 0.7 reshape.26.pattern
  4.9 0.7 stack.36.meta
  5.6 0.0 collective-permute-done.2.refs_3_
  5.6 0.0 copy-start.3
  5.6 0.7 collective-permute-done.1.refs_2_
  6.3 0.0 copy-start.4
  6.3 0.0 collective-permute-done.refs_1_
  6.3 0.0 copy-start.5
  6.3 0.0 copy-done.2
  6.3 0.0 copy-done.3
  6.3 0.6 copy-done.4
  6.9 0.0 copy-done.5
  6.9 33.4 %loss.1 = (bf16[128,1024]{1,0:T(8,128)(2,1)}, bf16[128,1024]{1,0:T(8,128)(2,1)}, bf16[128,1024]{1,0:T(8,128)(2,1)}, bf16[128,1024]{1,0:T(8,128)(2,1)}) custom-call(s32[6]{0:T(128)} %stack.36.meta, s32[256]{0:T(256)} %reshape.26.pattern, s32[2,2048]{1,0:T(2,128)} %copy-done.2, s32[2,2048]{1,0:T(2,128)} %copy-done.5, s32[2,2048]{1,0:T(2,128)} %copy-done.4, ...), custom_call_target="tpu_custom_call" | custom-call | tf_op jit(solution)/shard_map/loss/pallas_call | solution.py:231
  40.3 1.6 %collective-permute-start.3 = (bf16[128,1024]{1,0:T(8,128)(2,1)}, bf16[128,1024]{1,0:T(8,128)(2,1)S(1)}, u32[]{:S(2)}, u32[]{:S(2)}) collective-permute-start(bf16[128,1024]{1,0:T(8,128)(2,1)} %get-tuple-element.9), channel_id=1, source_target_pairs={{0,4},{4,8},{8,12},{12,0},{1,5},{5,9},{9,13},{13,1},{2,6},{6,10},{... | collective-permute-start | bytes 786440 | tf_op jit(solution)/shard_map/ppermute | solution.py:182
  41.8 1.2 %collective-permute-start.4 = (bf16[128,1024]{1,0:T(8,128)(2,1)}, bf16[128,1024]{1,0:T(8,128)(2,1)S(1)}, u32[]{:S(2)}, u32[]{:S(2)}) collective-permute-start(bf16[128,1024]{1,0:T(8,128)(2,1)} %get-tuple-element.10), channel_id=1, source_target_pairs={{0,8},{4,12},{8,0},{12,4},{1,9},{5,13},{9,1},{13,5},{2,10},{6,14},... | collective-permute-start | bytes 786440 | tf_op jit(solution)/shard_map/ppermute | solution.py:182
  43.1 1.8 %collective-permute-start.5 = (bf16[128,1024]{1,0:T(8,128)(2,1)}, bf16[128,1024]{1,0:T(8,128)(2,1)S(1)}, u32[]{:S(2)}, u32[]{:S(2)}) collective-permute-start(bf16[128,1024]{1,0:T(8,128)(2,1)} %get-tuple-element.11), channel_id=1, source_target_pairs={{0,12},{4,0},{8,4},{12,8},{1,13},{5,1},{9,5},{13,9},{2,14},{6,2},{... | collective-permute-start | bytes 786440 | tf_op jit(solution)/shard_map/ppermute | solution.py:182
  44.9 0.0 copy-done.6
  44.9 0.1 reshape.25.pattern
  45.0 15.2 %collective-permute-done.3.refs_1_ = bf16[128,1024]{1,0:T(8,128)(2,1)S(1)} collective-permute-done((bf16[128,1024]{1,0:T(8,128)(2,1)}, bf16[128,1024]{1,0:T(8,128)(2,1)S(1)}, u32[]{:S(2)}, u32[]{:S(2)}) %collective-permute-start.3) | collective-permute-done | bytes 262176 | tf_op jit(solution)/shard_map/ppermute | solution.py:182
  60.1 4.1 %collective-permute-done.4.refs_2_ = bf16[128,1024]{1,0:T(8,128)(2,1)S(1)} collective-permute-done((bf16[128,1024]{1,0:T(8,128)(2,1)}, bf16[128,1024]{1,0:T(8,128)(2,1)S(1)}, u32[]{:S(2)}, u32[]{:S(2)}) %collective-permute-start.4) | collective-permute-done | bytes 262176 | tf_op jit(solution)/shard_map/ppermute | solution.py:182
  64.3 1.7 %collective-permute-done.5.refs_3_ = bf16[128,1024]{1,0:T(8,128)(2,1)S(1)} collective-permute-done((bf16[128,1024]{1,0:T(8,128)(2,1)}, bf16[128,1024]{1,0:T(8,128)(2,1)S(1)}, u32[]{:S(2)}, u32[]{:S(2)}) %collective-permute-start.5) | collective-permute-done | bytes 262176 | tf_op jit(solution)/shard_map/ppermute | solution.py:182
  66.0 0.0 copy-done
  66.0 0.0 copy-start.1
  66.0 0.9 %copy-done.1 = bf16[128,1024]{1,0:T(8,128)(2,1)S(1)} copy-done((bf16[128,1024]{1,0:T(8,128)(2,1)S(1)}, bf16[128,1024]{1,0:T(8,128)(2,1)}, u32[]{:S(2)}) %copy-start.1) | copy-done | bytes 262168
  66.9 2.2 %net.1 = (f32[128,1024]{1,0:T(8,128)}, f32[2,1024]{1,0:T(2,128)S(1)}) custom-call(s32[64]{0:T(128)S(1)} %reshape.25.pattern, bf16[128,1024]{1,0:T(8,128)(2,1)S(1)} %copy-done.1, bf16[128,1024]{1,0:T(8,128)(2,1)S(1)} %collective-permute-done.3.refs_1_, bf16[128,1024]{1,0:T(8,128)(2,1)S(1)} %collective-permute-done.4.refs_2_, ...), custom_call_target="tpu_custom_call" | custom-call | tf_op jit(solution)/shard_map/net/pallas_call | solution.py:268
  69.1 1.0 %collective-permute-start.8 = (f32[2,1024]{1,0:T(2,128)S(1)}, f32[2,1024]{1,0:T(2,128)S(1)}, u32[]{:S(2)}, u32[]{:S(2)}) collective-permute-start(f32[2,1024]{1,0:T(2,128)S(1)} %get-tuple-element.13), channel_id=1, source_target_pairs={{0,3},{1,2},{2,1},{3,0},{4,7},{5,6},{6,5},{7,4},{8,11},{9,10},{10,... | collective-permute-start | bytes 24584 | tf_op jit(solution)/shard_map/ppermute | solution.py:186
  70.1 0.6 collective-permute-start.7
  70.8 0.2 collective-permute-start.6
  71.0 1.2 %collective-permute-done.8 = f32[2,1024]{1,0:T(2,128)S(1)} collective-permute-done((f32[2,1024]{1,0:T(2,128)S(1)}, f32[2,1024]{1,0:T(2,128)S(1)}, u32[]{:S(2)}, u32[]{:S(2)}) %collective-permute-start.8) | collective-permute-done | bytes 8224 | tf_op jit(solution)/shard_map/ppermute | solution.py:186
  72.2 1.6 %collective-permute-done.7 = f32[2,1024]{1,0:T(2,128)S(1)} collective-permute-done((f32[2,1024]{1,0:T(2,128)S(1)}, f32[2,1024]{1,0:T(2,128)S(1)}, u32[]{:S(2)}, u32[]{:S(2)}) %collective-permute-start.7) | collective-permute-done | bytes 8224 | tf_op jit(solution)/shard_map/ppermute | solution.py:186
  73.8 0.0 collective-permute-done.6
  73.8 0.6 add_multiply_fusion
Async XLA Ops:
  0.6 44.3 %copy-start.6 = (s32[8,8]{1,0:T(8,128)S(1)}, s32[8,8]{1,0:T(8,128)}, u32[]{:S(2)}) copy-start(s32[8,8]{1,0:T(8,128)} %param.17) | copy-start | bytes 772
  0.6 65.3 %copy-start = (bf16[8,8,128,128]{3,2,1,0:T(8,128)(2,1)S(1)}, bf16[8,8,128,128]{3,2,1,0:T(8,128)(2,1)}, u32[]{:S(2)}) copy-start(bf16[8,8,128,128]{3,2,1,0:T(8,128)(2,1)} %param.16) | copy-start | bytes 6291460
  1.5 4.8 %copy-start.2 = (s32[2,2048]{1,0:T(2,128)}, s32[2,2048]{1,0:T(2,128)S(1)}, u32[]{:S(2)}) copy-start(s32[2,2048]{1,0:T(2,128)S(1)} %pad_add_fusion.refs_0_) | copy-start | bytes 49156
  1.5 4.0 %collective-permute-start.2 = (s32[2,2048]{1,0:T(2,128)S(1)}, s32[2,2048]{1,0:T(2,128)S(1)}, u32[]{:S(2)}, u32[]{:S(2)}) collective-permute-start(s32[2,2048]{1,0:T(2,128)S(1)} %pad_add_fusion.refs_0_), channel_id=1, source_target_pairs={{0,3},{1,2},{2,1},{3,0},{4,7},{5,6},{6,5},{7,4},{8,11},{9,10},{10,... | collective-permute-start | bytes 49160 | tf_op jit(solution)/shard_map/ppermute | solution.py:186
  2.5 3.7 %collective-permute-start.1 = (s32[2,2048]{1,0:T(2,128)S(1)}, s32[2,2048]{1,0:T(2,128)S(1)}, u32[]{:S(2)}, u32[]{:S(2)}) collective-permute-start(s32[2,2048]{1,0:T(2,128)S(1)} %pad_add_fusion.refs_0_), channel_id=1, source_target_pairs={{0,2},{1,3},{2,0},{3,1},{4,6},{5,7},{6,4},{7,5},{8,10},{9,11},{10,... | collective-permute-start | bytes 49160 | tf_op jit(solution)/shard_map/ppermute | solution.py:186
  3.2 3.1 %collective-permute-start = (s32[2,2048]{1,0:T(2,128)S(1)}, s32[2,2048]{1,0:T(2,128)S(1)}, u32[]{:S(2)}, u32[]{:S(2)}) collective-permute-start(s32[2,2048]{1,0:T(2,128)S(1)} %pad_add_fusion.refs_0_), channel_id=1, source_target_pairs={{0,1},{1,0},{2,3},{3,2},{4,5},{5,4},{6,7},{7,6},{8,9},{9,8},{10,11... | collective-permute-start | bytes 49160 | tf_op jit(solution)/shard_map/ppermute | solution.py:186
  5.6 0.7 copy-start.3
  6.3 0.6 copy-start.4
  6.3 0.6 copy-start.5
  40.3 19.9 %collective-permute-start.3 = (bf16[128,1024]{1,0:T(8,128)(2,1)}, bf16[128,1024]{1,0:T(8,128)(2,1)S(1)}, u32[]{:S(2)}, u32[]{:S(2)}) collective-permute-start(bf16[128,1024]{1,0:T(8,128)(2,1)} %get-tuple-element.9), channel_id=1, source_target_pairs={{0,4},{4,8},{8,12},{12,0},{1,5},{5,9},{9,13},{13,1},{2,6},{6,10},{... | collective-permute-start | bytes 786440 | tf_op jit(solution)/shard_map/ppermute | solution.py:182
  41.8 22.4 %collective-permute-start.4 = (bf16[128,1024]{1,0:T(8,128)(2,1)}, bf16[128,1024]{1,0:T(8,128)(2,1)S(1)}, u32[]{:S(2)}, u32[]{:S(2)}) collective-permute-start(bf16[128,1024]{1,0:T(8,128)(2,1)} %get-tuple-element.10), channel_id=1, source_target_pairs={{0,8},{4,12},{8,0},{12,4},{1,9},{5,13},{9,1},{13,5},{2,10},{6,14},... | collective-permute-start | bytes 786440 | tf_op jit(solution)/shard_map/ppermute | solution.py:182
  43.1 22.9 %collective-permute-start.5 = (bf16[128,1024]{1,0:T(8,128)(2,1)}, bf16[128,1024]{1,0:T(8,128)(2,1)S(1)}, u32[]{:S(2)}, u32[]{:S(2)}) collective-permute-start(bf16[128,1024]{1,0:T(8,128)(2,1)} %get-tuple-element.11), channel_id=1, source_target_pairs={{0,12},{4,0},{8,4},{12,8},{1,13},{5,1},{9,5},{13,9},{2,14},{6,2},{... | collective-permute-start | bytes 786440 | tf_op jit(solution)/shard_map/ppermute | solution.py:182
  66.0 1.0 %copy-start.1 = (bf16[128,1024]{1,0:T(8,128)(2,1)S(1)}, bf16[128,1024]{1,0:T(8,128)(2,1)}, u32[]{:S(2)}) copy-start(bf16[128,1024]{1,0:T(8,128)(2,1)} %get-tuple-element.8.refs_0_) | copy-start | bytes 786436
  69.1 3.1 %collective-permute-start.8 = (f32[2,1024]{1,0:T(2,128)S(1)}, f32[2,1024]{1,0:T(2,128)S(1)}, u32[]{:S(2)}, u32[]{:S(2)}) collective-permute-start(f32[2,1024]{1,0:T(2,128)S(1)} %get-tuple-element.13), channel_id=1, source_target_pairs={{0,3},{1,2},{2,1},{3,0},{4,7},{5,6},{6,5},{7,4},{8,11},{9,10},{10,... | collective-permute-start | bytes 24584 | tf_op jit(solution)/shard_map/ppermute | solution.py:186
  70.1 3.7 %collective-permute-start.7 = (f32[2,1024]{1,0:T(2,128)S(1)}, f32[2,1024]{1,0:T(2,128)S(1)}, u32[]{:S(2)}, u32[]{:S(2)}) collective-permute-start(f32[2,1024]{1,0:T(2,128)S(1)} %get-tuple-element.13), channel_id=1, source_target_pairs={{0,2},{1,3},{2,0},{3,1},{4,6},{5,7},{6,4},{7,5},{8,10},{9,11},{10,... | collective-permute-start | bytes 24584 | tf_op jit(solution)/shard_map/ppermute | solution.py:186
  70.8 3.0 %collective-permute-start.6 = (f32[2,1024]{1,0:T(2,128)S(1)}, f32[2,1024]{1,0:T(2,128)S(1)}, u32[]{:S(2)}, u32[]{:S(2)}) collective-permute-start(f32[2,1024]{1,0:T(2,128)S(1)} %get-tuple-element.13), channel_id=1, source_target_pairs={{0,1},{1,0},{2,3},{3,2},{4,5},{5,4},{6,7},{7,6},{8,9},{9,8},{10,11... | collective-permute-start | bytes 24584 | tf_op jit(solution)/shard_map/ppermute | solution.py:186

commit v2 on v1

v2 whole, which is shorter than its diff:
```python
import functools

import jax
import jax.numpy as jnp
from jax import lax
from jax.experimental import pallas as pl
from jax.experimental.pallas import tpu as pltpu
from jax.sharding import PartitionSpec as P

P_SIZE = 512
LANES = 128
ROWS = 16
STEP_BLOCKS = 4
DEST_CHUNK = 4
DOT_ROWS = 512
PIECE = 256
CHUNKS = 2
VMEM_LIMIT = 48 << 20

QUANTILE_MID = 2.6095163822174072
QUANTILE = (
    2.883376121520996,
    1.5978178977966309,
    0.023873422294855118,
    -0.0908193290233612,
    0.0662941262125969,
    -0.010339167900383472,
    -0.019267892464995384,
    0.011844170279800892,
    0.003007495542988181,
    -0.004063245374709368,
    -0.00016578214126639068,
    0.0005968576297163963,
)
CDF_SHIFT = 3.0
CDF_MID = 0.1666666716337204
CDF = (
    0.729083776473999,
    3.0559914112091064,
    8.280515670776367,
    10.208822250366211,
    -13.521076202392578,
    -54.16969680786133,
    43.550254821777344,
    285.4417419433594,
    -214.20135498046875,
    -1204.82958984375,
)
HALF_LOG2E = 0.7213475204444817


def horner(coefs, x):
    total = coefs[-1]
    for coef in coefs[-2::-1]:
        total = total * x + coef
    return total


def quantile(scaled):
    x = scaled.astype(jnp.float32) * (2.0**-31)
    s = 2.0 - jnp.log(1.0 - x * x)
    y = s * lax.rsqrt(s)
    return x * horner(QUANTILE, y - QUANTILE_MID)


def weighted_prob(t, exposure):
    y = jnp.abs(t)
    r = lax.rsqrt(y + CDF_SHIFT)
    q = r * r
    tail = jnp.exp2(t * t * -HALF_LOG2E) * q * horner(CDF, q - CDF_MID)
    return exposure * jnp.where(t > 0.0, 1.0 - tail, tail)


def loss_kernel(n_parts, n_dest, split, sub, direct, first_point, meta, pattern, *refs):
    parts = refs[:n_parts]
    load_ref, thr_ref, expo_ref, seg_ref = refs[n_parts : n_parts + 4]
    outs = refs[n_parts + 4 : -8]
    panel, acc = refs[-8:-6]
    latents = refs[-6:-4]
    slots = (refs[-4:-2], refs[-2:])
    points = acc.shape[1]
    seg_sub = acc.shape[2]
    seg_dev = seg_sub * sub
    blocks = load_ref.shape[0]
    columns = parts[0].shape[1] // LANES
    chunks = n_dest // split
    steps = blocks // STEP_BLOCKS

    acc[...] = jnp.zeros_like(acc)
    row = lax.broadcasted_iota(jnp.int32, (ROWS, LANES), 0) + (meta[0] + first_point)
    for k in range(n_parts):
        first = meta[2 + k] * columns

        def fill(c, carry, k=k, first=first):
            at = pl.ds(pl.multiple_of(c * LANES, LANES), LANES)
            gen = parts[k][0:1, at]
            shift = parts[k][1:2, at]
            scaled = lax.shift_left(row * gen, 23) + (lax.shift_left(shift, 13) + (4096 - 2**31))
            jump = lax.shift_left(gen, 27)
            for r in range(points // ROWS):
                value = quantile(scaled)
                rows = pl.ds(r * ROWS, ROWS)
                panel[0, first + c, rows, :] = value.astype(jnp.bfloat16)
                panel[1, first + c, rows, :] = pltpu.roll(value, LANES // 2, 1).astype(jnp.bfloat16)
                scaled = scaled + jump
            return carry

        lax.fori_loop(0, columns, fill, 0, unroll=2)

    low = lax.broadcasted_iota(jnp.int32, (points, LANES), 1) < LANES // 2
    seg_row = lax.broadcasted_iota(jnp.int32, (seg_sub, LANES), 0)

    def part_of(seg):
        part = lax.shift_right_logical(seg, seg_sub.bit_length() - 1) - meta[1] * sub
        return jnp.where(part < 0, part + n_dest * sub, part)

    def project(b, j, latent):
        halves = []
        for k in (0, 2):
            q0 = pattern[4 * b + k]
            q1 = pattern[4 * b + k + 1]
            left = panel[q0 & 1, lax.shift_right_logical(q0, 1)]
            right = panel[1 - (q1 & 1), lax.shift_right_logical(q1, 1)]
            halves.append(jnp.where(low, left, right))
        picked = jnp.concatenate(halves, axis=1)
        latent[:, j * LANES : (j + 1) * LANES] = jnp.dot(
            picked, load_ref[b], preferred_element_type=jnp.float32
        )

    def weigh(b, j, latent, masked, onehot):
        here = slice(j * LANES, (j + 1) * LANES)
        one = pl.ds(b, 1)
        prob = weighted_prob(thr_ref[one, :] - latent[:, here], expo_ref[one, :]).astype(jnp.bfloat16)
        seg = seg_ref[one, :]
        part = part_of(seg)
        onehot[:, here] = jnp.where(seg_row == (seg & (seg_sub - 1)), 1.0, 0.0).astype(jnp.bfloat16)
        for d in range(n_dest * sub):
            mine = jnp.where(part == d, 1.0, 0.0).astype(jnp.bfloat16)
            masked[d * points : (d + 1) * points, here] = prob * mine

    def add_piece(masked, onehot, first, count, segs):
        sums = lax.dot_general(
            masked[pl.ds(first * points, count * points), :],
            onehot[segs, :],
            (((1,), (1,)), ((), ())),
            preferred_element_type=jnp.float32,
        )
        for d in range(count):
            acc[first + d, :, segs] += sums[d * points : (d + 1) * points]

    group = split * sub
    pieces = [
        slice(i * PIECE, (i + 1) * PIECE) for i in range(seg_sub // PIECE)
    ]

    def add_all(masked, onehot):
        for segs in pieces:
            if chunks == 1:
                add_piece(masked, onehot, 0, group, segs)
            else:
                lax.fori_loop(
                    0, chunks, lambda c, x: (add_piece(masked, onehot, c * group, group, segs), x)[1], 0
                )

    def stage(step, new, ahead=True, behind=True):
        old = 1 - new
        waiting = list(pieces) if behind and chunks == 1 else []
        each = -(-STEP_BLOCKS // max(len(waiting), 1))
        for j in range(STEP_BLOCKS):
            if ahead:
                project((step + 1) * STEP_BLOCKS + j, j, latents[old])
            if waiting and j % each == 0:
                add_piece(*slots[old], 0, group, waiting.pop(0))
            weigh(step * STEP_BLOCKS + j, j, latents[new], *slots[new])
        for segs in waiting:
            add_piece(*slots[old], 0, group, segs)
        if behind and chunks > 1:
            add_all(*slots[old])

    for j in range(STEP_BLOCKS):
        project(j, j, latents[0])
    stage(0, 0, behind=False)

    def pair(i, carry):
        stage(2 * i + 1, 1)
        stage(2 * i + 2, 0)
        return carry

    lax.fori_loop(0, steps // 2 - 1, pair, 0)
    stage(steps - 1, 1, ahead=False)
    add_all(*slots[1])

    for d in range(n_dest):
        for i in range(sub):
            at = slice(i * seg_sub, (i + 1) * seg_sub)
            value = acc[d * sub + i]
            if not direct:
                outs[0][d, :, at] = value.astype(jnp.bfloat16)
            else:
                outs[d][:, at] = value.astype(outs[d].dtype)


def net_kernel(n_chunks, pattern, *refs):
    tiles_ref, net_ref, sums_ref, losses = refs[-4:]
    received = refs[:-4]
    blocks = tiles_ref.shape[0]
    slots = tiles_ref.shape[1] // LANES
    count = len(received) // n_chunks
    points = losses.shape[1] // n_chunks
    for c in range(n_chunks):
        mine = received[c * count : (c + 1) * count]
        for q in range(blocks):
            at = slice(q * LANES, (q + 1) * LANES)
            if count == 1:
                total = jnp.sum(mine[0][:, :, at].astype(jnp.float32), axis=0)
            else:
                total = mine[0][:, at]
                for ref in mine[1:]:
                    total = total + ref[:, at].astype(jnp.float32)
            losses[q, c * points : (c + 1) * points] = total.astype(jnp.bfloat16)
    for b in range(blocks):
        at = slice(b * LANES, (b + 1) * LANES)
        picked = jnp.concatenate([losses[pattern[slots * b + k]] for k in range(slots)], axis=1)
        net = jnp.dot(picked, tiles_ref[b], preferred_element_type=jnp.float32)
        net_ref[:, at] = net
        sums_ref[0:1, at] = jnp.sum(net, axis=0, keepdims=True)
        sums_ref[1:2, at] = jnp.sum(net * net, axis=0, keepdims=True)


def loss_call(meta, pattern, parts, loadings, threshold, exposure, segment_map, n_dest, first_point, points, seg_dev, direct):
    blocks = loadings.shape[0]
    own = parts[0]
    n_parts = len(parts)
    split = min(n_dest, DEST_CHUNK)
    sub = max(1, DOT_ROWS // (split * points))
    if direct:
        out_shape = [
            jax.ShapeDtypeStruct((points, seg_dev), jnp.bfloat16 if d else jnp.float32)
            for d in range(n_dest)
        ]
    else:
        out_shape = [jax.ShapeDtypeStruct((n_dest, points, seg_dev), jnp.bfloat16)]
    width = STEP_BLOCKS * LANES
    seg_sub = seg_dev // sub
    slot = [
        pltpu.VMEM((n_dest * sub * points, width), jnp.bfloat16),
        pltpu.VMEM((seg_sub, width), jnp.bfloat16),
    ]
    vmem = pl.BlockSpec(memory_space=pltpu.VMEM)
    smem = pl.BlockSpec(memory_space=pltpu.SMEM)
    return pl.pallas_call(
        functools.partial(loss_kernel, n_parts, n_dest, split, sub, direct, first_point),
        out_shape=out_shape,
        in_specs=[smem, smem] + [vmem] * (n_parts + 4),
        out_specs=[vmem] * len(out_shape),
        scratch_shapes=[
            pltpu.VMEM((2, own.shape[1] * n_parts // LANES, points, LANES), jnp.bfloat16),
            pltpu.VMEM((n_dest * sub, points, seg_sub), jnp.float32),
            pltpu.VMEM((points, width), jnp.float32),
            pltpu.VMEM((points, width), jnp.float32),
        ]
        + slot * 2,
        compiler_params=pltpu.CompilerParams(vmem_limit_bytes=VMEM_LIMIT),
        name="loss",
    )(
        meta,
        pattern,
        *parts,
        loadings.reshape(blocks, 256, LANES),
        threshold.reshape(blocks, LANES),
        exposure.reshape(blocks, LANES),
        segment_map.reshape(blocks, LANES),
    )


def shifted(x, axis, k):
    n = lax.axis_size(axis)
    return lax.ppermute(x, axis, [(i, (i + k) % n) for i in range(n)])


def swapped(x, axis, k):
    return lax.ppermute(x, axis, [(i, i ^ k) for i in range(lax.axis_size(axis))])


def pair_sum(terms):
    while len(terms) > 1:
        terms = [terms[i] + terms[i + 1] for i in range(0, len(terms), 2)]
    return terms[0]


def body(
    generator,
    lattice_shift,
    loadings,
    load_pattern,
    threshold,
    exposure,
    segment_map,
    net_tiles,
    net_pattern,
):
    n_narrow = lax.axis_size("narrow")
    n_dest = lax.axis_size("wide")
    me = lax.axis_index("narrow")
    points = P_SIZE // n_narrow
    seg_blocks = net_tiles.shape[0]
    seg_dev = seg_blocks * LANES
    direct = n_dest <= 8

    own = jnp.stack([generator, lattice_shift])
    parts = [own] + [swapped(own, "narrow", k) for k in range(1, n_narrow)]
    quarter = [me ^ k for k in range(n_narrow)]
    base = lax.axis_index("wide") if direct else 0
    meta = jnp.stack([me * points, jnp.int32(base)] + quarter).astype(jnp.int32)

    slots = net_tiles.shape[1]
    tiles = net_tiles.reshape(seg_blocks, slots * LANES, LANES)
    chunk = points // CHUNKS
    net_loss, sums = None, None
    partials = [
        loss_call(
            meta,
            load_pattern.reshape(-1),
            parts,
            loadings,
            threshold,
            exposure,
            segment_map,
            n_dest,
            c * chunk,
            chunk,
            seg_dev,
            direct,
        )
        for c in range(CHUNKS)
    ]
    received = []
    for partial in partials:
        if direct:
            received += [partial[0]] + [shifted(partial[k], "wide", k) for k in range(1, n_dest)]
        else:
            received += [lax.all_to_all(partial[0], "wide", split_axis=0, concat_axis=0, tiled=True)]
    vmem = pl.BlockSpec(memory_space=pltpu.VMEM)
    net_loss, sums = pl.pallas_call(
        functools.partial(net_kernel, CHUNKS),
        out_shape=[
            jax.ShapeDtypeStruct((points, seg_dev), jnp.float32),
            jax.ShapeDtypeStruct((2, seg_dev), jnp.float32),
        ],
        in_specs=[pl.BlockSpec(memory_space=pltpu.SMEM)] + [vmem] * (len(received) + 1),
        out_specs=[vmem] * 2,
        scratch_shapes=[pltpu.VMEM((seg_blocks, points, LANES), jnp.bfloat16)],
        compiler_params=pltpu.CompilerParams(vmem_limit_bytes=VMEM_LIMIT),
        name="net",
    )(net_pattern.reshape(-1), *received, tiles)

    total = pair_sum([sums] + [swapped(sums, "narrow", k) for k in range(1, n_narrow)])
    return (net_loss, total / P_SIZE)


def solution(mesh):
    return jax.shard_map(
        body,
        mesh=mesh,
        in_specs=(
            P("narrow"),
            P(("groups", "narrow")),
            P(("groups", "wide"), None, None, None),
            P(("groups", "wide"), None),
            P(("groups", "wide")),
            P(("groups", "wide")),
            P(("groups", "wide")),
            P(("groups", "wide"), None, None, None),
            P(("groups", "wide"), None),
        ),
        out_specs=(P("narrow", ("groups", "wide")), P(None, ("groups", "wide"))),
        check_vma=False,
    )
```

time: 74.6 us -> 70 us (0.938)
  the two profiles are of different devices: /device:TPU:8 before, /device:TPU:0 now
where the time goes in v2:
time: 70 us; the launch traced here: 69.5 us
  Pallas kernels  35.8 us (51%)
  starting transfers between devices  14.3 us (20%)
  waiting for transfers between devices  11.9 us (17%)
  local copies, waits for them, and re-layouts  5.51 us (8%)
  other arithmetic  1.35 us (2%)
    pallas_call x2, Pallas kernels, loss_call(): pl.pallas_call(functools.partial(loss_kernel, n_parts, n_dest, split, sub...  33.6 us
    ppermute x6, starting transfers between devices, shifted(): return lax.ppermute(x, axis, [(i, (i + k) % n) for i in range(n)])  9.34 us
    ppermute x6, waiting for transfers between devices, shifted(): return lax.ppermute(x, axis, [(i, (i + k) % n) for i in range(n)])  8 us
    unnamed x15, local copies, waits for them, and re-layouts  5.24 us
    ppermute x6, starting transfers between devices, swapped(): lax.ppermute(x, axis, [(i, i ^ k) for i in range(lax.axis_size(axis))])  4.98 us
    ppermute x6, waiting for transfers between devices, swapped(): lax.ppermute(x, axis, [(i, i ^ k) for i in range(lax.axis_size(axis))])  3.92 us
    pallas_call x1, Pallas kernels, body(): pl.pallas_call(functools.partial(net_kernel, CHUNKS), out_shape=[jax.Shap...  2.15 us
  transfers between devices with their start and end apart: 12, of which 5 were waited for; matrix products, arithmetic and copies ran while one was open for 1% of the time, Pallas kernels for 24%

profile of v2, /device:TPU:0, one launch (start us, length us, event | category | flops | bytes accessed | tf_op | source)
XLA Modules:
  0.0 69.5 jit_solution(9422380702216543435)
XLA Ops:
  0.6 0.0 copy-start.5
  0.6 0.7 %pad_add_fusion.refs_0_ = s32[2,2048]{1,0:T(2,128)S(1)} fusion(s32[1,2048]{1,0:T(1,128)} %bitcast.22, s32[1,2048]{1,0:T(1,128)} %bitcast.23), kind=kLoop, calls=%fused_computation | loop fusion | flops 4096 | bytes 32768 | tf_op jit(solution)/shard_map/stack | solution.py:310
  1.4 2.4 %collective-permute-start.2 = (s32[2,2048]{1,0:T(2,128)S(1)}, s32[2,2048]{1,0:T(2,128)S(1)}, u32[]{:S(2)}, u32[]{:S(2)}) collective-permute-start(s32[2,2048]{1,0:T(2,128)S(1)} %pad_add_fusion.refs_0_), channel_id=1, source_target_pairs={{0,3},{1,2},{2,1},{3,0},{4,7},{5,6},{6,5},{7,4},{8,11},{9,10},{10,... | collective-permute-start | bytes 49160 | tf_op jit(solution)/shard_map/ppermute | solution.py:282
  3.8 0.6 collective-permute-start.1
  4.5 0.0 collective-permute-start
  4.5 0.8 %copy.11 = s32[64,4]{1,0:T(8,128)S(1)} copy(s32[64,4]{0,1:T(4,128)} %param.12) | data formatting | bytes 2048 | tf_op args[3]
  5.3 0.1 reshape.31.pattern
  5.4 0.1 stack.36.meta
  5.5 0.0 collective-permute-done.2.refs_3_
  5.5 2.1 %collective-permute-done.1.refs_2_ = s32[2,2048]{1,0:T(2,128)S(1)} collective-permute-done((s32[2,2048]{1,0:T(2,128)S(1)}, s32[2,2048]{1,0:T(2,128)S(1)}, u32[]{:S(2)}, u32[]{:S(2)}) %collective-permute-start.1) | collective-permute-done | bytes 16416 | tf_op jit(solution)/shard_map/ppermute | solution.py:282
  7.6 0.0 collective-permute-done.refs_1_
  7.6 0.0 copy-start
  7.6 2.2 %copy-done = bf16[64,4,64,128]{3,2,1,0:T(8,128)(2,1)S(1)} copy-done((bf16[64,4,64,128]{3,2,1,0:T(8,128)(2,1)S(1)}, bf16[64,4,64,128]{3,2,1,0:T(8,128)(2,1)}, u32[]{:S(2)}) %copy-start) | copy-done | bytes 4194328
  9.8 0.0 copy-start.2
  9.8 0.8 %copy-done.2 = f32[8192]{0:T(1024)S(1)} copy-done((f32[8192]{0:T(1024)S(1)}, f32[8192]{0:T(1024)}, u32[]{:S(2)}) %copy-start.2) | copy-done | bytes 32792
  10.5 0.0 copy-start.3
  10.5 0.8 %copy-done.3 = f32[8192]{0:T(1024)S(1)} copy-done((f32[8192]{0:T(1024)S(1)}, f32[8192]{0:T(1024)}, u32[]{:S(2)}) %copy-start.3) | copy-done | bytes 32792
  11.3 0.0 copy-start.4
  11.3 0.8 %copy-done.4 = s32[8192]{0:T(1024)S(1)} copy-done((s32[8192]{0:T(1024)S(1)}, s32[8192]{0:T(1024)}, u32[]{:S(2)}) %copy-start.4) | copy-done | bytes 32792
  12.0 0.0 copy-start.6
  12.0 0.0 copy-start.1
  12.0 16.8 %loss.3 = (f32[64,1024]{1,0:T(8,128)S(1)}, bf16[64,1024]{1,0:T(8,128)(2,1)S(1)}, bf16[64,1024]{1,0:T(8,128)(2,1)}, bf16[64,1024]{1,0:T(8,128)(2,1)}) custom-call(s32[6]{0:T(128)S(1)} %stack.36.meta, s32[256]{0:T(256)S(1)} %reshape.31.pattern, s32[2,2048]{1,0:T(2,128)S(1)} %pad_add_fusion.refs_0_, s32[2,2048]{1,0:T(2,128)S(1)} %collective-permute-done.refs_1_, ...), custom_call_target="tpu_custom_call" | custom-call | tf_op jit(solution)/shard_map/loss/pallas_call | solution.py:251
  28.8 1.6 %collective-permute-start.6 = (bf16[64,1024]{1,0:T(8,128)(2,1)S(1)}, bf16[64,1024]{1,0:T(8,128)(2,1)S(1)}, u32[]{:S(2)}, u32[]{:S(2)}) collective-permute-start(bf16[64,1024]{1,0:T(8,128)(2,1)S(1)} %get-tuple-element.17), channel_id=1, source_target_pairs={{0,4},{4,8},{8,12},{12,0},{1,5},{5,9},{9,13},{13,1},{2,6},{6,10},{... | collective-permute-start | bytes 393224 | tf_op jit(solution)/shard_map/ppermute | solution.py:278
  30.4 2.6 %collective-permute-start.7 = (bf16[64,1024]{1,0:T(8,128)(2,1)}, bf16[64,1024]{1,0:T(8,128)(2,1)S(1)}, u32[]{:S(2)}, u32[]{:S(2)}) collective-permute-start(bf16[64,1024]{1,0:T(8,128)(2,1)} %get-tuple-element.18), channel_id=1, source_target_pairs={{0,8},{4,12},{8,0},{12,4},{1,9},{5,13},{9,1},{13,5},{2,10},{6,14},... | collective-permute-start | bytes 393224 | tf_op jit(solution)/shard_map/ppermute | solution.py:278
  33.0 1.3 %collective-permute-start.8 = (bf16[64,1024]{1,0:T(8,128)(2,1)}, bf16[64,1024]{1,0:T(8,128)(2,1)S(1)}, u32[]{:S(2)}, u32[]{:S(2)}) collective-permute-start(bf16[64,1024]{1,0:T(8,128)(2,1)} %get-tuple-element.19), channel_id=1, source_target_pairs={{0,12},{4,0},{8,4},{12,8},{1,13},{5,1},{9,5},{13,9},{2,14},{6,2},{... | collective-permute-start | bytes 393224 | tf_op jit(solution)/shard_map/ppermute | solution.py:278
  34.4 0.0 copy-done.5
  34.4 16.8 %loss.2 = (f32[64,1024]{1,0:T(8,128)S(1)}, bf16[64,1024]{1,0:T(8,128)(2,1)}, bf16[64,1024]{1,0:T(8,128)(2,1)}, bf16[64,1024]{1,0:T(8,128)(2,1)}) custom-call(s32[6]{0:T(128)S(1)} %stack.36.meta, s32[256]{0:T(256)S(1)} %reshape.31.pattern, s32[2,2048]{1,0:T(2,128)S(1)} %pad_add_fusion.refs_0_, s32[2,2048]{1,0:T(2,128)S(1)} %collective-permute-done.refs_1_, ...), custom_call_target="tpu_custom_call" | custom-call | tf_op jit(solution)/shard_map/loss/pallas_call | solution.py:251
  51.2 0.7 collective-permute-start.3
  51.9 0.3 collective-permute-start.4
  52.2 0.0 collective-permute-done.6.refs_5_
  52.2 2.8 %collective-permute-start.5 = (bf16[64,1024]{1,0:T(8,128)(2,1)}, bf16[64,1024]{1,0:T(8,128)(2,1)S(1)}, u32[]{:S(2)}, u32[]{:S(2)}) collective-permute-start(bf16[64,1024]{1,0:T(8,128)(2,1)} %get-tuple-element.15), channel_id=1, source_target_pairs={{0,12},{4,0},{8,4},{12,8},{1,13},{5,1},{9,5},{13,9},{2,14},{6,2},{... | collective-permute-start | bytes 393224 | tf_op jit(solution)/shard_map/ppermute | solution.py:278
  55.0 0.0 copy-done.6
  55.0 0.1 reshape.30.pattern
  55.1 0.0 collective-permute-done.7.refs_6_
  55.1 0.0 collective-permute-done.8.refs_7_
  55.1 4.6 %collective-permute-done.3.refs_1_ = bf16[64,1024]{1,0:T(8,128)(2,1)S(1)} collective-permute-done((bf16[64,1024]{1,0:T(8,128)(2,1)}, bf16[64,1024]{1,0:T(8,128)(2,1)S(1)}, u32[]{:S(2)}, u32[]{:S(2)}) %collective-permute-start.3) | collective-permute-done | bytes 131104 | tf_op jit(solution)/shard_map/ppermute | solution.py:278
  59.7 3.4 %collective-permute-done.4.refs_2_ = bf16[64,1024]{1,0:T(8,128)(2,1)S(1)} collective-permute-done((bf16[64,1024]{1,0:T(8,128)(2,1)}, bf16[64,1024]{1,0:T(8,128)(2,1)S(1)}, u32[]{:S(2)}, u32[]{:S(2)}) %collective-permute-start.4) | collective-permute-done | bytes 131104 | tf_op jit(solution)/shard_map/ppermute | solution.py:278
  63.1 0.0 collective-permute-done.5.refs_3_
  63.1 0.0 copy-done.1
  63.1 2.1 %net.1 = (f32[128,1024]{1,0:T(8,128)}, f32[2,1024]{1,0:T(2,128)S(1)}) custom-call(s32[64]{0:T(128)S(1)} %reshape.30.pattern, f32[64,1024]{1,0:T(8,128)S(1)} %get-tuple-element.12.refs_0_, bf16[64,1024]{1,0:T(8,128)(2,1)S(1)} %collective-permute-done.3.refs_1_, bf16[64,1024]{1,0:T(8,128)(2,1)S(1)} %collective-permute-done.4.refs_2_, ...), custom_call_target="tpu_custom_call" | custom-call | tf_op jit(solution)/shard_map/net/pallas_call | solution.py:344
  65.2 0.0 collective-permute-start.11
  65.2 0.8 %collective-permute-start.10 = (f32[2,1024]{1,0:T(2,128)S(1)}, f32[2,1024]{1,0:T(2,128)S(1)}, u32[]{:S(2)}, u32[]{:S(2)}) collective-permute-start(f32[2,1024]{1,0:T(2,128)S(1)} %get-tuple-element.21), channel_id=1, source_target_pairs={{0,2},{1,3},{2,0},{3,1},{4,6},{5,7},{6,4},{7,5},{8,10},{9,11},{10,... | collective-permute-start | bytes 24584 | tf_op jit(solution)/shard_map/ppermute | solution.py:282
  66.0 1.1 %collective-permute-start.9 = (f32[2,1024]{1,0:T(2,128)S(1)}, f32[2,1024]{1,0:T(2,128)S(1)}, u32[]{:S(2)}, u32[]{:S(2)}) collective-permute-start(f32[2,1024]{1,0:T(2,128)S(1)} %get-tuple-element.21), channel_id=1, source_target_pairs={{0,1},{1,0},{2,3},{3,2},{4,5},{5,4},{6,7},{7,6},{8,9},{9,8},{10,11... | collective-permute-start | bytes 24584 | tf_op jit(solution)/shard_map/ppermute | solution.py:282
  67.1 1.2 %collective-permute-done.11 = f32[2,1024]{1,0:T(2,128)S(1)} collective-permute-done((f32[2,1024]{1,0:T(2,128)S(1)}, f32[2,1024]{1,0:T(2,128)S(1)}, u32[]{:S(2)}, u32[]{:S(2)}) %collective-permute-start.11) | collective-permute-done | bytes 8224 | tf_op jit(solution)/shard_map/ppermute | solution.py:282
  68.3 0.6 collective-permute-done.10
  68.9 0.0 collective-permute-done.9
  68.9 0.6 add_multiply_fusion
Async XLA Ops:
  0.6 33.7 %copy-start.5 = (s32[8192]{0:T(1024)S(1)}, s32[8192]{0:T(1024)}, u32[]{:S(2)}) copy-start(s32[8192]{0:T(1024)} %param.15) | copy-start | bytes 98308
  1.4 4.1 %collective-permute-start.2 = (s32[2,2048]{1,0:T(2,128)S(1)}, s32[2,2048]{1,0:T(2,128)S(1)}, u32[]{:S(2)}, u32[]{:S(2)}) collective-permute-start(s32[2,2048]{1,0:T(2,128)S(1)} %pad_add_fusion.refs_0_), channel_id=1, source_target_pairs={{0,3},{1,2},{2,1},{3,0},{4,7},{5,6},{6,5},{7,4},{8,11},{9,10},{10,... | collective-permute-start | bytes 49160 | tf_op jit(solution)/shard_map/ppermute | solution.py:282
  3.8 3.7 %collective-permute-start.1 = (s32[2,2048]{1,0:T(2,128)S(1)}, s32[2,2048]{1,0:T(2,128)S(1)}, u32[]{:S(2)}, u32[]{:S(2)}) collective-permute-start(s32[2,2048]{1,0:T(2,128)S(1)} %pad_add_fusion.refs_0_), channel_id=1, source_target_pairs={{0,2},{1,3},{2,0},{3,1},{4,6},{5,7},{6,4},{7,5},{8,10},{9,11},{10,... | collective-permute-start | bytes 49160 | tf_op jit(solution)/shard_map/ppermute | solution.py:282
  4.5 3.1 %collective-permute-start = (s32[2,2048]{1,0:T(2,128)S(1)}, s32[2,2048]{1,0:T(2,128)S(1)}, u32[]{:S(2)}, u32[]{:S(2)}) collective-permute-start(s32[2,2048]{1,0:T(2,128)S(1)} %pad_add_fusion.refs_0_), channel_id=1, source_target_pairs={{0,1},{1,0},{2,3},{3,2},{4,5},{5,4},{6,7},{7,6},{8,9},{9,8},{10,11... | collective-permute-start | bytes 49160 | tf_op jit(solution)/shard_map/ppermute | solution.py:282
  7.6 2.2 %copy-start = (bf16[64,4,64,128]{3,2,1,0:T(8,128)(2,1)S(1)}, bf16[64,4,64,128]{3,2,1,0:T(8,128)(2,1)}, u32[]{:S(2)}) copy-start(bf16[64,4,64,128]{3,2,1,0:T(8,128)(2,1)} %param.11) | copy-start | bytes 12582916
  9.8 0.8 %copy-start.2 = (f32[8192]{0:T(1024)S(1)}, f32[8192]{0:T(1024)}, u32[]{:S(2)}) copy-start(f32[8192]{0:T(1024)} %param.13) | copy-start | bytes 98308
  10.5 0.8 %copy-start.3 = (f32[8192]{0:T(1024)S(1)}, f32[8192]{0:T(1024)}, u32[]{:S(2)}) copy-start(f32[8192]{0:T(1024)} %param.14) | copy-start | bytes 98308
  11.3 0.8 %copy-start.4 = (s32[8192]{0:T(1024)S(1)}, s32[8192]{0:T(1024)}, u32[]{:S(2)}) copy-start(s32[8192]{0:T(1024)} %param.15) | copy-start | bytes 98308
  12.0 43.0 %copy-start.6 = (s32[8,8]{1,0:T(8,128)S(1)}, s32[8,8]{1,0:T(8,128)}, u32[]{:S(2)}) copy-start(s32[8,8]{1,0:T(8,128)} %param.17) | copy-start | bytes 772
  12.0 51.1 %copy-start.1 = (bf16[8,8,128,128]{3,2,1,0:T(8,128)(2,1)S(1)}, bf16[8,8,128,128]{3,2,1,0:T(8,128)(2,1)}, u32[]{:S(2)}) copy-start(bf16[8,8,128,128]{3,2,1,0:T(8,128)(2,1)} %param.16) | copy-start | bytes 6291460
  28.8 23.4 %collective-permute-start.6 = (bf16[64,1024]{1,0:T(8,128)(2,1)S(1)}, bf16[64,1024]{1,0:T(8,128)(2,1)S(1)}, u32[]{:S(2)}, u32[]{:S(2)}) collective-permute-start(bf16[64,1024]{1,0:T(8,128)(2,1)S(1)} %get-tuple-element.17), channel_id=1, source_target_pairs={{0,4},{4,8},{8,12},{12,0},{1,5},{5,9},{9,13},{13,1},{2,6},{6,10},{... | collective-permute-start | bytes 393224 | tf_op jit(solution)/shard_map/ppermute | solution.py:278
  30.4 24.7 %collective-permute-start.7 = (bf16[64,1024]{1,0:T(8,128)(2,1)}, bf16[64,1024]{1,0:T(8,128)(2,1)S(1)}, u32[]{:S(2)}, u32[]{:S(2)}) collective-permute-start(bf16[64,1024]{1,0:T(8,128)(2,1)} %get-tuple-element.18), channel_id=1, source_target_pairs={{0,8},{4,12},{8,0},{12,4},{1,9},{5,13},{9,1},{13,5},{2,10},{6,14},... | collective-permute-start | bytes 393224 | tf_op jit(solution)/shard_map/ppermute | solution.py:278
  33.0 22.1 %collective-permute-start.8 = (bf16[64,1024]{1,0:T(8,128)(2,1)}, bf16[64,1024]{1,0:T(8,128)(2,1)S(1)}, u32[]{:S(2)}, u32[]{:S(2)}) collective-permute-start(bf16[64,1024]{1,0:T(8,128)(2,1)} %get-tuple-element.19), channel_id=1, source_target_pairs={{0,12},{4,0},{8,4},{12,8},{1,13},{5,1},{9,5},{13,9},{2,14},{6,2},{... | collective-permute-start | bytes 393224 | tf_op jit(solution)/shard_map/ppermute | solution.py:278
  51.2 8.5 %collective-permute-start.3 = (bf16[64,1024]{1,0:T(8,128)(2,1)}, bf16[64,1024]{1,0:T(8,128)(2,1)S(1)}, u32[]{:S(2)}, u32[]{:S(2)}) collective-permute-start(bf16[64,1024]{1,0:T(8,128)(2,1)} %get-tuple-element.13), channel_id=1, source_target_pairs={{0,4},{4,8},{8,12},{12,0},{1,5},{5,9},{9,13},{13,1},{2,6},{6,10},{... | collective-permute-start | bytes 393224 | tf_op jit(solution)/shard_map/ppermute | solution.py:278
  51.9 11.2 %collective-permute-start.4 = (bf16[64,1024]{1,0:T(8,128)(2,1)}, bf16[64,1024]{1,0:T(8,128)(2,1)S(1)}, u32[]{:S(2)}, u32[]{:S(2)}) collective-permute-start(bf16[64,1024]{1,0:T(8,128)(2,1)} %get-tuple-element.14), channel_id=1, source_target_pairs={{0,8},{4,12},{8,0},{12,4},{1,9},{5,13},{9,1},{13,5},{2,10},{6,14},... | collective-permute-start | bytes 393224 | tf_op jit(solution)/shard_map/ppermute | solution.py:278
  52.2 10.9 %collective-permute-start.5 = (bf16[64,1024]{1,0:T(8,128)(2,1)}, bf16[64,1024]{1,0:T(8,128)(2,1)S(1)}, u32[]{:S(2)}, u32[]{:S(2)}) collective-permute-start(bf16[64,1024]{1,0:T(8,128)(2,1)} %get-tuple-element.15), channel_id=1, source_target_pairs={{0,12},{4,0},{8,4},{12,8},{1,13},{5,1},{9,5},{13,9},{2,14},{6,2},{... | collective-permute-start | bytes 393224 | tf_op jit(solution)/shard_map/ppermute | solution.py:278
  65.2 3.1 %collective-permute-start.11 = (f32[2,1024]{1,0:T(2,128)S(1)}, f32[2,1024]{1,0:T(2,128)S(1)}, u32[]{:S(2)}, u32[]{:S(2)}) collective-permute-start(f32[2,1024]{1,0:T(2,128)S(1)} %get-tuple-element.21), channel_id=1, source_target_pairs={{0,3},{1,2},{2,1},{3,0},{4,7},{5,6},{6,5},{7,4},{8,11},{9,10},{10,... | collective-permute-start | bytes 24584 | tf_op jit(solution)/shard_map/ppermute | solution.py:282
  65.2 3.7 %collective-permute-start.10 = (f32[2,1024]{1,0:T(2,128)S(1)}, f32[2,1024]{1,0:T(2,128)S(1)}, u32[]{:S(2)}, u32[]{:S(2)}) collective-permute-start(f32[2,1024]{1,0:T(2,128)S(1)} %get-tuple-element.21), channel_id=1, source_target_pairs={{0,2},{1,3},{2,0},{3,1},{4,6},{5,7},{6,4},{7,5},{8,10},{9,11},{10,... | collective-permute-start | bytes 24584 | tf_op jit(solution)/shard_map/ppermute | solution.py:282
  66.0 2.9 %collective-permute-start.9 = (f32[2,1024]{1,0:T(2,128)S(1)}, f32[2,1024]{1,0:T(2,128)S(1)}, u32[]{:S(2)}, u32[]{:S(2)}) collective-permute-start(f32[2,1024]{1,0:T(2,128)S(1)} %get-tuple-element.21), channel_id=1, source_target_pairs={{0,1},{1,0},{2,3},{3,2},{4,5},{5,4},{6,7},{7,6},{8,9},{9,8},{10,11... | collective-permute-start | bytes 24584 | tf_op jit(solution)/shard_map/ppermute | solution.py:282

commit v3 on v2

--- a/solution.py
+++ b/solution.py
@@ -10,10 +10,8 @@
 P_SIZE = 512
 LANES = 128
 ROWS = 16
-STEP_BLOCKS = 4
 DEST_CHUNK = 4
-DOT_ROWS = 512
-PIECE = 256
+MXU = 256
 CHUNKS = 2
 VMEM_LIMIT = 48 << 20
 
@@ -71,22 +69,27 @@
     return exposure * jnp.where(t > 0.0, 1.0 - tail, tail)
 
 
-def loss_kernel(n_parts, n_dest, split, sub, direct, first_point, meta, pattern, *refs):
+def loss_kernel(n_parts, n_dest, split, direct, first_point, meta, pattern, *refs):
     parts = refs[:n_parts]
-    load_ref, thr_ref, expo_ref, seg_ref = refs[n_parts : n_parts + 4]
+    sources = refs[n_parts : n_parts + 4]
     outs = refs[n_parts + 4 : -8]
-    panel, acc = refs[-8:-6]
-    latents = refs[-6:-4]
-    slots = (refs[-4:-2], refs[-2:])
-    points = acc.shape[1]
-    seg_sub = acc.shape[2]
-    seg_dev = seg_sub * sub
+    panel, load_ref, thr_ref, expo_ref, seg_ref, even, odd, sems = refs[-8:]
+    masked = (even, odd)
+    points = panel.shape[2]
     blocks = load_ref.shape[0]
     columns = parts[0].shape[1] // LANES
-    chunks = n_dest // split
-    steps = blocks // STEP_BLOCKS
-
-    acc[...] = jnp.zeros_like(acc)
+    seg_dev = (outs[0] if direct else outs[0].at[0]).shape[1]
+    sub = seg_dev // (2 * MXU)
+    group = split * sub
+    steps = blocks // 2
+
+    copies = [
+        pltpu.make_async_copy(source, target, sems.at[i])
+        for i, (source, target) in enumerate(zip(sources, (load_ref, thr_ref, expo_ref, seg_ref)))
+    ]
+    for copy in copies:
+        copy.start()
+
     row = lax.broadcasted_iota(jnp.int32, (ROWS, LANES), 0) + (meta[0] + first_point)
     for k in range(n_parts):
         first = meta[2 + k] * columns
@@ -105,16 +108,15 @@
                 scaled = scaled + jump
             return carry
 
-        lax.fori_loop(0, columns, fill, 0, unroll=2)
+        lax.fori_loop(0, columns, fill, 0, unroll=8)
+
+    for copy in copies:
+        copy.wait()
 
     low = lax.broadcasted_iota(jnp.int32, (points, LANES), 1) < LANES // 2
-    seg_row = lax.broadcasted_iota(jnp.int32, (seg_sub, LANES), 0)
-
-    def part_of(seg):
-        part = lax.shift_right_logical(seg, seg_sub.bit_length() - 1) - meta[1] * sub
-        return jnp.where(part < 0, part + n_dest * sub, part)
-
-    def project(b, j, latent):
+    seg_row = lax.broadcasted_iota(jnp.int32, (MXU, LANES), 0)
+
+    def picked(b):
         halves = []
         for k in (0, 2):
             q0 = pattern[4 * b + k]
@@ -122,82 +124,82 @@
             left = panel[q0 & 1, lax.shift_right_logical(q0, 1)]
             right = panel[1 - (q1 & 1), lax.shift_right_logical(q1, 1)]
             halves.append(jnp.where(low, left, right))
-        picked = jnp.concatenate(halves, axis=1)
-        latent[:, j * LANES : (j + 1) * LANES] = jnp.dot(
-            picked, load_ref[b], preferred_element_type=jnp.float32
-        )
-
-    def weigh(b, j, latent, masked, onehot):
-        here = slice(j * LANES, (j + 1) * LANES)
-        one = pl.ds(b, 1)
-        prob = weighted_prob(thr_ref[one, :] - latent[:, here], expo_ref[one, :]).astype(jnp.bfloat16)
-        seg = seg_ref[one, :]
-        part = part_of(seg)
-        onehot[:, here] = jnp.where(seg_row == (seg & (seg_sub - 1)), 1.0, 0.0).astype(jnp.bfloat16)
-        for d in range(n_dest * sub):
-            mine = jnp.where(part == d, 1.0, 0.0).astype(jnp.bfloat16)
-            masked[d * points : (d + 1) * points, here] = prob * mine
-
-    def add_piece(masked, onehot, first, count, segs):
-        sums = lax.dot_general(
-            masked[pl.ds(first * points, count * points), :],
-            onehot[segs, :],
-            (((1,), (1,)), ((), ())),
-            preferred_element_type=jnp.float32,
-        )
-        for d in range(count):
-            acc[first + d, :, segs] += sums[d * points : (d + 1) * points]
-
-    group = split * sub
-    pieces = [
-        slice(i * PIECE, (i + 1) * PIECE) for i in range(seg_sub // PIECE)
-    ]
-
-    def add_all(masked, onehot):
-        for segs in pieces:
-            if chunks == 1:
-                add_piece(masked, onehot, 0, group, segs)
-            else:
-                lax.fori_loop(
-                    0, chunks, lambda c, x: (add_piece(masked, onehot, c * group, group, segs), x)[1], 0
-                )
-
-    def stage(step, new, ahead=True, behind=True):
-        old = 1 - new
-        waiting = list(pieces) if behind and chunks == 1 else []
-        each = -(-STEP_BLOCKS // max(len(waiting), 1))
-        for j in range(STEP_BLOCKS):
+        return jnp.concatenate(halves, axis=1)
+
+    def one_pass(chunk, sums, latents):
+        def project(step, parity):
+            b = 2 * step
+            loads = jnp.concatenate([load_ref[b], load_ref[b + 1]], axis=1)
+            pltpu.matmul_push_rhs(loads, parity, parity)
+            pltpu.matmul_acc_lhs(
+                latents[parity], jnp.concatenate([picked(b), picked(b + 1)], axis=0), parity
+            )
+
+        def push_onehot(step, parity):
+            local = [seg_ref[pl.ds(2 * step + j, 1), :] & (2 * MXU - 1) for j in range(2)]
+            for n in range(2):
+                tile = [jnp.where(seg_row == at - n * MXU, 1.0, 0.0).astype(jnp.bfloat16) for at in local]
+                pltpu.matmul_push_rhs(jnp.concatenate(tile, axis=1), parity, n, transpose=True)
+
+        def add_up(parity):
+            for n in range(2):
+                pltpu.matmul_acc_lhs(sums[n], masked[parity][...], parity)
+
+        def weigh(step, parity):
+            latent = pltpu.matmul_pop(latents[parity])
+            for j in range(2):
+                one = pl.ds(2 * step + j, 1)
+                here = slice(j * LANES, (j + 1) * LANES)
+                t = thr_ref[one, :] - latent[j * points : (j + 1) * points, here]
+                prob = weighted_prob(t, expo_ref[one, :]).astype(jnp.bfloat16)
+                part = lax.shift_right_logical(seg_ref[one, :], (2 * MXU).bit_length() - 1) - meta[1] * sub
+                part = jnp.where(part < 0, part + n_dest * sub, part) - chunk * group
+                for d in range(group):
+                    mine = jnp.where(part == d, 1.0, 0.0).astype(jnp.bfloat16)
+                    masked[parity][d * points : (d + 1) * points, here] = prob * mine
+
+        def stage(step, parity, ahead=True, behind=True):
+            push_onehot(step, parity)
+            if behind:
+                add_up(1 - parity)
             if ahead:
-                project((step + 1) * STEP_BLOCKS + j, j, latents[old])
-            if waiting and j % each == 0:
-                add_piece(*slots[old], 0, group, waiting.pop(0))
-            weigh(step * STEP_BLOCKS + j, j, latents[new], *slots[new])
-        for segs in waiting:
-            add_piece(*slots[old], 0, group, segs)
-        if behind and chunks > 1:
-            add_all(*slots[old])
-
-    for j in range(STEP_BLOCKS):
-        project(j, j, latents[0])
-    stage(0, 0, behind=False)
-
-    def pair(i, carry):
-        stage(2 * i + 1, 1)
-        stage(2 * i + 2, 0)
-        return carry
-
-    lax.fori_loop(0, steps // 2 - 1, pair, 0)
-    stage(steps - 1, 1, ahead=False)
-    add_all(*slots[1])
-
-    for d in range(n_dest):
-        for i in range(sub):
-            at = slice(i * seg_sub, (i + 1) * seg_sub)
-            value = acc[d * sub + i]
-            if not direct:
-                outs[0][d, :, at] = value.astype(jnp.bfloat16)
-            else:
-                outs[d][:, at] = value.astype(outs[d].dtype)
+                project(step + 1, 1 - parity)
+            weigh(step, parity)
+
+        project(0, 0)
+        stage(0, 0, behind=False)
+
+        def pair(i, carry):
+            stage(2 * i + 1, 1)
+            stage(2 * i + 2, 0)
+            return carry
+
+        lax.fori_loop(0, steps // 2 - 1, pair, 0)
+        stage(steps - 1, 1, ahead=False)
+        add_up(1)
+
+        for n in range(2):
+            total = pltpu.matmul_pop(sums[n])
+            for d in range(split):
+                for i in range(sub):
+                    at = slice(i * 2 * MXU + n * MXU, i * 2 * MXU + (n + 1) * MXU)
+                    value = total[(d * sub + i) * points : (d * sub + i + 1) * points]
+                    if direct:
+                        outs[d][:, at] = value.astype(outs[d].dtype)
+                    else:
+                        outs[0][chunk * split + d, :, at] = value.astype(jnp.bfloat16)
+
+    def passes(*accs):
+        if n_dest == split:
+            one_pass(0, accs[:2], accs[2:])
+        else:
+            lax.fori_loop(0, n_dest // split, lambda c, x: (one_pass(c, accs[:2], accs[2:]), x)[1], 0)
+
+    pl.run_scoped(
+        passes,
+        *[pltpu.ACC(n)((group * points, MXU), jnp.float32) for n in range(2)],
+        *[pltpu.ACC(n)((2 * points, MXU), jnp.float32) for n in range(2)],
+    )
 
 
 def net_kernel(n_chunks, pattern, *refs):
@@ -232,7 +234,6 @@
     own = parts[0]
     n_parts = len(parts)
     split = min(n_dest, DEST_CHUNK)
-    sub = max(1, DOT_ROWS // (split * points))
     if direct:
         out_shape = [
             jax.ShapeDtypeStruct((points, seg_dev), jnp.bfloat16 if d else jnp.float32)
@@ -240,26 +241,25 @@
         ]
     else:
         out_shape = [jax.ShapeDtypeStruct((n_dest, points, seg_dev), jnp.bfloat16)]
-    width = STEP_BLOCKS * LANES
-    seg_sub = seg_dev // sub
-    slot = [
-        pltpu.VMEM((n_dest * sub * points, width), jnp.bfloat16),
-        pltpu.VMEM((seg_sub, width), jnp.bfloat16),
-    ]
+    slot = pltpu.VMEM((split * seg_dev // (2 * MXU) * points, MXU), jnp.bfloat16)
     vmem = pl.BlockSpec(memory_space=pltpu.VMEM)
     smem = pl.BlockSpec(memory_space=pltpu.SMEM)
+    hbm = pl.BlockSpec(memory_space=pl.ANY)
     return pl.pallas_call(
-        functools.partial(loss_kernel, n_parts, n_dest, split, sub, direct, first_point),
+        functools.partial(loss_kernel, n_parts, n_dest, split, direct, first_point),
         out_shape=out_shape,
-        in_specs=[smem, smem] + [vmem] * (n_parts + 4),
+        in_specs=[smem, smem] + [vmem] * n_parts + [hbm] * 4,
         out_specs=[vmem] * len(out_shape),
         scratch_shapes=[
             pltpu.VMEM((2, own.shape[1] * n_parts // LANES, points, LANES), jnp.bfloat16),
-            pltpu.VMEM((n_dest * sub, points, seg_sub), jnp.float32),
-            pltpu.VMEM((points, width), jnp.float32),
-            pltpu.VMEM((points, width), jnp.float32),
-        ]
-        + slot * 2,
+            pltpu.VMEM((blocks, 256, LANES), jnp.bfloat16),
+            pltpu.VMEM((blocks, LANES), jnp.float32),
+            pltpu.VMEM((blocks, LANES), jnp.float32),
+            pltpu.VMEM((blocks, LANES), jnp.int32),
+            slot,
+            slot,
+            pltpu.SemaphoreType.DMA((4,)),
+        ],
         compiler_params=pltpu.CompilerParams(vmem_limit_bytes=VMEM_LIMIT),
         name="loss",
     )(

time: 70 us -> 61.7 us (0.88)
  Pallas kernels: 35.8 us -> 27.4 us
    pallas_call x2, Pallas kernels: 33.6 us -> 25.2 us  [loss_call(): pl.pallas_call(functools.partial(loss_kernel, n_parts, n_dest, split, dir...]
  transfers between devices with their start and end apart: 12 -> 12, of which waited for: 5 -> 5; matrix products, arithmetic and copies ran while one was open for 1% -> 2% of each run, Pallas kernels for 24% -> 21%
where the time goes in v3:
time: 61.7 us; the launch traced here: 61.2 us
  Pallas kernels  27.4 us (44%)
  starting transfers between devices  14.4 us (23%)
  waiting for transfers between devices  11.9 us (19%)
  local copies, waits for them, and re-layouts  5.51 us (9%)
  other arithmetic  1.35 us (2%)
  between operations  0.69 us (1%)
    pallas_call x2, Pallas kernels, loss_call(): pl.pallas_call(functools.partial(loss_kernel, n_parts, n_dest, split, dir...  25.2 us
    ppermute x6, starting transfers between devices, shifted(): return lax.ppermute(x, axis, [(i, (i + k) % n) for i in range(n)])  9.42 us
    ppermute x6, waiting for transfers between devices, shifted(): return lax.ppermute(x, axis, [(i, (i + k) % n) for i in range(n)])  8.01 us
    unnamed x15, local copies, waits for them, and re-layouts  5.24 us
    ppermute x6, starting transfers between devices, swapped(): lax.ppermute(x, axis, [(i, i ^ k) for i in range(lax.axis_size(axis))])  4.98 us
    ppermute x6, waiting for transfers between devices, swapped(): lax.ppermute(x, axis, [(i, i ^ k) for i in range(lax.axis_size(axis))])  3.92 us
    pallas_call x1, Pallas kernels, body(): pl.pallas_call(functools.partial(net_kernel, CHUNKS), out_shape=[jax.Shap...  2.14 us
  transfers between devices with their start and end apart: 12, of which 5 were waited for; matrix products, arithmetic and copies ran while one was open for 2% of the time, Pallas kernels for 21%

profile of v3, /device:TPU:0, one launch (start us, length us, event | category | flops | bytes accessed | tf_op | source)
XLA Modules:
  0.0 61.2 jit_solution(1018405227834291465)
XLA Ops:
  0.6 0.0 copy-start.5
  0.6 0.7 %pad_add_fusion.refs_0_ = s32[2,2048]{1,0:T(2,128)S(1)} fusion(s32[1,2048]{1,0:T(1,128)} %bitcast.22, s32[1,2048]{1,0:T(1,128)} %bitcast.23), kind=kLoop, calls=%fused_computation | loop fusion | flops 4096 | bytes 32768 | tf_op jit(solution)/shard_map/stack | solution.py:310
  1.4 2.4 %collective-permute-start.2 = (s32[2,2048]{1,0:T(2,128)S(1)}, s32[2,2048]{1,0:T(2,128)S(1)}, u32[]{:S(2)}, u32[]{:S(2)}) collective-permute-start(s32[2,2048]{1,0:T(2,128)S(1)} %pad_add_fusion.refs_0_), channel_id=1, source_target_pairs={{0,3},{1,2},{2,1},{3,0},{4,7},{5,6},{6,5},{7,4},{8,11},{9,10},{10,... | collective-permute-start | bytes 49160 | tf_op jit(solution)/shard_map/ppermute | solution.py:282
  3.8 0.6 %collective-permute-start.1 = (s32[2,2048]{1,0:T(2,128)S(1)}, s32[2,2048]{1,0:T(2,128)S(1)}, u32[]{:S(2)}, u32[]{:S(2)}) collective-permute-start(s32[2,2048]{1,0:T(2,128)S(1)} %pad_add_fusion.refs_0_), channel_id=1, source_target_pairs={{0,2},{1,3},{2,0},{3,1},{4,6},{5,7},{6,4},{7,5},{8,10},{9,11},{10,... | collective-permute-start | bytes 49160 | tf_op jit(solution)/shard_map/ppermute | solution.py:282
  4.5 0.0 collective-permute-start
  4.5 0.8 %copy.11 = s32[64,4]{1,0:T(8,128)S(1)} copy(s32[64,4]{0,1:T(4,128)} %param.12) | data formatting | bytes 2048 | tf_op args[3]
  5.3 0.1 reshape.31.pattern
  5.4 0.1 stack.36.meta
  5.5 0.0 collective-permute-done.2.refs_3_
  5.5 2.1 %collective-permute-done.1.refs_2_ = s32[2,2048]{1,0:T(2,128)S(1)} collective-permute-done((s32[2,2048]{1,0:T(2,128)S(1)}, s32[2,2048]{1,0:T(2,128)S(1)}, u32[]{:S(2)}, u32[]{:S(2)}) %collective-permute-start.1) | collective-permute-done | bytes 16416 | tf_op jit(solution)/shard_map/ppermute | solution.py:282
  7.6 0.0 collective-permute-done.refs_1_
  7.6 0.0 copy-start
  7.6 2.2 %copy-done = bf16[64,4,64,128]{3,2,1,0:T(8,128)(2,1)S(1)} copy-done((bf16[64,4,64,128]{3,2,1,0:T(8,128)(2,1)S(1)}, bf16[64,4,64,128]{3,2,1,0:T(8,128)(2,1)}, u32[]{:S(2)}) %copy-start) | copy-done | bytes 4194328
  9.8 0.0 copy-start.2
  9.8 0.8 %copy-done.2 = f32[8192]{0:T(1024)S(1)} copy-done((f32[8192]{0:T(1024)S(1)}, f32[8192]{0:T(1024)}, u32[]{:S(2)}) %copy-start.2) | copy-done | bytes 32792
  10.5 0.0 copy-start.3
  10.5 0.8 %copy-done.3 = f32[8192]{0:T(1024)S(1)} copy-done((f32[8192]{0:T(1024)S(1)}, f32[8192]{0:T(1024)}, u32[]{:S(2)}) %copy-start.3) | copy-done | bytes 32792
  11.3 0.0 copy-start.4
  11.3 0.8 %copy-done.4 = s32[8192]{0:T(1024)S(1)} copy-done((s32[8192]{0:T(1024)S(1)}, s32[8192]{0:T(1024)}, u32[]{:S(2)}) %copy-start.4) | copy-done | bytes 32792
  12.0 0.0 copy-start.6
  12.0 0.0 copy-start.1
  12.0 12.6 %loss.3 = (f32[64,1024]{1,0:T(8,128)S(1)}, bf16[64,1024]{1,0:T(8,128)(2,1)S(1)}, bf16[64,1024]{1,0:T(8,128)(2,1)}, bf16[64,1024]{1,0:T(8,128)(2,1)}) custom-call(s32[6]{0:T(128)S(1)} %stack.36.meta, s32[256]{0:T(256)S(1)} %reshape.31.pattern, s32[2,2048]{1,0:T(2,128)S(1)} %pad_add_fusion.refs_0_, s32[2,2048]{1,0:T(2,128)S(1)} %collective-permute-done.refs_1_, ...), custom_call_target="tpu_custom_call" | custom-call | tf_op jit(solution)/shard_map/loss/pallas_call | solution.py:248
  24.7 1.6 %collective-permute-start.6 = (bf16[64,1024]{1,0:T(8,128)(2,1)S(1)}, bf16[64,1024]{1,0:T(8,128)(2,1)S(1)}, u32[]{:S(2)}, u32[]{:S(2)}) collective-permute-start(bf16[64,1024]{1,0:T(8,128)(2,1)S(1)} %get-tuple-element.17), channel_id=1, source_target_pairs={{0,4},{4,8},{8,12},{12,0},{1,5},{5,9},{9,13},{13,1},{2,6},{6,10},{... | collective-permute-start | bytes 393224 | tf_op jit(solution)/shard_map/ppermute | solution.py:278
  26.3 2.6 %collective-permute-start.7 = (bf16[64,1024]{1,0:T(8,128)(2,1)}, bf16[64,1024]{1,0:T(8,128)(2,1)S(1)}, u32[]{:S(2)}, u32[]{:S(2)}) collective-permute-start(bf16[64,1024]{1,0:T(8,128)(2,1)} %get-tuple-element.18), channel_id=1, source_target_pairs={{0,8},{4,12},{8,0},{12,4},{1,9},{5,13},{9,1},{13,5},{2,10},{6,14},... | collective-permute-start | bytes 393224 | tf_op jit(solution)/shard_map/ppermute | solution.py:278
  28.9 1.3 %collective-permute-start.8 = (bf16[64,1024]{1,0:T(8,128)(2,1)}, bf16[64,1024]{1,0:T(8,128)(2,1)S(1)}, u32[]{:S(2)}, u32[]{:S(2)}) collective-permute-start(bf16[64,1024]{1,0:T(8,128)(2,1)} %get-tuple-element.19), channel_id=1, source_target_pairs={{0,12},{4,0},{8,4},{12,8},{1,13},{5,1},{9,5},{13,9},{2,14},{6,2},{... | collective-permute-start | bytes 393224 | tf_op jit(solution)/shard_map/ppermute | solution.py:278
  30.2 0.0 copy-done.5
  30.2 12.6 %loss.2 = (f32[64,1024]{1,0:T(8,128)S(1)}, bf16[64,1024]{1,0:T(8,128)(2,1)}, bf16[64,1024]{1,0:T(8,128)(2,1)}, bf16[64,1024]{1,0:T(8,128)(2,1)}) custom-call(s32[6]{0:T(128)S(1)} %stack.36.meta, s32[256]{0:T(256)S(1)} %reshape.31.pattern, s32[2,2048]{1,0:T(2,128)S(1)} %pad_add_fusion.refs_0_, s32[2,2048]{1,0:T(2,128)S(1)} %collective-permute-done.refs_1_, ...), custom_call_target="tpu_custom_call" | custom-call | tf_op jit(solution)/shard_map/loss/pallas_call | solution.py:248
  42.8 0.7 %collective-permute-start.3 = (bf16[64,1024]{1,0:T(8,128)(2,1)}, bf16[64,1024]{1,0:T(8,128)(2,1)S(1)}, u32[]{:S(2)}, u32[]{:S(2)}) collective-permute-start(bf16[64,1024]{1,0:T(8,128)(2,1)} %get-tuple-element.13), channel_id=1, source_target_pairs={{0,4},{4,8},{8,12},{12,0},{1,5},{5,9},{9,13},{13,1},{2,6},{6,10},{... | collective-permute-start | bytes 393224 | tf_op jit(solution)/shard_map/ppermute | solution.py:278
  43.6 0.3 collective-permute-start.4
  43.9 0.0 collective-permute-done.6.refs_5_
  43.9 2.8 %collective-permute-start.5 = (bf16[64,1024]{1,0:T(8,128)(2,1)}, bf16[64,1024]{1,0:T(8,128)(2,1)S(1)}, u32[]{:S(2)}, u32[]{:S(2)}) collective-permute-start(bf16[64,1024]{1,0:T(8,128)(2,1)} %get-tuple-element.15), channel_id=1, source_target_pairs={{0,12},{4,0},{8,4},{12,8},{1,13},{5,1},{9,5},{13,9},{2,14},{6,2},{... | collective-permute-start | bytes 393224 | tf_op jit(solution)/shard_map/ppermute | solution.py:278
  46.7 0.0 copy-done.6
  46.7 0.1 reshape.30.pattern
  46.8 0.0 collective-permute-done.7.refs_6_
  46.8 0.0 collective-permute-done.8.refs_7_
  46.8 4.6 %collective-permute-done.3.refs_1_ = bf16[64,1024]{1,0:T(8,128)(2,1)S(1)} collective-permute-done((bf16[64,1024]{1,0:T(8,128)(2,1)}, bf16[64,1024]{1,0:T(8,128)(2,1)S(1)}, u32[]{:S(2)}, u32[]{:S(2)}) %collective-permute-start.3) | collective-permute-done | bytes 131104 | tf_op jit(solution)/shard_map/ppermute | solution.py:278
  51.4 3.4 %collective-permute-done.4.refs_2_ = bf16[64,1024]{1,0:T(8,128)(2,1)S(1)} collective-permute-done((bf16[64,1024]{1,0:T(8,128)(2,1)}, bf16[64,1024]{1,0:T(8,128)(2,1)S(1)}, u32[]{:S(2)}, u32[]{:S(2)}) %collective-permute-start.4) | collective-permute-done | bytes 131104 | tf_op jit(solution)/shard_map/ppermute | solution.py:278
  54.8 0.0 collective-permute-done.5.refs_3_
  54.8 0.0 copy-done.1
  54.8 2.1 %net.1 = (f32[128,1024]{1,0:T(8,128)}, f32[2,1024]{1,0:T(2,128)S(1)}) custom-call(s32[64]{0:T(128)S(1)} %reshape.30.pattern, f32[64,1024]{1,0:T(8,128)S(1)} %get-tuple-element.12.refs_0_, bf16[64,1024]{1,0:T(8,128)(2,1)S(1)} %collective-permute-done.3.refs_1_, bf16[64,1024]{1,0:T(8,128)(2,1)S(1)} %collective-permute-done.4.refs_2_, ...), custom_call_target="tpu_custom_call" | custom-call | tf_op jit(solution)/shard_map/net/pallas_call | solution.py:344
  57.0 0.0 collective-permute-start.11
  57.0 0.8 %collective-permute-start.10 = (f32[2,1024]{1,0:T(2,128)S(1)}, f32[2,1024]{1,0:T(2,128)S(1)}, u32[]{:S(2)}, u32[]{:S(2)}) collective-permute-start(f32[2,1024]{1,0:T(2,128)S(1)} %get-tuple-element.21), channel_id=1, source_target_pairs={{0,2},{1,3},{2,0},{3,1},{4,6},{5,7},{6,4},{7,5},{8,10},{9,11},{10,... | collective-permute-start | bytes 24584 | tf_op jit(solution)/shard_map/ppermute | solution.py:282
  57.7 1.1 %collective-permute-start.9 = (f32[2,1024]{1,0:T(2,128)S(1)}, f32[2,1024]{1,0:T(2,128)S(1)}, u32[]{:S(2)}, u32[]{:S(2)}) collective-permute-start(f32[2,1024]{1,0:T(2,128)S(1)} %get-tuple-element.21), channel_id=1, source_target_pairs={{0,1},{1,0},{2,3},{3,2},{4,5},{5,4},{6,7},{7,6},{8,9},{9,8},{10,11... | collective-permute-start | bytes 24584 | tf_op jit(solution)/shard_map/ppermute | solution.py:282
  58.8 1.2 %collective-permute-done.11 = f32[2,1024]{1,0:T(2,128)S(1)} collective-permute-done((f32[2,1024]{1,0:T(2,128)S(1)}, f32[2,1024]{1,0:T(2,128)S(1)}, u32[]{:S(2)}, u32[]{:S(2)}) %collective-permute-start.11) | collective-permute-done | bytes 8224 | tf_op jit(solution)/shard_map/ppermute | solution.py:282
  60.0 0.6 collective-permute-done.10
  60.6 0.0 collective-permute-done.9
  60.6 0.6 add_multiply_fusion
Async XLA Ops:
  0.6 29.6 %copy-start.5 = (s32[8192]{0:T(1024)S(1)}, s32[8192]{0:T(1024)}, u32[]{:S(2)}) copy-start(s32[8192]{0:T(1024)} %param.15) | copy-start | bytes 98308
  1.4 4.1 %collective-permute-start.2 = (s32[2,2048]{1,0:T(2,128)S(1)}, s32[2,2048]{1,0:T(2,128)S(1)}, u32[]{:S(2)}, u32[]{:S(2)}) collective-permute-start(s32[2,2048]{1,0:T(2,128)S(1)} %pad_add_fusion.refs_0_), channel_id=1, source_target_pairs={{0,3},{1,2},{2,1},{3,0},{4,7},{5,6},{6,5},{7,4},{8,11},{9,10},{10,... | collective-permute-start | bytes 49160 | tf_op jit(solution)/shard_map/ppermute | solution.py:282
  3.8 3.7 %collective-permute-start.1 = (s32[2,2048]{1,0:T(2,128)S(1)}, s32[2,2048]{1,0:T(2,128)S(1)}, u32[]{:S(2)}, u32[]{:S(2)}) collective-permute-start(s32[2,2048]{1,0:T(2,128)S(1)} %pad_add_fusion.refs_0_), channel_id=1, source_target_pairs={{0,2},{1,3},{2,0},{3,1},{4,6},{5,7},{6,4},{7,5},{8,10},{9,11},{10,... | collective-permute-start | bytes 49160 | tf_op jit(solution)/shard_map/ppermute | solution.py:282
  4.5 3.1 %collective-permute-start = (s32[2,2048]{1,0:T(2,128)S(1)}, s32[2,2048]{1,0:T(2,128)S(1)}, u32[]{:S(2)}, u32[]{:S(2)}) collective-permute-start(s32[2,2048]{1,0:T(2,128)S(1)} %pad_add_fusion.refs_0_), channel_id=1, source_target_pairs={{0,1},{1,0},{2,3},{3,2},{4,5},{5,4},{6,7},{7,6},{8,9},{9,8},{10,11... | collective-permute-start | bytes 49160 | tf_op jit(solution)/shard_map/ppermute | solution.py:282
  7.6 2.2 %copy-start = (bf16[64,4,64,128]{3,2,1,0:T(8,128)(2,1)S(1)}, bf16[64,4,64,128]{3,2,1,0:T(8,128)(2,1)}, u32[]{:S(2)}) copy-start(bf16[64,4,64,128]{3,2,1,0:T(8,128)(2,1)} %param.11) | copy-start | bytes 12582916
  9.8 0.8 %copy-start.2 = (f32[8192]{0:T(1024)S(1)}, f32[8192]{0:T(1024)}, u32[]{:S(2)}) copy-start(f32[8192]{0:T(1024)} %param.13) | copy-start | bytes 98308
  10.5 0.8 %copy-start.3 = (f32[8192]{0:T(1024)S(1)}, f32[8192]{0:T(1024)}, u32[]{:S(2)}) copy-start(f32[8192]{0:T(1024)} %param.14) | copy-start | bytes 98308
  11.3 0.8 %copy-start.4 = (s32[8192]{0:T(1024)S(1)}, s32[8192]{0:T(1024)}, u32[]{:S(2)}) copy-start(s32[8192]{0:T(1024)} %param.15) | copy-start | bytes 98308
  12.0 34.7 %copy-start.6 = (s32[8,8]{1,0:T(8,128)S(1)}, s32[8,8]{1,0:T(8,128)}, u32[]{:S(2)}) copy-start(s32[8,8]{1,0:T(8,128)} %param.17) | copy-start | bytes 772
  12.0 42.8 %copy-start.1 = (bf16[8,8,128,128]{3,2,1,0:T(8,128)(2,1)S(1)}, bf16[8,8,128,128]{3,2,1,0:T(8,128)(2,1)}, u32[]{:S(2)}) copy-start(bf16[8,8,128,128]{3,2,1,0:T(8,128)(2,1)} %param.16) | copy-start | bytes 6291460
  24.7 19.3 %collective-permute-start.6 = (bf16[64,1024]{1,0:T(8,128)(2,1)S(1)}, bf16[64,1024]{1,0:T(8,128)(2,1)S(1)}, u32[]{:S(2)}, u32[]{:S(2)}) collective-permute-start(bf16[64,1024]{1,0:T(8,128)(2,1)S(1)} %get-tuple-element.17), channel_id=1, source_target_pairs={{0,4},{4,8},{8,12},{12,0},{1,5},{5,9},{9,13},{13,1},{2,6},{6,10},{... | collective-permute-start | bytes 393224 | tf_op jit(solution)/shard_map/ppermute | solution.py:278
  26.3 20.5 %collective-permute-start.7 = (bf16[64,1024]{1,0:T(8,128)(2,1)}, bf16[64,1024]{1,0:T(8,128)(2,1)S(1)}, u32[]{:S(2)}, u32[]{:S(2)}) collective-permute-start(bf16[64,1024]{1,0:T(8,128)(2,1)} %get-tuple-element.18), channel_id=1, source_target_pairs={{0,8},{4,12},{8,0},{12,4},{1,9},{5,13},{9,1},{13,5},{2,10},{6,14},... | collective-permute-start | bytes 393224 | tf_op jit(solution)/shard_map/ppermute | solution.py:278
  28.9 17.9 %collective-permute-start.8 = (bf16[64,1024]{1,0:T(8,128)(2,1)}, bf16[64,1024]{1,0:T(8,128)(2,1)S(1)}, u32[]{:S(2)}, u32[]{:S(2)}) collective-permute-start(bf16[64,1024]{1,0:T(8,128)(2,1)} %get-tuple-element.19), channel_id=1, source_target_pairs={{0,12},{4,0},{8,4},{12,8},{1,13},{5,1},{9,5},{13,9},{2,14},{6,2},{... | collective-permute-start | bytes 393224 | tf_op jit(solution)/shard_map/ppermute | solution.py:278
  42.8 8.6 %collective-permute-start.3 = (bf16[64,1024]{1,0:T(8,128)(2,1)}, bf16[64,1024]{1,0:T(8,128)(2,1)S(1)}, u32[]{:S(2)}, u32[]{:S(2)}) collective-permute-start(bf16[64,1024]{1,0:T(8,128)(2,1)} %get-tuple-element.13), channel_id=1, source_target_pairs={{0,4},{4,8},{8,12},{12,0},{1,5},{5,9},{9,13},{13,1},{2,6},{6,10},{... | collective-permute-start | bytes 393224 | tf_op jit(solution)/shard_map/ppermute | solution.py:278
  43.6 11.2 %collective-permute-start.4 = (bf16[64,1024]{1,0:T(8,128)(2,1)}, bf16[64,1024]{1,0:T(8,128)(2,1)S(1)}, u32[]{:S(2)}, u32[]{:S(2)}) collective-permute-start(bf16[64,1024]{1,0:T(8,128)(2,1)} %get-tuple-element.14), channel_id=1, source_target_pairs={{0,8},{4,12},{8,0},{12,4},{1,9},{5,13},{9,1},{13,5},{2,10},{6,14},... | collective-permute-start | bytes 393224 | tf_op jit(solution)/shard_map/ppermute | solution.py:278
  43.9 10.9 %collective-permute-start.5 = (bf16[64,1024]{1,0:T(8,128)(2,1)}, bf16[64,1024]{1,0:T(8,128)(2,1)S(1)}, u32[]{:S(2)}, u32[]{:S(2)}) collective-permute-start(bf16[64,1024]{1,0:T(8,128)(2,1)} %get-tuple-element.15), channel_id=1, source_target_pairs={{0,12},{4,0},{8,4},{12,8},{1,13},{5,1},{9,5},{13,9},{2,14},{6,2},{... | collective-permute-start | bytes 393224 | tf_op jit(solution)/shard_map/ppermute | solution.py:278
  57.0 3.1 %collective-permute-start.11 = (f32[2,1024]{1,0:T(2,128)S(1)}, f32[2,1024]{1,0:T(2,128)S(1)}, u32[]{:S(2)}, u32[]{:S(2)}) collective-permute-start(f32[2,1024]{1,0:T(2,128)S(1)} %get-tuple-element.21), channel_id=1, source_target_pairs={{0,3},{1,2},{2,1},{3,0},{4,7},{5,6},{6,5},{7,4},{8,11},{9,10},{10,... | collective-permute-start | bytes 24584 | tf_op jit(solution)/shard_map/ppermute | solution.py:282
  57.0 3.7 %collective-permute-start.10 = (f32[2,1024]{1,0:T(2,128)S(1)}, f32[2,1024]{1,0:T(2,128)S(1)}, u32[]{:S(2)}, u32[]{:S(2)}) collective-permute-start(f32[2,1024]{1,0:T(2,128)S(1)} %get-tuple-element.21), channel_id=1, source_target_pairs={{0,2},{1,3},{2,0},{3,1},{4,6},{5,7},{6,4},{7,5},{8,10},{9,11},{10,... | collective-permute-start | bytes 24584 | tf_op jit(solution)/shard_map/ppermute | solution.py:282
  57.7 2.9 %collective-permute-start.9 = (f32[2,1024]{1,0:T(2,128)S(1)}, f32[2,1024]{1,0:T(2,128)S(1)}, u32[]{:S(2)}, u32[]{:S(2)}) collective-permute-start(f32[2,1024]{1,0:T(2,128)S(1)} %get-tuple-element.21), channel_id=1, source_target_pairs={{0,1},{1,0},{2,3},{3,2},{4,5},{5,4},{6,7},{7,6},{8,9},{9,8},{10,11... | collective-permute-start | bytes 24584 | tf_op jit(solution)/shard_map/ppermute | solution.py:282

commit v4 on v3

--- a/solution.py
+++ b/solution.py
@@ -12,8 +12,9 @@
 ROWS = 16
 DEST_CHUNK = 4
 MXU = 256
-CHUNKS = 2
+CHUNKS = (64, 64)
 VMEM_LIMIT = 48 << 20
+NET_VMEM = 24 << 20
 
 QUANTILE_MID = 2.6095163822174072
 QUANTILE = (
@@ -69,15 +70,41 @@
     return exposure * jnp.where(t > 0.0, 1.0 - tail, tail)
 
 
+def fill_panel(panel, first, part, first_point):
+    points = panel.shape[2]
+    row = lax.broadcasted_iota(jnp.int32, (ROWS, LANES), 0) + first_point
+
+    def fill(c, carry):
+        at = pl.ds(pl.multiple_of(c * LANES, LANES), LANES)
+        gen = part[0:1, at]
+        shift = part[1:2, at]
+        scaled = lax.shift_left(row * gen, 23) + (lax.shift_left(shift, 13) + (4096 - 2**31))
+        jump = lax.shift_left(gen, 27)
+        for r in range(points // ROWS):
+            value = quantile(scaled).astype(jnp.bfloat16)
+            rows = pl.ds(r * ROWS, ROWS)
+            panel[0, first + c, rows, :] = value
+            panel[1, first + c, rows, :] = pltpu.roll(value, LANES // 2, 1)
+            scaled = scaled + jump
+        return carry
+
+    lax.fori_loop(0, part.shape[1] // LANES, fill, 0, unroll=max(1, 1024 // points))
+
+
+def panel_kernel(meta, part, panel):
+    fill_panel(panel, 0, part, meta[0])
+
+
 def loss_kernel(n_parts, n_dest, split, direct, first_point, meta, pattern, *refs):
-    parts = refs[:n_parts]
+    own_panel = refs[0]
+    parts = refs[1:n_parts]
     sources = refs[n_parts : n_parts + 4]
     outs = refs[n_parts + 4 : -8]
     panel, load_ref, thr_ref, expo_ref, seg_ref, even, odd, sems = refs[-8:]
     masked = (even, odd)
     points = panel.shape[2]
     blocks = load_ref.shape[0]
-    columns = parts[0].shape[1] // LANES
+    columns = own_panel.shape[1]
     seg_dev = (outs[0] if direct else outs[0].at[0]).shape[1]
     sub = seg_dev // (2 * MXU)
     group = split * sub
@@ -90,31 +117,19 @@
     for copy in copies:
         copy.start()
 
-    row = lax.broadcasted_iota(jnp.int32, (ROWS, LANES), 0) + (meta[0] + first_point)
-    for k in range(n_parts):
-        first = meta[2 + k] * columns
-
-        def fill(c, carry, k=k, first=first):
-            at = pl.ds(pl.multiple_of(c * LANES, LANES), LANES)
-            gen = parts[k][0:1, at]
-            shift = parts[k][1:2, at]
-            scaled = lax.shift_left(row * gen, 23) + (lax.shift_left(shift, 13) + (4096 - 2**31))
-            jump = lax.shift_left(gen, 27)
-            for r in range(points // ROWS):
-                value = quantile(scaled)
-                rows = pl.ds(r * ROWS, ROWS)
-                panel[0, first + c, rows, :] = value.astype(jnp.bfloat16)
-                panel[1, first + c, rows, :] = pltpu.roll(value, LANES // 2, 1).astype(jnp.bfloat16)
-                scaled = scaled + jump
-            return carry
-
-        lax.fori_loop(0, columns, fill, 0, unroll=8)
+    def reuse(c, carry):
+        panel[:, meta[2] * columns + c] = own_panel[:, c, first_point : first_point + points, :]
+        return carry
+
+    lax.fori_loop(0, columns, reuse, 0, unroll=4)
+    for k in range(1, n_parts):
+        fill_panel(panel, meta[2 + k] * columns, parts[k - 1], meta[0] + first_point)
 
     for copy in copies:
         copy.wait()
 
     low = lax.broadcasted_iota(jnp.int32, (points, LANES), 1) < LANES // 2
-    seg_row = lax.broadcasted_iota(jnp.int32, (MXU, LANES), 0)
+    seg_row = lax.broadcasted_iota(jnp.int32, (ROWS, LANES), 0)
 
     def picked(b):
         halves = []
@@ -137,8 +152,22 @@
 
         def push_onehot(step, parity):
             local = [seg_ref[pl.ds(2 * step + j, 1), :] & (2 * MXU - 1) for j in range(2)]
+            low_rows = [jnp.where(seg_row == (at & (ROWS - 1)), 1.0, 0.0).astype(jnp.bfloat16) for at in local]
+            high = [
+                jnp.broadcast_to(lax.shift_right_logical(at, 4), (ROWS, LANES)).astype(jnp.int16)
+                for at in local
+            ]
             for n in range(2):
-                tile = [jnp.where(seg_row == at - n * MXU, 1.0, 0.0).astype(jnp.bfloat16) for at in local]
+                tile = [
+                    jnp.concatenate(
+                        [
+                            jnp.where(high[j] == jnp.int16(n * MXU // ROWS + r), low_rows[j], jnp.bfloat16(0))
+                            for r in range(MXU // ROWS)
+                        ],
+                        axis=0,
+                    )
+                    for j in range(2)
+                ]
                 pltpu.matmul_push_rhs(jnp.concatenate(tile, axis=1), parity, n, transpose=True)
 
         def add_up(parity):
@@ -154,9 +183,13 @@
                 prob = weighted_prob(t, expo_ref[one, :]).astype(jnp.bfloat16)
                 part = lax.shift_right_logical(seg_ref[one, :], (2 * MXU).bit_length() - 1) - meta[1] * sub
                 part = jnp.where(part < 0, part + n_dest * sub, part) - chunk * group
+                part = jnp.broadcast_to(part, (ROWS, LANES)).astype(jnp.int16)
                 for d in range(group):
-                    mine = jnp.where(part == d, 1.0, 0.0).astype(jnp.bfloat16)
-                    masked[parity][d * points : (d + 1) * points, here] = prob * mine
+                    mine = part == jnp.int16(d)
+                    for r in range(0, points, ROWS):
+                        masked[parity][d * points + r : d * points + r + ROWS, here] = jnp.where(
+                            mine, prob[r : r + ROWS], jnp.bfloat16(0)
+                        )
 
         def stage(step, parity, ahead=True, behind=True):
             push_onehot(step, parity)
@@ -202,37 +235,68 @@
     )
 
 
-def net_kernel(n_chunks, pattern, *refs):
-    tiles_ref, net_ref, sums_ref, losses = refs[-4:]
-    received = refs[:-4]
+def net_kernel(first_point, n_received, pattern, tiles_ref, *refs):
+    received = refs[:n_received]
+    out_ref, sums_ref, losses, net_rows, sem = refs[-5:]
+    before = refs[n_received : -5]
     blocks = tiles_ref.shape[0]
+    points = losses.shape[1]
     slots = tiles_ref.shape[1] // LANES
-    count = len(received) // n_chunks
-    points = losses.shape[1] // n_chunks
-    for c in range(n_chunks):
-        mine = received[c * count : (c + 1) * count]
-        for q in range(blocks):
-            at = slice(q * LANES, (q + 1) * LANES)
-            if count == 1:
-                total = jnp.sum(mine[0][:, :, at].astype(jnp.float32), axis=0)
-            else:
-                total = mine[0][:, at]
-                for ref in mine[1:]:
-                    total = total + ref[:, at].astype(jnp.float32)
-            losses[q, c * points : (c + 1) * points] = total.astype(jnp.bfloat16)
+    for q in range(blocks):
+        at = slice(q * LANES, (q + 1) * LANES)
+        if n_received == 1:
+            total = jnp.sum(received[0][:, :, at].astype(jnp.float32), axis=0)
+        else:
+            total = received[0][:, at].astype(jnp.float32)
+            for ref in received[1:]:
+                total = total + ref[:, at].astype(jnp.float32)
+        losses[q] = total.astype(jnp.bfloat16)
     for b in range(blocks):
         at = slice(b * LANES, (b + 1) * LANES)
         picked = jnp.concatenate([losses[pattern[slots * b + k]] for k in range(slots)], axis=1)
         net = jnp.dot(picked, tiles_ref[b], preferred_element_type=jnp.float32)
-        net_ref[:, at] = net
-        sums_ref[0:1, at] = jnp.sum(net, axis=0, keepdims=True)
-        sums_ref[1:2, at] = jnp.sum(net * net, axis=0, keepdims=True)
-
-
-def loss_call(meta, pattern, parts, loadings, threshold, exposure, segment_map, n_dest, first_point, points, seg_dev, direct):
+        net_rows[:, at] = net
+        first = jnp.sum(net, axis=0, keepdims=True)
+        second = jnp.sum(net * net, axis=0, keepdims=True)
+        if before:
+            first += before[0][0:1, at]
+            second += before[0][1:2, at]
+        sums_ref[0:1, at] = first
+        sums_ref[1:2, at] = second
+    copy = pltpu.make_async_copy(net_rows, out_ref.at[pl.ds(first_point, points), :], sem)
+    copy.start()
+    copy.wait()
+
+
+def net_call(net_pattern, tiles, received, first_point, chunk, points, seg_dev, before):
+    vmem = pl.BlockSpec(memory_space=pltpu.VMEM)
+    hbm = pl.BlockSpec(memory_space=pltpu.HBM)
+    extra = [] if before is None else [before[1], before[0]]
+    return pl.pallas_call(
+        functools.partial(net_kernel, first_point, len(received)),
+        out_shape=[
+            jax.ShapeDtypeStruct((points, seg_dev), jnp.float32),
+            jax.ShapeDtypeStruct((2, seg_dev), jnp.float32),
+        ],
+        in_specs=[pl.BlockSpec(memory_space=pltpu.SMEM)]
+        + [vmem] * (1 + len(received))
+        + [vmem, hbm][: len(extra)],
+        out_specs=[hbm, vmem],
+        scratch_shapes=[
+            pltpu.VMEM((seg_dev // LANES, chunk, LANES), jnp.bfloat16),
+            pltpu.VMEM((chunk, seg_dev), jnp.float32),
+            pltpu.SemaphoreType.DMA,
+        ],
+        input_output_aliases={} if before is None else {3 + len(received): 0},
+        compiler_params=pltpu.CompilerParams(vmem_limit_bytes=NET_VMEM),
+        name="net",
+    )(net_pattern, tiles, *received, *extra)
+
+
+def loss_call(meta, pattern, own_panel, parts, loadings, threshold, exposure, segment_map, n_dest, first_point, points, seg_dev, direct):
     blocks = loadings.shape[0]
-    own = parts[0]
-    n_parts = len(parts)
+    n_parts = len(parts) + 1
+    columns = own_panel.shape[1] * n_parts
     split = min(n_dest, DEST_CHUNK)
     if direct:
         out_shape = [
@@ -244,14 +308,14 @@
     slot = pltpu.VMEM((split * seg_dev // (2 * MXU) * points, MXU), jnp.bfloat16)
     vmem = pl.BlockSpec(memory_space=pltpu.VMEM)
     smem = pl.BlockSpec(memory_space=pltpu.SMEM)
-    hbm = pl.BlockSpec(memory_space=pl.ANY)
+    hbm = pl.BlockSpec(memory_space=pltpu.HBM)
     return pl.pallas_call(
         functools.partial(loss_kernel, n_parts, n_dest, split, direct, first_point),
         out_shape=out_shape,
         in_specs=[smem, smem] + [vmem] * n_parts + [hbm] * 4,
         out_specs=[vmem] * len(out_shape),
         scratch_shapes=[
-            pltpu.VMEM((2, own.shape[1] * n_parts // LANES, points, LANES), jnp.bfloat16),
+            pltpu.VMEM((2, columns, points, LANES), jnp.bfloat16),
             pltpu.VMEM((blocks, 256, LANES), jnp.bfloat16),
             pltpu.VMEM((blocks, LANES), jnp.float32),
             pltpu.VMEM((blocks, LANES), jnp.float32),
@@ -265,6 +329,7 @@
     )(
         meta,
         pattern,
+        own_panel,
         *parts,
         loadings.reshape(blocks, 256, LANES),
         threshold.reshape(blocks, LANES),
@@ -308,51 +373,51 @@
     direct = n_dest <= 8
 
     own = jnp.stack([generator, lattice_shift])
-    parts = [own] + [swapped(own, "narrow", k) for k in range(1, n_narrow)]
+    parts = [swapped(own, "narrow", k) for k in range(1, n_narrow)]
     quarter = [me ^ k for k in range(n_narrow)]
     base = lax.axis_index("wide") if direct else 0
     meta = jnp.stack([me * points, jnp.int32(base)] + quarter).astype(jnp.int32)
 
+    vmem = pl.BlockSpec(memory_space=pltpu.VMEM)
+    own_panel = pl.pallas_call(
+        panel_kernel,
+        out_shape=jax.ShapeDtypeStruct((2, own.shape[1] // LANES, points, LANES), jnp.bfloat16),
+        in_specs=[pl.BlockSpec(memory_space=pltpu.SMEM), vmem],
+        out_specs=vmem,
+        name="panel",
+    )(meta, own)
+    pattern = load_pattern.reshape(-1)
     slots = net_tiles.shape[1]
     tiles = net_tiles.reshape(seg_blocks, slots * LANES, LANES)
-    chunk = points // CHUNKS
-    net_loss, sums = None, None
-    partials = [
-        loss_call(
+    chunks = []
+    first = 0
+    for chunk in CHUNKS:
+        chunk = chunk * points // sum(CHUNKS)
+        partial = loss_call(
             meta,
-            load_pattern.reshape(-1),
+            pattern,
+            own_panel,
             parts,
             loadings,
             threshold,
             exposure,
             segment_map,
             n_dest,
-            c * chunk,
+            first,
             chunk,
             seg_dev,
             direct,
         )
-        for c in range(CHUNKS)
-    ]
-    received = []
-    for partial in partials:
         if direct:
-            received += [partial[0]] + [shifted(partial[k], "wide", k) for k in range(1, n_dest)]
+            received = [partial[0]] + [shifted(partial[k], "wide", k) for k in range(1, n_dest)]
         else:
-            received += [lax.all_to_all(partial[0], "wide", split_axis=0, concat_axis=0, tiled=True)]
-    vmem = pl.BlockSpec(memory_space=pltpu.VMEM)
-    net_loss, sums = pl.pallas_call(
-        functools.partial(net_kernel, CHUNKS),
-        out_shape=[
-            jax.ShapeDtypeStruct((points, seg_dev), jnp.float32),
-            jax.ShapeDtypeStruct((2, seg_dev), jnp.float32),
-        ],
-        in_specs=[pl.BlockSpec(memory_space=pltpu.SMEM)] + [vmem] * (len(received) + 1),
-        out_specs=[vmem] * 2,
-        scratch_shapes=[pltpu.VMEM((seg_blocks, points, LANES), jnp.bfloat16)],
-        compiler_params=pltpu.CompilerParams(vmem_limit_bytes=VMEM_LIMIT),
-        name="net",
-    )(net_pattern.reshape(-1), *received, tiles)
+            received = [lax.all_to_all(partial[0], "wide", split_axis=0, concat_axis=0, tiled=True)]
+        chunks.append((first, chunk, received))
+        first += chunk
+    done = None
+    for first, chunk, received in chunks:
+        done = net_call(net_pattern.reshape(-1), tiles, received, first, chunk, points, seg_dev, done)
+    net_loss, sums = done
 
     total = pair_sum([sums] + [swapped(sums, "narrow", k) for k in range(1, n_narrow)])
     return (net_loss, total / P_SIZE)

time: 61.7 us -> 63.6 us (1.031)
  waiting for transfers between devices: 11.9 us -> 9.35 us
  local copies, waits for them, and re-layouts: 5.51 us -> 7.98 us
  Pallas kernels: 27.4 us -> 28.6 us
    pallas_call x1 -> x3, Pallas kernels: 2.14 us -> 6.88 us  [the longest x2 3.68 us: net_call(): pl.pallas_call(functools.partial(net_kernel, first_point, len(received)),...]
    pallas_call x2, Pallas kernels: 25.2 us -> 21.7 us  [loss_call(): pl.pallas_call(functools.partial(loss_kernel, n_parts, n_dest, split, dir...]
    unnamed x15 -> x19, local copies, waits for them, and re-layouts: 5.24 us -> 7.13 us
    ppermute x6, waiting for transfers between devices: 3.92 us -> 2.43 us  [swapped(): lax.ppermute(x, axis, [(i, i ^ k) for i in range(lax.axis_size(axis))])]
    ppermute x6, waiting for transfers between devices: 8.01 us -> 6.92 us  [shifted(): return lax.ppermute(x, axis, [(i, (i + k) % n) for i in range(n)])]
  transfers between devices with their start and end apart: 12 -> 12, of which waited for: 5 -> 4; matrix products, arithmetic and copies ran while one was open for 2% -> 3% of each run, Pallas kernels for 21% -> 25%
where the time goes in v4:
time: 63.6 us; the launch traced here: 63 us
  Pallas kernels  28.6 us (45%)
  starting transfers between devices  15 us (24%)
  waiting for transfers between devices  9.35 us (15%)
  local copies, waits for them, and re-layouts  7.98 us (13%)
  other arithmetic  1.34 us (2%)
  between operations  0.74 us (1%)
    pallas_call x2, Pallas kernels, loss_call(): pl.pallas_call(functools.partial(loss_kernel, n_parts, n_dest, split, dir...  21.7 us
    ppermute x6, starting transfers between devices, shifted(): return lax.ppermute(x, axis, [(i, (i + k) % n) for i in range(n)])  9.68 us
    unnamed x19, local copies, waits for them, and re-layouts  7.13 us
    ppermute x6, waiting for transfers between devices, shifted(): return lax.ppermute(x, axis, [(i, (i + k) % n) for i in range(n)])  6.92 us
    ppermute x6, starting transfers between devices, swapped(): lax.ppermute(x, axis, [(i, i ^ k) for i in range(lax.axis_size(axis))])  5.36 us
    pallas_call x2, Pallas kernels, net_call(): pl.pallas_call(functools.partial(net_kernel, first_point, len(received)),...  3.68 us
    pallas_call x1, Pallas kernels, body(): pl.pallas_call(panel_kernel, out_shape=jax.ShapeDtypeStruct((2, own.shape...  3.2 us
    ppermute x6, waiting for transfers between devices, swapped(): lax.ppermute(x, axis, [(i, i ^ k) for i in range(lax.axis_size(axis))])  2.43 us
  transfers between devices with their start and end apart: 12, of which 4 were waited for; matrix products, arithmetic and copies ran while one was open for 3% of the time, Pallas kernels for 25%

profile of v4, /device:TPU:0, one launch (start us, length us, event | category | flops | bytes accessed | tf_op | source)
XLA Modules:
  0.0 63.0 jit_solution(9571836660110523030)
XLA Ops:
  0.6 0.7 %pad_add_fusion.part = s32[2,2048]{1,0:T(2,128)S(1)} fusion(s32[1,2048]{1,0:T(1,128)} %bitcast.23, s32[1,2048]{1,0:T(1,128)} %bitcast.24), kind=kLoop, calls=%fused_computation | loop fusion | flops 4096 | bytes 32768 | tf_op jit(solution)/shard_map/stack | solution.py:375
  1.4 0.0 copy-start.7
  1.4 0.5 collective-permute-start
  1.9 2.6 %collective-permute-start.1 = (s32[2,2048]{1,0:T(2,128)S(1)}, s32[2,2048]{1,0:T(2,128)S(1)}, u32[]{:S(2)}, u32[]{:S(2)}) collective-permute-start(s32[2,2048]{1,0:T(2,128)S(1)} %pad_add_fusion.part), channel_id=1, source_target_pairs={{0,2},{1,3},{2,0},{3,1},{4,6},{5,7},{6,4},{7,5},{8,10},{9,11},{10,... | collective-permute-start | bytes 49160 | tf_op jit(solution)/shard_map/ppermute | solution.py:347
  4.5 0.1 collective-permute-start.2
  4.5 0.7 %stack.36.meta = s32[6]{0:T(128)} concatenate(s32[1]{0:T(128)} %bitcast.1, s32[1]{0:T(128)} %bitcast.2, s32[1]{0:T(128)} %bitcast.3, s32[1]{0:T(128)} %bitcast.4, s32[1]{0:T(128)} %bitcast.5, s32[1]{0:T(128)} %bitcast.6), dimensions={0} | concatenate | bytes 48 | tf_op jit(solution)/shard_map/stack | solution.py:379
  5.2 0.0 copy-done.7
  5.2 3.2 %panel.1.refs_0_ = bf16[2,16,128,128]{3,2,1,0:T(8,128)(2,1)} custom-call(s32[6]{0:T(128)} %stack.36.meta, s32[2,2048]{1,0:T(2,128)} %copy-done.7), custom_call_target="tpu_custom_call" | custom-call | tf_op jit(solution)/shard_map/panel/pallas_call | solution.py:382
  8.4 0.8 %copy.12 = s32[64,4]{1,0:T(8,128)S(1)} copy(s32[64,4]{0,1:T(4,128)} %param.12) | data formatting | bytes 2048 | tf_op args[3]
  9.2 0.1 reshape.32.pattern
  9.3 0.0 collective-permute-done.refs_1_
  9.3 0.0 collective-permute-done.1.refs_2_
  9.3 0.0 collective-permute-done.2.refs_3_
  9.3 0.0 copy-start
  9.3 2.2 %copy-done = bf16[64,4,64,128]{3,2,1,0:T(8,128)(2,1)S(1)} copy-done((bf16[64,4,64,128]{3,2,1,0:T(8,128)(2,1)S(1)}, bf16[64,4,64,128]{3,2,1,0:T(8,128)(2,1)}, u32[]{:S(2)}) %copy-start) | copy-done | bytes 4194328
  11.5 0.0 copy-start.1
  11.5 1.2 %copy-done.1 = bf16[2,16,128,128]{3,2,1,0:T(8,128)(2,1)S(1)} copy-done((bf16[2,16,128,128]{3,2,1,0:T(8,128)(2,1)S(1)}, bf16[2,16,128,128]{3,2,1,0:T(8,128)(2,1)}, u32[]{:S(2)}) %copy-start.1) | copy-done | bytes 1048600
  12.7 0.0 copy-start.3
  12.7 0.8 %copy-done.3 = f32[8192]{0:T(1024)S(1)} copy-done((f32[8192]{0:T(1024)S(1)}, f32[8192]{0:T(1024)}, u32[]{:S(2)}) %copy-start.3) | copy-done | bytes 32792
  13.5 0.8 %copy-done.4 = f32[8192]{0:T(1024)S(1)} copy-done((f32[8192]{0:T(1024)S(1)}, f32[8192]{0:T(1024)}, u32[]{:S(2)}) %copy-start.4) | copy-done | bytes 32792
  14.2 0.8 %copy-done.5 = s32[8192]{0:T(1024)S(1)} copy-done((s32[8192]{0:T(1024)S(1)}, s32[8192]{0:T(1024)}, u32[]{:S(2)}) %copy-start.5) | copy-done | bytes 32792
  15.0 0.7 %copy-done.6 = s32[6]{0:T(128)S(1)} copy-done((s32[6]{0:T(128)S(1)}, s32[6]{0:T(128)}, u32[]{:S(2)}) %copy-start.6) | copy-done | bytes 48
  15.7 10.8 %loss.3 = (f32[64,1024]{1,0:T(8,128)S(1)}, bf16[64,1024]{1,0:T(8,128)(2,1)S(1)}, bf16[64,1024]{1,0:T(8,128)(2,1)}, bf16[64,1024]{1,0:T(8,128)(2,1)}) custom-call(s32[6]{0:T(128)S(1)} %copy-done.6, s32[256]{0:T(256)S(1)} %reshape.32.pattern, bf16[2,16,128,128]{3,2,1,0:T(8,128)(2,1)S(1)} %copy-done.1, s32[2,2048]{1,0:T(2,128)S(1)} %collective-permute-done.refs_1_, ...), custom_call_target="tpu_custom_call" | custom-call | tf_op jit(solution)/shard_map/loss/pallas_call | solution.py:312
  26.5 1.9 %collective-permute-start.6 = (bf16[64,1024]{1,0:T(8,128)(2,1)S(1)}, bf16[64,1024]{1,0:T(8,128)(2,1)S(1)}, u32[]{:S(2)}, u32[]{:S(2)}) collective-permute-start(bf16[64,1024]{1,0:T(8,128)(2,1)S(1)} %get-tuple-element.19), channel_id=1, source_target_pairs={{0,4},{4,8},{8,12},{12,0},{1,5},{5,9},{9,13},{13,1},{2,6},{6,10},{... | collective-permute-start | bytes 393224 | tf_op jit(solution)/shard_map/ppermute | solution.py:343
  28.4 2.6 %collective-permute-start.7 = (bf16[64,1024]{1,0:T(8,128)(2,1)}, bf16[64,1024]{1,0:T(8,128)(2,1)S(1)}, u32[]{:S(2)}, u32[]{:S(2)}) collective-permute-start(bf16[64,1024]{1,0:T(8,128)(2,1)} %get-tuple-element.20), channel_id=1, source_target_pairs={{0,8},{4,12},{8,0},{12,4},{1,9},{5,13},{9,1},{13,5},{2,10},{6,14},... | collective-permute-start | bytes 393224 | tf_op jit(solution)/shard_map/ppermute | solution.py:343
  31.0 1.3 %collective-permute-start.8 = (bf16[64,1024]{1,0:T(8,128)(2,1)}, bf16[64,1024]{1,0:T(8,128)(2,1)S(1)}, u32[]{:S(2)}, u32[]{:S(2)}) collective-permute-start(bf16[64,1024]{1,0:T(8,128)(2,1)} %get-tuple-element.21), channel_id=1, source_target_pairs={{0,12},{4,0},{8,4},{12,8},{1,13},{5,1},{9,5},{13,9},{2,14},{6,2},{... | collective-permute-start | bytes 393224 | tf_op jit(solution)/shard_map/ppermute | solution.py:343
  32.3 10.9 %loss.2 = (f32[64,1024]{1,0:T(8,128)S(1)}, bf16[64,1024]{1,0:T(8,128)(2,1)}, bf16[64,1024]{1,0:T(8,128)(2,1)}, bf16[64,1024]{1,0:T(8,128)(2,1)S(1)}) custom-call(s32[6]{0:T(128)S(1)} %copy-done.6, s32[256]{0:T(256)S(1)} %reshape.32.pattern, bf16[2,16,128,128]{3,2,1,0:T(8,128)(2,1)S(1)} %copy-done.1, s32[2,2048]{1,0:T(2,128)S(1)} %collective-permute-done.refs_1_, ...), custom_call_target="tpu_custom_call" | custom-call | tf_op jit(solution)/shard_map/loss/pallas_call | solution.py:312
  43.2 0.7 %collective-permute-start.3 = (bf16[64,1024]{1,0:T(8,128)(2,1)}, bf16[64,1024]{1,0:T(8,128)(2,1)S(1)}, u32[]{:S(2)}, u32[]{:S(2)}) collective-permute-start(bf16[64,1024]{1,0:T(8,128)(2,1)} %get-tuple-element.15), channel_id=1, source_target_pairs={{0,4},{4,8},{8,12},{12,0},{1,5},{5,9},{9,13},{13,1},{2,6},{6,10},{... | collective-permute-start | bytes 393224 | tf_op jit(solution)/shard_map/ppermute | solution.py:343
  43.9 0.3 collective-permute-start.4
  44.3 0.0 collective-permute-done.6.refs_1_
  44.3 2.8 %collective-permute-start.5 = (bf16[64,1024]{1,0:T(8,128)(2,1)S(1)}, bf16[64,1024]{1,0:T(8,128)(2,1)S(1)}, u32[]{:S(2)}, u32[]{:S(2)}) collective-permute-start(bf16[64,1024]{1,0:T(8,128)(2,1)S(1)} %get-tuple-element.17), channel_id=1, source_target_pairs={{0,12},{4,0},{8,4},{12,8},{1,13},{5,1},{9,5},{13,9},{2,14},{6,2},{... | collective-permute-start | bytes 393224 | tf_op jit(solution)/shard_map/ppermute | solution.py:343
  47.1 0.0 copy-done.8
  47.1 0.1 reshape.30.pattern
  47.2 0.0 collective-permute-done.7.refs_2_
  47.2 0.0 collective-permute-done.8.refs_3_
  47.2 0.0 copy-done.2
  47.2 1.8 %net.2 = (f32[128,1024]{1,0:T(8,128)}, f32[2,1024]{1,0:T(2,128)S(1)}) custom-call(s32[64]{0:T(128)S(1)} %reshape.30.pattern, bf16[8,1024,128]{2,1,0:T(8,128)(2,1)S(1)} %bitcast.15, f32[64,1024]{1,0:T(8,128)S(1)} %get-tuple-element.18.refs_0_, bf16[64,1024]{1,0:T(8,128)(2,1)S(1)} %collective-permute-done.6.refs_1_, ...), custom_call_target="tpu_custom_call" | custom-call | tf_op jit(solution)/shard_map/net/pallas_call | solution.py:275
  49.0 2.7 %collective-permute-done.3.refs_1_ = bf16[64,1024]{1,0:T(8,128)(2,1)S(1)} collective-permute-done((bf16[64,1024]{1,0:T(8,128)(2,1)}, bf16[64,1024]{1,0:T(8,128)(2,1)S(1)}, u32[]{:S(2)}, u32[]{:S(2)}) %collective-permute-start.3) | collective-permute-done | bytes 131104 | tf_op jit(solution)/shard_map/ppermute | solution.py:343
  51.7 4.2 %collective-permute-done.4.refs_2_ = bf16[64,1024]{1,0:T(8,128)(2,1)S(1)} collective-permute-done((bf16[64,1024]{1,0:T(8,128)(2,1)}, bf16[64,1024]{1,0:T(8,128)(2,1)S(1)}, u32[]{:S(2)}, u32[]{:S(2)}) %collective-permute-start.4) | collective-permute-done | bytes 131104 | tf_op jit(solution)/shard_map/ppermute | solution.py:343
  55.9 0.0 collective-permute-done.5.refs_3_
  55.9 1.8 %net.3 = (f32[128,1024]{1,0:T(8,128)}, f32[2,1024]{1,0:T(2,128)S(1)}) custom-call(s32[64]{0:T(128)S(1)} %reshape.30.pattern, bf16[8,1024,128]{2,1,0:T(8,128)(2,1)S(1)} %bitcast.16, f32[64,1024]{1,0:T(8,128)S(1)} %get-tuple-element.14.refs_0_, bf16[64,1024]{1,0:T(8,128)(2,1)S(1)} %collective-permute-done.3.refs_1_, ...), custom_call_target="tpu_custom_call", output_to_operand_aliasing={{0}: (7, {})} | custom-call | tf_op jit(solution)/shard_map/net/pallas_call | solution.py:275
  57.8 1.6 %collective-permute-start.10 = (f32[2,1024]{1,0:T(2,128)S(1)}, f32[2,1024]{1,0:T(2,128)S(1)}, u32[]{:S(2)}, u32[]{:S(2)}) collective-permute-start(f32[2,1024]{1,0:T(2,128)S(1)} %get-tuple-element.25), channel_id=1, source_target_pairs={{0,2},{1,3},{2,0},{3,1},{4,6},{5,7},{6,4},{7,5},{8,10},{9,11},{10,... | collective-permute-start | bytes 24584 | tf_op jit(solution)/shard_map/ppermute | solution.py:347
  59.4 0.0 collective-permute-start.11
  59.4 0.7 %collective-permute-start.9 = (f32[2,1024]{1,0:T(2,128)S(1)}, f32[2,1024]{1,0:T(2,128)S(1)}, u32[]{:S(2)}, u32[]{:S(2)}) collective-permute-start(f32[2,1024]{1,0:T(2,128)S(1)} %get-tuple-element.25), channel_id=1, source_target_pairs={{0,1},{1,0},{2,3},{3,2},{4,5},{5,4},{6,7},{7,6},{8,9},{9,8},{10,11... | collective-permute-start | bytes 24584 | tf_op jit(solution)/shard_map/ppermute | solution.py:347
  60.0 1.5 %collective-permute-done.10 = f32[2,1024]{1,0:T(2,128)S(1)} collective-permute-done((f32[2,1024]{1,0:T(2,128)S(1)}, f32[2,1024]{1,0:T(2,128)S(1)}, u32[]{:S(2)}, u32[]{:S(2)}) %collective-permute-start.10) | collective-permute-done | bytes 8224 | tf_op jit(solution)/shard_map/ppermute | solution.py:347
  61.5 0.9 %collective-permute-done.11 = f32[2,1024]{1,0:T(2,128)S(1)} collective-permute-done((f32[2,1024]{1,0:T(2,128)S(1)}, f32[2,1024]{1,0:T(2,128)S(1)}, u32[]{:S(2)}, u32[]{:S(2)}) %collective-permute-start.11) | collective-permute-done | bytes 8224 | tf_op jit(solution)/shard_map/ppermute | solution.py:347
  62.4 0.0 collective-permute-done.9
  62.4 0.6 add_multiply_fusion
  (5 shorter events, 0.0 us)
Async XLA Ops:
  1.4 3.8 %copy-start.7 = (s32[2,2048]{1,0:T(2,128)}, s32[2,2048]{1,0:T(2,128)S(1)}, u32[]{:S(2)}) copy-start(s32[2,2048]{1,0:T(2,128)S(1)} %pad_add_fusion.part) | copy-start | bytes 49156
  1.4 7.9 %collective-permute-start = (s32[2,2048]{1,0:T(2,128)S(1)}, s32[2,2048]{1,0:T(2,128)S(1)}, u32[]{:S(2)}, u32[]{:S(2)}) collective-permute-start(s32[2,2048]{1,0:T(2,128)S(1)} %pad_add_fusion.part), channel_id=1, source_target_pairs={{0,1},{1,0},{2,3},{3,2},{4,5},{5,4},{6,7},{7,6},{8,9},{9,8},{10,11... | collective-permute-start | bytes 49160 | tf_op jit(solution)/shard_map/ppermute | solution.py:347
  1.9 7.4 %collective-permute-start.1 = (s32[2,2048]{1,0:T(2,128)S(1)}, s32[2,2048]{1,0:T(2,128)S(1)}, u32[]{:S(2)}, u32[]{:S(2)}) collective-permute-start(s32[2,2048]{1,0:T(2,128)S(1)} %pad_add_fusion.part), channel_id=1, source_target_pairs={{0,2},{1,3},{2,0},{3,1},{4,6},{5,7},{6,4},{7,5},{8,10},{9,11},{10,... | collective-permute-start | bytes 49160 | tf_op jit(solution)/shard_map/ppermute | solution.py:347
  4.5 4.8 %collective-permute-start.2 = (s32[2,2048]{1,0:T(2,128)S(1)}, s32[2,2048]{1,0:T(2,128)S(1)}, u32[]{:S(2)}, u32[]{:S(2)}) collective-permute-start(s32[2,2048]{1,0:T(2,128)S(1)} %pad_add_fusion.part), channel_id=1, source_target_pairs={{0,3},{1,2},{2,1},{3,0},{4,7},{5,6},{6,5},{7,4},{8,11},{9,10},{10,... | collective-permute-start | bytes 49160 | tf_op jit(solution)/shard_map/ppermute | solution.py:347
  9.3 2.2 %copy-start = (bf16[64,4,64,128]{3,2,1,0:T(8,128)(2,1)S(1)}, bf16[64,4,64,128]{3,2,1,0:T(8,128)(2,1)}, u32[]{:S(2)}) copy-start(bf16[64,4,64,128]{3,2,1,0:T(8,128)(2,1)} %param.11) | copy-start | bytes 12582916
  11.5 1.2 %copy-start.1 = (bf16[2,16,128,128]{3,2,1,0:T(8,128)(2,1)S(1)}, bf16[2,16,128,128]{3,2,1,0:T(8,128)(2,1)}, u32[]{:S(2)}) copy-start(bf16[2,16,128,128]{3,2,1,0:T(8,128)(2,1)} %panel.1.refs_0_) | copy-start | bytes 3145732
  12.7 0.8 %copy-start.3 = (f32[8192]{0:T(1024)S(1)}, f32[8192]{0:T(1024)}, u32[]{:S(2)}) copy-start(f32[8192]{0:T(1024)} %param.13) | copy-start | bytes 98308
  13.5 0.8 %copy-start.4 = (f32[8192]{0:T(1024)S(1)}, f32[8192]{0:T(1024)}, u32[]{:S(2)}) copy-start(f32[8192]{0:T(1024)} %param.14) | copy-start | bytes 98308
  14.2 0.8 %copy-start.5 = (s32[8192]{0:T(1024)S(1)}, s32[8192]{0:T(1024)}, u32[]{:S(2)}) copy-start(s32[8192]{0:T(1024)} %param.15) | copy-start | bytes 98308
  15.0 0.7 %copy-start.6 = (s32[6]{0:T(128)S(1)}, s32[6]{0:T(128)}, u32[]{:S(2)}) copy-start(s32[6]{0:T(128)} %stack.36.meta) | copy-start | bytes 76
  15.7 31.4 %copy-start.8 = (s32[8,8]{1,0:T(8,128)S(1)}, s32[8,8]{1,0:T(8,128)}, u32[]{:S(2)}) copy-start(s32[8,8]{1,0:T(8,128)} %param.17) | copy-start | bytes 772
  15.7 31.5 %copy-start.2 = (bf16[8,8,128,128]{3,2,1,0:T(8,128)(2,1)S(1)}, bf16[8,8,128,128]{3,2,1,0:T(8,128)(2,1)}, u32[]{:S(2)}) copy-start(bf16[8,8,128,128]{3,2,1,0:T(8,128)(2,1)} %param.16) | copy-start | bytes 6291460
  26.5 17.7 %collective-permute-start.6 = (bf16[64,1024]{1,0:T(8,128)(2,1)S(1)}, bf16[64,1024]{1,0:T(8,128)(2,1)S(1)}, u32[]{:S(2)}, u32[]{:S(2)}) collective-permute-start(bf16[64,1024]{1,0:T(8,128)(2,1)S(1)} %get-tuple-element.19), channel_id=1, source_target_pairs={{0,4},{4,8},{8,12},{12,0},{1,5},{5,9},{9,13},{13,1},{2,6},{6,10},{... | collective-permute-start | bytes 393224 | tf_op jit(solution)/shard_map/ppermute | solution.py:343
  28.4 18.8 %collective-permute-start.7 = (bf16[64,1024]{1,0:T(8,128)(2,1)}, bf16[64,1024]{1,0:T(8,128)(2,1)S(1)}, u32[]{:S(2)}, u32[]{:S(2)}) collective-permute-start(bf16[64,1024]{1,0:T(8,128)(2,1)} %get-tuple-element.20), channel_id=1, source_target_pairs={{0,8},{4,12},{8,0},{12,4},{1,9},{5,13},{9,1},{13,5},{2,10},{6,14},... | collective-permute-start | bytes 393224 | tf_op jit(solution)/shard_map/ppermute | solution.py:343
  31.0 16.2 %collective-permute-start.8 = (bf16[64,1024]{1,0:T(8,128)(2,1)}, bf16[64,1024]{1,0:T(8,128)(2,1)S(1)}, u32[]{:S(2)}, u32[]{:S(2)}) collective-permute-start(bf16[64,1024]{1,0:T(8,128)(2,1)} %get-tuple-element.21), channel_id=1, source_target_pairs={{0,12},{4,0},{8,4},{12,8},{1,13},{5,1},{9,5},{13,9},{2,14},{6,2},{... | collective-permute-start | bytes 393224 | tf_op jit(solution)/shard_map/ppermute | solution.py:343
  43.2 8.5 %collective-permute-start.3 = (bf16[64,1024]{1,0:T(8,128)(2,1)}, bf16[64,1024]{1,0:T(8,128)(2,1)S(1)}, u32[]{:S(2)}, u32[]{:S(2)}) collective-permute-start(bf16[64,1024]{1,0:T(8,128)(2,1)} %get-tuple-element.15), channel_id=1, source_target_pairs={{0,4},{4,8},{8,12},{12,0},{1,5},{5,9},{9,13},{13,1},{2,6},{6,10},{... | collective-permute-start | bytes 393224 | tf_op jit(solution)/shard_map/ppermute | solution.py:343
  43.9 12.0 %collective-permute-start.4 = (bf16[64,1024]{1,0:T(8,128)(2,1)}, bf16[64,1024]{1,0:T(8,128)(2,1)S(1)}, u32[]{:S(2)}, u32[]{:S(2)}) collective-permute-start(bf16[64,1024]{1,0:T(8,128)(2,1)} %get-tuple-element.16), channel_id=1, source_target_pairs={{0,8},{4,12},{8,0},{12,4},{1,9},{5,13},{9,1},{13,5},{2,10},{6,14},... | collective-permute-start | bytes 393224 | tf_op jit(solution)/shard_map/ppermute | solution.py:343
  44.3 11.7 %collective-permute-start.5 = (bf16[64,1024]{1,0:T(8,128)(2,1)S(1)}, bf16[64,1024]{1,0:T(8,128)(2,1)S(1)}, u32[]{:S(2)}, u32[]{:S(2)}) collective-permute-start(bf16[64,1024]{1,0:T(8,128)(2,1)S(1)} %get-tuple-element.17), channel_id=1, source_target_pairs={{0,12},{4,0},{8,4},{12,8},{1,13},{5,1},{9,5},{13,9},{2,14},{6,2},{... | collective-permute-start | bytes 393224 | tf_op jit(solution)/shard_map/ppermute | solution.py:343
  57.8 3.7 %collective-permute-start.10 = (f32[2,1024]{1,0:T(2,128)S(1)}, f32[2,1024]{1,0:T(2,128)S(1)}, u32[]{:S(2)}, u32[]{:S(2)}) collective-permute-start(f32[2,1024]{1,0:T(2,128)S(1)} %get-tuple-element.25), channel_id=1, source_target_pairs={{0,2},{1,3},{2,0},{3,1},{4,6},{5,7},{6,4},{7,5},{8,10},{9,11},{10,... | collective-permute-start | bytes 24584 | tf_op jit(solution)/shard_map/ppermute | solution.py:347
  59.4 3.1 %collective-permute-start.11 = (f32[2,1024]{1,0:T(2,128)S(1)}, f32[2,1024]{1,0:T(2,128)S(1)}, u32[]{:S(2)}, u32[]{:S(2)}) collective-permute-start(f32[2,1024]{1,0:T(2,128)S(1)} %get-tuple-element.25), channel_id=1, source_target_pairs={{0,3},{1,2},{2,1},{3,0},{4,7},{5,6},{6,5},{7,4},{8,11},{9,10},{10,... | collective-permute-start | bytes 24584 | tf_op jit(solution)/shard_map/ppermute | solution.py:347
  59.4 3.1 %collective-permute-start.9 = (f32[2,1024]{1,0:T(2,128)S(1)}, f32[2,1024]{1,0:T(2,128)S(1)}, u32[]{:S(2)}, u32[]{:S(2)}) collective-permute-start(f32[2,1024]{1,0:T(2,128)S(1)} %get-tuple-element.25), channel_id=1, source_target_pairs={{0,1},{1,0},{2,3},{3,2},{4,5},{5,4},{6,7},{7,6},{8,9},{9,8},{10,11... | collective-permute-start | bytes 24584 | tf_op jit(solution)/shard_map/ppermute | solution.py:347

commit v5 on v4

--- a/solution.py
+++ b/solution.py
@@ -13,8 +13,8 @@
 DEST_CHUNK = 4
 MXU = 256
 CHUNKS = (64, 64)
-VMEM_LIMIT = 48 << 20
-NET_VMEM = 24 << 20
+VMEM_LIMIT = 63 << 20
+NET_VMEM = 63 << 20
 
 QUANTILE_MID = 2.6095163822174072
 QUANTILE = (
@@ -91,11 +91,13 @@
     lax.fori_loop(0, part.shape[1] // LANES, fill, 0, unroll=max(1, 1024 // points))
 
 
-def panel_kernel(meta, part, panel):
-    fill_panel(panel, 0, part, meta[0])
-
-
-def loss_kernel(n_parts, n_dest, split, direct, first_point, meta, pattern, *refs):
+def panel_kernel(part, panel):
+    fill_panel(panel, 0, part, lax.axis_index("narrow") * panel.shape[2])
+
+
+def loss_kernel(n_parts, n_dest, split, direct, first_point, pattern, *refs):
+    me = lax.axis_index("narrow")
+    base = lax.axis_index("wide") if direct else 0
     own_panel = refs[0]
     parts = refs[1:n_parts]
     sources = refs[n_parts : n_parts + 4]
@@ -105,6 +107,7 @@
     points = panel.shape[2]
     blocks = load_ref.shape[0]
     columns = own_panel.shape[1]
+    all_points = own_panel.shape[2]
     seg_dev = (outs[0] if direct else outs[0].at[0]).shape[1]
     sub = seg_dev // (2 * MXU)
     group = split * sub
@@ -114,16 +117,18 @@
         pltpu.make_async_copy(source, target, sems.at[i])
         for i, (source, target) in enumerate(zip(sources, (load_ref, thr_ref, expo_ref, seg_ref)))
     ]
+    copies.append(
+        pltpu.make_async_copy(
+            own_panel.at[:, :, pl.ds(first_point, points), :],
+            panel.at[:, pl.ds(me * columns, columns)],
+            sems.at[4],
+        )
+    )
     for copy in copies:
         copy.start()
 
-    def reuse(c, carry):
-        panel[:, meta[2] * columns + c] = own_panel[:, c, first_point : first_point + points, :]
-        return carry
-
-    lax.fori_loop(0, columns, reuse, 0, unroll=4)
     for k in range(1, n_parts):
-        fill_panel(panel, meta[2 + k] * columns, parts[k - 1], meta[0] + first_point)
+        fill_panel(panel, (me ^ k) * columns, parts[k - 1], me * all_points + first_point)
 
     for copy in copies:
         copy.wait()
@@ -181,7 +186,7 @@
                 here = slice(j * LANES, (j + 1) * LANES)
                 t = thr_ref[one, :] - latent[j * points : (j + 1) * points, here]
                 prob = weighted_prob(t, expo_ref[one, :]).astype(jnp.bfloat16)
-                part = lax.shift_right_logical(seg_ref[one, :], (2 * MXU).bit_length() - 1) - meta[1] * sub
+                part = lax.shift_right_logical(seg_ref[one, :], (2 * MXU).bit_length() - 1) - base * sub
                 part = jnp.where(part < 0, part + n_dest * sub, part) - chunk * group
                 part = jnp.broadcast_to(part, (ROWS, LANES)).astype(jnp.int16)
                 for d in range(group):
@@ -235,11 +240,14 @@
     )
 
 
-def net_kernel(first_point, n_received, pattern, tiles_ref, *refs):
+def net_kernel(first_point, n_received, pattern, tiles_hbm, *refs):
     received = refs[:n_received]
-    out_ref, sums_ref, losses, net_rows, sem = refs[-5:]
-    before = refs[n_received : -5]
+    out_ref, sums_ref, losses, net_rows, tiles_ref, sem, sems = refs[-7:]
+    before = refs[n_received : -7]
     blocks = tiles_ref.shape[0]
+    copies = [pltpu.make_async_copy(tiles_hbm.at[b], tiles_ref.at[b], sems.at[b]) for b in range(blocks)]
+    for copy in copies:
+        copy.start()
     points = losses.shape[1]
     slots = tiles_ref.shape[1] // LANES
     for q in range(blocks):
@@ -254,6 +262,7 @@
     for b in range(blocks):
         at = slice(b * LANES, (b + 1) * LANES)
         picked = jnp.concatenate([losses[pattern[slots * b + k]] for k in range(slots)], axis=1)
+        copies[b].wait()
         net = jnp.dot(picked, tiles_ref[b], preferred_element_type=jnp.float32)
         net_rows[:, at] = net
         first = jnp.sum(net, axis=0, keepdims=True)
@@ -279,13 +288,16 @@
             jax.ShapeDtypeStruct((2, seg_dev), jnp.float32),
         ],
         in_specs=[pl.BlockSpec(memory_space=pltpu.SMEM)]
-        + [vmem] * (1 + len(received))
+        + [hbm]
+        + [vmem] * len(received)
         + [vmem, hbm][: len(extra)],
         out_specs=[hbm, vmem],
         scratch_shapes=[
             pltpu.VMEM((seg_dev // LANES, chunk, LANES), jnp.bfloat16),
             pltpu.VMEM((chunk, seg_dev), jnp.float32),
+            pltpu.VMEM(tiles.shape, jnp.bfloat16),
             pltpu.SemaphoreType.DMA,
+            pltpu.SemaphoreType.DMA((tiles.shape[0],)),
         ],
         input_output_aliases={} if before is None else {3 + len(received): 0},
         compiler_params=pltpu.CompilerParams(vmem_limit_bytes=NET_VMEM),
@@ -293,7 +305,7 @@
     )(net_pattern, tiles, *received, *extra)
 
 
-def loss_call(meta, pattern, own_panel, parts, loadings, threshold, exposure, segment_map, n_dest, first_point, points, seg_dev, direct):
+def loss_call(pattern, own_panel, parts, loadings, threshold, exposure, segment_map, n_dest, first_point, points, seg_dev, direct):
     blocks = loadings.shape[0]
     n_parts = len(parts) + 1
     columns = own_panel.shape[1] * n_parts
@@ -312,7 +324,7 @@
     return pl.pallas_call(
         functools.partial(loss_kernel, n_parts, n_dest, split, direct, first_point),
         out_shape=out_shape,
-        in_specs=[smem, smem] + [vmem] * n_parts + [hbm] * 4,
+        in_specs=[smem, hbm] + [vmem] * (n_parts - 1) + [hbm] * 4,
         out_specs=[vmem] * len(out_shape),
         scratch_shapes=[
             pltpu.VMEM((2, columns, points, LANES), jnp.bfloat16),
@@ -322,12 +334,11 @@
             pltpu.VMEM((blocks, LANES), jnp.int32),
             slot,
             slot,
-            pltpu.SemaphoreType.DMA((4,)),
+            pltpu.SemaphoreType.DMA((5,)),
         ],
         compiler_params=pltpu.CompilerParams(vmem_limit_bytes=VMEM_LIMIT),
         name="loss",
     )(
-        meta,
         pattern,
         own_panel,
         *parts,
@@ -366,7 +377,6 @@
 ):
     n_narrow = lax.axis_size("narrow")
     n_dest = lax.axis_size("wide")
-    me = lax.axis_index("narrow")
     points = P_SIZE // n_narrow
     seg_blocks = net_tiles.shape[0]
     seg_dev = seg_blocks * LANES
@@ -374,18 +384,14 @@
 
     own = jnp.stack([generator, lattice_shift])
     parts = [swapped(own, "narrow", k) for k in range(1, n_narrow)]
-    quarter = [me ^ k for k in range(n_narrow)]
-    base = lax.axis_index("wide") if direct else 0
-    meta = jnp.stack([me * points, jnp.int32(base)] + quarter).astype(jnp.int32)
-
     vmem = pl.BlockSpec(memory_space=pltpu.VMEM)
     own_panel = pl.pallas_call(
         panel_kernel,
         out_shape=jax.ShapeDtypeStruct((2, own.shape[1] // LANES, points, LANES), jnp.bfloat16),
-        in_specs=[pl.BlockSpec(memory_space=pltpu.SMEM), vmem],
+        in_specs=[vmem],
         out_specs=vmem,
         name="panel",
-    )(meta, own)
+    )(own)
     pattern = load_pattern.reshape(-1)
     slots = net_tiles.shape[1]
     tiles = net_tiles.reshape(seg_blocks, slots * LANES, LANES)
@@ -394,7 +400,6 @@
     for chunk in CHUNKS:
         chunk = chunk * points // sum(CHUNKS)
         partial = loss_call(
-            meta,
             pattern,
             own_panel,
             parts,

time: 63.6 us -> 62.4 us (0.981)
  Pallas kernels: 28.6 us -> 34.7 us
  waiting for transfers between devices: 9.35 us -> 5.12 us
  local copies, waits for them, and re-layouts: 7.98 us -> 4.06 us
  other arithmetic: 1.34 us -> 2.04 us
    pallas_call x2, Pallas kernels: 3.68 us -> 9.93 us  [net_call(): pl.pallas_call(functools.partial(net_kernel, first_point, len(received)),...]
    ppermute x6, waiting for transfers between devices: 6.92 us -> 2.47 us  [shifted(): return lax.ppermute(x, axis, [(i, (i + k) % n) for i in range(n)])]
    unnamed x19 -> x23, local copies, waits for them, and re-layouts: 7.13 us -> 2.73 us
    div x1, other arithmetic: 0.61 us -> 1.31 us  [body(): return (net_loss, total / P_SIZE)]
    another operation x1 -> x0, local copies, waits for them, and re-layouts: 0.67 us -> none  [body(): meta = jnp.stack([me * points, jnp.int32(base)] + quarter).astype(jnp.int32)]
  transfers between devices with their start and end apart: 12 -> 12, of which waited for: 4 -> 3; matrix products, arithmetic and copies ran while one was open for 3% -> 3% of each run, Pallas kernels for 25% -> 31%
where the time goes in v5:
time: 62.4 us; the launch traced here: 61.8 us
  Pallas kernels  34.7 us (56%)
  starting transfers between devices  15.1 us (24%)
  waiting for transfers between devices  5.12 us (8%)
  local copies, waits for them, and re-layouts  4.06 us (7%)
  other arithmetic  2.04 us (3%)
  between operations  0.76 us (1%)
    pallas_call x2, Pallas kernels, loss_call(): pl.pallas_call(functools.partial(loss_kernel, n_parts, n_dest, split, dir...  21.6 us
    pallas_call x2, Pallas kernels, net_call(): pl.pallas_call(functools.partial(net_kernel, first_point, len(received)),...  9.93 us
    ppermute x6, starting transfers between devices, shifted(): return lax.ppermute(x, axis, [(i, (i + k) % n) for i in range(n)])  9.74 us
    ppermute x6, starting transfers between devices, swapped(): lax.ppermute(x, axis, [(i, i ^ k) for i in range(lax.axis_size(axis))])  5.36 us
    pallas_call x1, Pallas kernels, body(): pl.pallas_call(panel_kernel, out_shape=jax.ShapeDtypeStruct((2, own.shape...  3.22 us
    unnamed x23, local copies, waits for them, and re-layouts  2.73 us
    ppermute x6, waiting for transfers between devices, swapped(): lax.ppermute(x, axis, [(i, i ^ k) for i in range(lax.axis_size(axis))])  2.65 us
    ppermute x6, waiting for transfers between devices, shifted(): return lax.ppermute(x, axis, [(i, (i + k) % n) for i in range(n)])  2.47 us
  transfers between devices with their start and end apart: 12, of which 3 were waited for; matrix products, arithmetic and copies ran while one was open for 3% of the time, Pallas kernels for 31%

profile of v5, /device:TPU:0, one launch (start us, length us, event | category | flops | bytes accessed | tf_op | source)
XLA Modules:
  0.0 61.8 jit_solution(4161664203182067898)
XLA Ops:
  0.6 0.7 %pad_add_fusion.part = s32[2,2048]{1,0:T(2,128)S(1)} fusion(s32[1,2048]{1,0:T(1,128)} %bitcast.17, s32[1,2048]{1,0:T(1,128)} %bitcast.18), kind=kLoop, calls=%fused_computation | loop fusion | flops 4096 | bytes 32768 | tf_op jit(solution)/shard_map/stack | solution.py:385
  1.4 0.0 copy-start.9
  1.4 0.5 collective-permute-start
  1.9 2.6 %collective-permute-start.1 = (s32[2,2048]{1,0:T(2,128)S(1)}, s32[2,2048]{1,0:T(2,128)S(1)}, u32[]{:S(2)}, u32[]{:S(2)}) collective-permute-start(s32[2,2048]{1,0:T(2,128)S(1)} %pad_add_fusion.part), channel_id=1, source_target_pairs={{0,2},{1,3},{2,0},{3,1},{4,6},{5,7},{6,4},{7,5},{8,10},{9,11},{10,... | collective-permute-start | bytes 49160 | tf_op jit(solution)/shard_map/ppermute | solution.py:358
  4.5 0.1 collective-permute-start.2
  4.5 0.0 copy-done.9
  4.5 3.2 %panel.1.refs_0_ = bf16[2,16,128,128]{3,2,1,0:T(8,128)(2,1)} custom-call(s32[2,2048]{1,0:T(2,128)} %copy-done.9), custom_call_target="tpu_custom_call" | custom-call | tf_op jit(solution)/shard_map/panel/pallas_call | solution.py:388
  7.8 0.8 %copy.12 = s32[64,4]{1,0:T(8,128)S(1)} copy(s32[64,4]{0,1:T(4,128)} %param.12) | data formatting | bytes 2048 | tf_op args[3]
  8.5 0.7 %reshape.32.pattern = s32[256]{0:T(256)} reshape(s32[64,4]{1,0:T(8,128)S(1)} %copy.12) | data formatting | bytes 2048 | tf_op jit(solution)/shard_map/reshape | solution.py:395
  9.2 0.0 collective-permute-done.refs_1_
  9.2 0.0 collective-permute-done.1.refs_2_
  9.2 0.0 copy-start.7
  9.2 0.0 collective-permute-done.2.refs_3_
  9.2 0.0 copy-start.8
  9.2 0.6 copy-done.6
  9.8 0.0 copy-done.7
  9.8 0.0 copy-done.8
  9.8 10.8 %loss.3 = (f32[64,1024]{1,0:T(8,128)}, bf16[64,1024]{1,0:T(8,128)(2,1)}, bf16[64,1024]{1,0:T(8,128)(2,1)}, bf16[64,1024]{1,0:T(8,128)(2,1)}) custom-call(s32[256]{0:T(256)} %reshape.32.pattern, bf16[2,16,128,128]{3,2,1,0:T(8,128)(2,1)} %panel.1.refs_0_, s32[2,2048]{1,0:T(2,128)} %copy-done.6, s32[2,2048]{1,0:T(2,128)} %copy-done.7, s32[2,2048]{1,0:T(2,128)} %copy-done.8, ...), custom_call_target="tpu_custom_call" | custom-call | tf_op jit(solution)/shard_map/loss/pallas_call | solution.py:324
  20.6 1.9 %collective-permute-start.6 = (bf16[64,1024]{1,0:T(8,128)(2,1)}, bf16[64,1024]{1,0:T(8,128)(2,1)S(1)}, u32[]{:S(2)}, u32[]{:S(2)}) collective-permute-start(bf16[64,1024]{1,0:T(8,128)(2,1)} %get-tuple-element.19), channel_id=1, source_target_pairs={{0,4},{4,8},{8,12},{12,0},{1,5},{5,9},{9,13},{13,1},{2,6},{6,10},{... | collective-permute-start | bytes 393224 | tf_op jit(solution)/shard_map/ppermute | solution.py:354
  22.5 2.6 %collective-permute-start.7 = (bf16[64,1024]{1,0:T(8,128)(2,1)}, bf16[64,1024]{1,0:T(8,128)(2,1)S(1)}, u32[]{:S(2)}, u32[]{:S(2)}) collective-permute-start(bf16[64,1024]{1,0:T(8,128)(2,1)} %get-tuple-element.20), channel_id=1, source_target_pairs={{0,8},{4,12},{8,0},{12,4},{1,9},{5,13},{9,1},{13,5},{2,10},{6,14},... | collective-permute-start | bytes 393224 | tf_op jit(solution)/shard_map/ppermute | solution.py:354
  25.1 1.3 %collective-permute-start.8 = (bf16[64,1024]{1,0:T(8,128)(2,1)}, bf16[64,1024]{1,0:T(8,128)(2,1)S(1)}, u32[]{:S(2)}, u32[]{:S(2)}) collective-permute-start(bf16[64,1024]{1,0:T(8,128)(2,1)} %get-tuple-element.21), channel_id=1, source_target_pairs={{0,12},{4,0},{8,4},{12,8},{1,13},{5,1},{9,5},{13,9},{2,14},{6,2},{... | collective-permute-start | bytes 393224 | tf_op jit(solution)/shard_map/ppermute | solution.py:354
  26.4 10.8 %loss.2 = (f32[64,1024]{1,0:T(8,128)}, bf16[64,1024]{1,0:T(8,128)(2,1)}, bf16[64,1024]{1,0:T(8,128)(2,1)}, bf16[64,1024]{1,0:T(8,128)(2,1)}) custom-call(s32[256]{0:T(256)} %reshape.32.pattern, bf16[2,16,128,128]{3,2,1,0:T(8,128)(2,1)} %panel.1.refs_0_, s32[2,2048]{1,0:T(2,128)} %copy-done.6, s32[2,2048]{1,0:T(2,128)} %copy-done.7, s32[2,2048]{1,0:T(2,128)} %copy-done.8, ...), custom_call_target="tpu_custom_call" | custom-call | tf_op jit(solution)/shard_map/loss/pallas_call | solution.py:324
  37.2 0.7 %collective-permute-start.3 = (bf16[64,1024]{1,0:T(8,128)(2,1)}, bf16[64,1024]{1,0:T(8,128)(2,1)S(1)}, u32[]{:S(2)}, u32[]{:S(2)}) collective-permute-start(bf16[64,1024]{1,0:T(8,128)(2,1)} %get-tuple-element.15), channel_id=1, source_target_pairs={{0,4},{4,8},{8,12},{12,0},{1,5},{5,9},{9,13},{13,1},{2,6},{6,10},{... | collective-permute-start | bytes 393224 | tf_op jit(solution)/shard_map/ppermute | solution.py:354
  38.0 0.3 collective-permute-start.4
  38.3 0.0 collective-permute-done.6.refs_1_
  38.3 2.9 %collective-permute-start.5 = (bf16[64,1024]{1,0:T(8,128)(2,1)}, bf16[64,1024]{1,0:T(8,128)(2,1)S(1)}, u32[]{:S(2)}, u32[]{:S(2)}) collective-permute-start(bf16[64,1024]{1,0:T(8,128)(2,1)} %get-tuple-element.17), channel_id=1, source_target_pairs={{0,12},{4,0},{8,4},{12,8},{1,13},{5,1},{9,5},{13,9},{2,14},{6,2},{... | collective-permute-start | bytes 393224 | tf_op jit(solution)/shard_map/ppermute | solution.py:354
  41.2 0.0 copy-done.10
  41.2 0.7 %reshape.30.pattern = s32[64]{0:T(128)} reshape(s32[8,8]{1,0:T(8,128)S(1)} %copy-done.10) | data formatting | bytes 512 | tf_op jit(solution)/shard_map/reshape | solution.py:424
  41.8 0.0 collective-permute-done.7.refs_2_
  41.8 0.0 collective-permute-done.8.refs_3_
  41.8 0.0 copy-start.4
  41.8 0.0 copy-done
  41.9 0.6 %copy-done.2 = bf16[64,1024]{1,0:T(8,128)(2,1)} copy-done((bf16[64,1024]{1,0:T(8,128)(2,1)}, bf16[64,1024]{1,0:T(8,128)(2,1)S(1)}, u32[]{:S(2)}) %copy-start.2) | copy-done | bytes 131096
  42.5 0.0 copy-done.4
  42.5 5.0 %net.2 = (f32[128,1024]{1,0:T(8,128)}, f32[2,1024]{1,0:T(2,128)}) custom-call(s32[64]{0:T(128)} %reshape.30.pattern, bf16[8,1024,128]{2,1,0:T(8,128)(2,1)} %bitcast.9, f32[64,1024]{1,0:T(8,128)} %get-tuple-element.18.refs_0_, bf16[64,1024]{1,0:T(8,128)(2,1)} %copy-done, bf16[64,1024]{1,0:T(8,128)(2,1)} %copy-done.2, bf16[64,1024]{1,0:T(8,128)(2,1)} %copy-done.4), custom_call_target="tpu_custom_call" | custom-call | tf_op jit(solution)/shard_map/net/pallas_call | solution.py:284
  47.5 0.0 collective-permute-done.3.refs_1_
  47.5 2.5 %collective-permute-done.4.refs_2_ = bf16[64,1024]{1,0:T(8,128)(2,1)S(1)} collective-permute-done((bf16[64,1024]{1,0:T(8,128)(2,1)}, bf16[64,1024]{1,0:T(8,128)(2,1)S(1)}, u32[]{:S(2)}, u32[]{:S(2)}) %collective-permute-start.4) | collective-permute-done | bytes 131104 | tf_op jit(solution)/shard_map/ppermute | solution.py:354
  50.0 0.0 collective-permute-done.5.refs_3_
  50.0 0.6 %copy-done.3 = bf16[64,1024]{1,0:T(8,128)(2,1)} copy-done((bf16[64,1024]{1,0:T(8,128)(2,1)}, bf16[64,1024]{1,0:T(8,128)(2,1)S(1)}, u32[]{:S(2)}) %copy-start.3) | copy-done | bytes 131096
  50.6 0.0 copy-done.5
  50.7 5.0 %net.3 = (f32[128,1024]{1,0:T(8,128)}, f32[2,1024]{1,0:T(2,128)}) custom-call(s32[64]{0:T(128)} %reshape.30.pattern, bf16[8,1024,128]{2,1,0:T(8,128)(2,1)} %bitcast.10, f32[64,1024]{1,0:T(8,128)} %get-tuple-element.14.refs_0_, bf16[64,1024]{1,0:T(8,128)(2,1)} %copy-done.1, bf16[64,1024]{1,0:T(8,128)(2,1)} %copy-done.3, ...), custom_call_target="tpu_custom_call", output_to_operand_aliasing={{0}: (7, {})} | custom-call | tf_op jit(solution)/shard_map/net/pallas_call | solution.py:284
  55.6 1.6 %collective-permute-start.10 = (f32[2,1024]{1,0:T(2,128)}, f32[2,1024]{1,0:T(2,128)S(1)}, u32[]{:S(2)}, u32[]{:S(2)}) collective-permute-start(f32[2,1024]{1,0:T(2,128)} %get-tuple-element.25), channel_id=1, source_target_pairs={{0,2},{1,3},{2,0},{3,1},{4,6},{5,7},{6,4},{7,5},{8,10},{9,11},{10,... | collective-permute-start | bytes 24584 | tf_op jit(solution)/shard_map/ppermute | solution.py:358
  57.2 0.0 collective-permute-start.11
  57.2 0.6 %collective-permute-start.9 = (f32[2,1024]{1,0:T(2,128)}, f32[2,1024]{1,0:T(2,128)S(1)}, u32[]{:S(2)}, u32[]{:S(2)}) collective-permute-start(f32[2,1024]{1,0:T(2,128)} %get-tuple-element.25), channel_id=1, source_target_pairs={{0,1},{1,0},{2,3},{3,2},{4,5},{5,4},{6,7},{7,6},{8,9},{9,8},{10,11... | collective-permute-start | bytes 24584 | tf_op jit(solution)/shard_map/ppermute | solution.py:358
  57.8 1.7 %collective-permute-done.10 = f32[2,1024]{1,0:T(2,128)S(1)} collective-permute-done((f32[2,1024]{1,0:T(2,128)}, f32[2,1024]{1,0:T(2,128)S(1)}, u32[]{:S(2)}, u32[]{:S(2)}) %collective-permute-start.10) | collective-permute-done | bytes 8224 | tf_op jit(solution)/shard_map/ppermute | solution.py:358
  59.6 0.9 %collective-permute-done.11 = f32[2,1024]{1,0:T(2,128)S(1)} collective-permute-done((f32[2,1024]{1,0:T(2,128)}, f32[2,1024]{1,0:T(2,128)S(1)}, u32[]{:S(2)}, u32[]{:S(2)}) %collective-permute-start.11) | collective-permute-done | bytes 8224 | tf_op jit(solution)/shard_map/ppermute | solution.py:358
  60.5 0.0 collective-permute-done.9
  60.5 1.3 %add_multiply_fusion = f32[2,1024]{1,0:T(2,128)} fusion(f32[2,1024]{1,0:T(2,128)S(1)} %collective-permute-done.10, f32[2,1024]{1,0:T(2,128)S(1)} %collective-permute-done.11, f32[2,1024]{1,0:T(2,128)} %get-tuple-element.25, f32[2,1024]{1,0:T(2,128)S(1)} %collective-permute-done.9), kind=kLoop, calls=%fused_computation.1 | loop fusion | flops 8192 | bytes 40960 | tf_op jit(solution)/shard_map/div | solution.py:428
  (8 shorter events, 0.0 us)
Async XLA Ops:
  1.4 3.2 %copy-start.9 = (s32[2,2048]{1,0:T(2,128)}, s32[2,2048]{1,0:T(2,128)S(1)}, u32[]{:S(2)}) copy-start(s32[2,2048]{1,0:T(2,128)S(1)} %pad_add_fusion.part) | copy-start | bytes 49156
  1.4 7.8 %collective-permute-start = (s32[2,2048]{1,0:T(2,128)S(1)}, s32[2,2048]{1,0:T(2,128)S(1)}, u32[]{:S(2)}, u32[]{:S(2)}) collective-permute-start(s32[2,2048]{1,0:T(2,128)S(1)} %pad_add_fusion.part), channel_id=1, source_target_pairs={{0,1},{1,0},{2,3},{3,2},{4,5},{5,4},{6,7},{7,6},{8,9},{9,8},{10,11... | collective-permute-start | bytes 49160 | tf_op jit(solution)/shard_map/ppermute | solution.py:358
  1.9 7.3 %collective-permute-start.1 = (s32[2,2048]{1,0:T(2,128)S(1)}, s32[2,2048]{1,0:T(2,128)S(1)}, u32[]{:S(2)}, u32[]{:S(2)}) collective-permute-start(s32[2,2048]{1,0:T(2,128)S(1)} %pad_add_fusion.part), channel_id=1, source_target_pairs={{0,2},{1,3},{2,0},{3,1},{4,6},{5,7},{6,4},{7,5},{8,10},{9,11},{10,... | collective-permute-start | bytes 49160 | tf_op jit(solution)/shard_map/ppermute | solution.py:358
  4.5 4.8 %collective-permute-start.2 = (s32[2,2048]{1,0:T(2,128)S(1)}, s32[2,2048]{1,0:T(2,128)S(1)}, u32[]{:S(2)}, u32[]{:S(2)}) collective-permute-start(s32[2,2048]{1,0:T(2,128)S(1)} %pad_add_fusion.part), channel_id=1, source_target_pairs={{0,3},{1,2},{2,1},{3,0},{4,7},{5,6},{6,5},{7,4},{8,11},{9,10},{10,... | collective-permute-start | bytes 49160 | tf_op jit(solution)/shard_map/ppermute | solution.py:358
  9.2 0.6 copy-start.6
  9.2 0.6 copy-start.7
  9.2 0.6 copy-start.8
  9.8 31.3 %copy-start.10 = (s32[8,8]{1,0:T(8,128)S(1)}, s32[8,8]{1,0:T(8,128)}, u32[]{:S(2)}) copy-start(s32[8,8]{1,0:T(8,128)} %param.17) | copy-start | bytes 772
  20.6 17.7 %collective-permute-start.6 = (bf16[64,1024]{1,0:T(8,128)(2,1)}, bf16[64,1024]{1,0:T(8,128)(2,1)S(1)}, u32[]{:S(2)}, u32[]{:S(2)}) collective-permute-start(bf16[64,1024]{1,0:T(8,128)(2,1)} %get-tuple-element.19), channel_id=1, source_target_pairs={{0,4},{4,8},{8,12},{12,0},{1,5},{5,9},{9,13},{13,1},{2,6},{6,10},{... | collective-permute-start | bytes 393224 | tf_op jit(solution)/shard_map/ppermute | solution.py:354
  22.5 19.3 %collective-permute-start.7 = (bf16[64,1024]{1,0:T(8,128)(2,1)}, bf16[64,1024]{1,0:T(8,128)(2,1)S(1)}, u32[]{:S(2)}, u32[]{:S(2)}) collective-permute-start(bf16[64,1024]{1,0:T(8,128)(2,1)} %get-tuple-element.20), channel_id=1, source_target_pairs={{0,8},{4,12},{8,0},{12,4},{1,9},{5,13},{9,1},{13,5},{2,10},{6,14},... | collective-permute-start | bytes 393224 | tf_op jit(solution)/shard_map/ppermute | solution.py:354
  25.1 16.8 %collective-permute-start.8 = (bf16[64,1024]{1,0:T(8,128)(2,1)}, bf16[64,1024]{1,0:T(8,128)(2,1)S(1)}, u32[]{:S(2)}, u32[]{:S(2)}) collective-permute-start(bf16[64,1024]{1,0:T(8,128)(2,1)} %get-tuple-element.21), channel_id=1, source_target_pairs={{0,12},{4,0},{8,4},{12,8},{1,13},{5,1},{9,5},{13,9},{2,14},{6,2},{... | collective-permute-start | bytes 393224 | tf_op jit(solution)/shard_map/ppermute | solution.py:354
  37.2 10.3 %collective-permute-start.3 = (bf16[64,1024]{1,0:T(8,128)(2,1)}, bf16[64,1024]{1,0:T(8,128)(2,1)S(1)}, u32[]{:S(2)}, u32[]{:S(2)}) collective-permute-start(bf16[64,1024]{1,0:T(8,128)(2,1)} %get-tuple-element.15), channel_id=1, source_target_pairs={{0,4},{4,8},{8,12},{12,0},{1,5},{5,9},{9,13},{13,1},{2,6},{6,10},{... | collective-permute-start | bytes 393224 | tf_op jit(solution)/shard_map/ppermute | solution.py:354
  38.0 12.0 %collective-permute-start.4 = (bf16[64,1024]{1,0:T(8,128)(2,1)}, bf16[64,1024]{1,0:T(8,128)(2,1)S(1)}, u32[]{:S(2)}, u32[]{:S(2)}) collective-permute-start(bf16[64,1024]{1,0:T(8,128)(2,1)} %get-tuple-element.16), channel_id=1, source_target_pairs={{0,8},{4,12},{8,0},{12,4},{1,9},{5,13},{9,1},{13,5},{2,10},{6,14},... | collective-permute-start | bytes 393224 | tf_op jit(solution)/shard_map/ppermute | solution.py:354
  38.3 3.6 %copy-start = (bf16[64,1024]{1,0:T(8,128)(2,1)}, bf16[64,1024]{1,0:T(8,128)(2,1)S(1)}, u32[]{:S(2)}) copy-start(bf16[64,1024]{1,0:T(8,128)(2,1)S(1)} %collective-permute-done.6.refs_1_) | copy-start | bytes 393220
  38.3 11.7 %collective-permute-start.5 = (bf16[64,1024]{1,0:T(8,128)(2,1)}, bf16[64,1024]{1,0:T(8,128)(2,1)S(1)}, u32[]{:S(2)}, u32[]{:S(2)}) collective-permute-start(bf16[64,1024]{1,0:T(8,128)(2,1)} %get-tuple-element.17), channel_id=1, source_target_pairs={{0,12},{4,0},{8,4},{12,8},{1,13},{5,1},{9,5},{13,9},{2,14},{6,2},{... | collective-permute-start | bytes 393224 | tf_op jit(solution)/shard_map/ppermute | solution.py:354
  41.8 0.6 %copy-start.2 = (bf16[64,1024]{1,0:T(8,128)(2,1)}, bf16[64,1024]{1,0:T(8,128)(2,1)S(1)}, u32[]{:S(2)}) copy-start(bf16[64,1024]{1,0:T(8,128)(2,1)S(1)} %collective-permute-done.7.refs_2_) | copy-start | bytes 393220
  41.8 0.7 %copy-start.4 = (bf16[64,1024]{1,0:T(8,128)(2,1)}, bf16[64,1024]{1,0:T(8,128)(2,1)S(1)}, u32[]{:S(2)}) copy-start(bf16[64,1024]{1,0:T(8,128)(2,1)S(1)} %collective-permute-done.8.refs_3_) | copy-start | bytes 393220
  47.5 2.5 %copy-start.1 = (bf16[64,1024]{1,0:T(8,128)(2,1)}, bf16[64,1024]{1,0:T(8,128)(2,1)S(1)}, u32[]{:S(2)}) copy-start(bf16[64,1024]{1,0:T(8,128)(2,1)S(1)} %collective-permute-done.3.refs_1_) | copy-start | bytes 393220
  50.0 0.7 %copy-start.3 = (bf16[64,1024]{1,0:T(8,128)(2,1)}, bf16[64,1024]{1,0:T(8,128)(2,1)S(1)}, u32[]{:S(2)}) copy-start(bf16[64,1024]{1,0:T(8,128)(2,1)S(1)} %collective-permute-done.4.refs_2_) | copy-start | bytes 393220
  50.0 0.7 %copy-start.5 = (bf16[64,1024]{1,0:T(8,128)(2,1)}, bf16[64,1024]{1,0:T(8,128)(2,1)S(1)}, u32[]{:S(2)}) copy-start(bf16[64,1024]{1,0:T(8,128)(2,1)S(1)} %collective-permute-done.5.refs_3_) | copy-start | bytes 393220
  55.6 3.9 %collective-permute-start.10 = (f32[2,1024]{1,0:T(2,128)}, f32[2,1024]{1,0:T(2,128)S(1)}, u32[]{:S(2)}, u32[]{:S(2)}) collective-permute-start(f32[2,1024]{1,0:T(2,128)} %get-tuple-element.25), channel_id=1, source_target_pairs={{0,2},{1,3},{2,0},{3,1},{4,6},{5,7},{6,4},{7,5},{8,10},{9,11},{10,... | collective-permute-start | bytes 24584 | tf_op jit(solution)/shard_map/ppermute | solution.py:358
  57.2 3.3 %collective-permute-start.11 = (f32[2,1024]{1,0:T(2,128)}, f32[2,1024]{1,0:T(2,128)S(1)}, u32[]{:S(2)}, u32[]{:S(2)}) collective-permute-start(f32[2,1024]{1,0:T(2,128)} %get-tuple-element.25), channel_id=1, source_target_pairs={{0,3},{1,2},{2,1},{3,0},{4,7},{5,6},{6,5},{7,4},{8,11},{9,10},{10,... | collective-permute-start | bytes 24584 | tf_op jit(solution)/shard_map/ppermute | solution.py:358
  57.2 3.3 %collective-permute-start.9 = (f32[2,1024]{1,0:T(2,128)}, f32[2,1024]{1,0:T(2,128)S(1)}, u32[]{:S(2)}, u32[]{:S(2)}) collective-permute-start(f32[2,1024]{1,0:T(2,128)} %get-tuple-element.25), channel_id=1, source_target_pairs={{0,1},{1,0},{2,3},{3,2},{4,5},{5,4},{6,7},{7,6},{8,9},{9,8},{10,11... | collective-permute-start | bytes 24584 | tf_op jit(solution)/shard_map/ppermute | solution.py:358

commit v6 on v5

--- a/solution.py
+++ b/solution.py
@@ -14,7 +14,7 @@
 MXU = 256
 CHUNKS = (64, 64)
 VMEM_LIMIT = 63 << 20
-NET_VMEM = 63 << 20
+NET_VMEM = 16 << 20
 
 QUANTILE_MID = 2.6095163822174072
 QUANTILE = (
@@ -88,7 +88,7 @@
             scaled = scaled + jump
         return carry
 
-    lax.fori_loop(0, part.shape[1] // LANES, fill, 0, unroll=max(1, 1024 // points))
+    lax.fori_loop(0, part.shape[1] // LANES, fill, 0, unroll=part.shape[1] // LANES)
 
 
 def panel_kernel(part, panel):
@@ -139,8 +139,8 @@
     def picked(b):
         halves = []
         for k in (0, 2):
-            q0 = pattern[4 * b + k]
-            q1 = pattern[4 * b + k + 1]
+            q0 = pattern[k, b]
+            q1 = pattern[k + 1, b]
             left = panel[q0 & 1, lax.shift_right_logical(q0, 1)]
             right = panel[1 - (q1 & 1), lax.shift_right_logical(q1, 1)]
             halves.append(jnp.where(low, left, right))
@@ -240,14 +240,11 @@
     )
 
 
-def net_kernel(first_point, n_received, pattern, tiles_hbm, *refs):
+def net_kernel(first_point, n_received, pattern, tiles_ref, *refs):
     received = refs[:n_received]
-    out_ref, sums_ref, losses, net_rows, tiles_ref, sem, sems = refs[-7:]
-    before = refs[n_received : -7]
+    out_ref, sums_ref, losses, net_rows, sem = refs[-5:]
+    before = refs[n_received : -5]
     blocks = tiles_ref.shape[0]
-    copies = [pltpu.make_async_copy(tiles_hbm.at[b], tiles_ref.at[b], sems.at[b]) for b in range(blocks)]
-    for copy in copies:
-        copy.start()
     points = losses.shape[1]
     slots = tiles_ref.shape[1] // LANES
     for q in range(blocks):
@@ -261,8 +258,7 @@
         losses[q] = total.astype(jnp.bfloat16)
     for b in range(blocks):
         at = slice(b * LANES, (b + 1) * LANES)
-        picked = jnp.concatenate([losses[pattern[slots * b + k]] for k in range(slots)], axis=1)
-        copies[b].wait()
+        picked = jnp.concatenate([losses[pattern[b, k]] for k in range(slots)], axis=1)
         net = jnp.dot(picked, tiles_ref[b], preferred_element_type=jnp.float32)
         net_rows[:, at] = net
         first = jnp.sum(net, axis=0, keepdims=True)
@@ -288,16 +284,13 @@
             jax.ShapeDtypeStruct((2, seg_dev), jnp.float32),
         ],
         in_specs=[pl.BlockSpec(memory_space=pltpu.SMEM)]
-        + [hbm]
-        + [vmem] * len(received)
+        + [vmem] * (1 + len(received))
         + [vmem, hbm][: len(extra)],
         out_specs=[hbm, vmem],
         scratch_shapes=[
             pltpu.VMEM((seg_dev // LANES, chunk, LANES), jnp.bfloat16),
             pltpu.VMEM((chunk, seg_dev), jnp.float32),
-            pltpu.VMEM(tiles.shape, jnp.bfloat16),
             pltpu.SemaphoreType.DMA,
-            pltpu.SemaphoreType.DMA((tiles.shape[0],)),
         ],
         input_output_aliases={} if before is None else {3 + len(received): 0},
         compiler_params=pltpu.CompilerParams(vmem_limit_bytes=NET_VMEM),
@@ -392,7 +385,7 @@
         out_specs=vmem,
         name="panel",
     )(own)
-    pattern = load_pattern.reshape(-1)
+    pattern = load_pattern.T
     slots = net_tiles.shape[1]
     tiles = net_tiles.reshape(seg_blocks, slots * LANES, LANES)
     chunks = []
@@ -421,7 +414,7 @@
         first += chunk
     done = None
     for first, chunk, received in chunks:
-        done = net_call(net_pattern.reshape(-1), tiles, received, first, chunk, points, seg_dev, done)
+        done = net_call(net_pattern, tiles, received, first, chunk, points, seg_dev, done)
     net_loss, sums = done
 
     total = pair_sum([sums] + [swapped(sums, "narrow", k) for k in range(1, n_narrow)])

time: 62.4 us -> 57.1 us (0.915)
  Pallas kernels: 34.7 us -> 28.6 us
  waiting for transfers between devices: 5.12 us -> 7.77 us
  local copies, waits for them, and re-layouts: 4.06 us -> 3.15 us
  other arithmetic: 2.04 us -> 1.34 us
    pallas_call x2, Pallas kernels: 9.93 us -> 3.84 us  [net_call(): pl.pallas_call(functools.partial(net_kernel, first_point, len(received)),...]
    ppermute x6, waiting for transfers between devices: 2.47 us -> 5.34 us  [shifted(): return lax.ppermute(x, axis, [(i, (i + k) % n) for i in range(n)])]
    reshape x2 -> x0, local copies, waits for them, and re-layouts: 1.33 us -> none  [the longest x1 0.67 us: body(): pattern = load_pattern.reshape(-1)]
    div x1, other arithmetic: 1.31 us -> 0.61 us  [body(): return (net_loss, total / P_SIZE)]
    unnamed x23 -> x16, local copies, waits for them, and re-layouts: 2.73 us -> 3.15 us
  transfers between devices with their start and end apart: 12 -> 12, of which waited for: 3 -> 4; matrix products, arithmetic and copies ran while one was open for 3% -> 0% of each run, Pallas kernels for 31% -> 28%
where the time goes in v6:
time: 57.1 us; the launch traced here: 56.7 us
  Pallas kernels  28.6 us (50%)
  starting transfers between devices  15 us (26%)
  waiting for transfers between devices  7.77 us (14%)
  local copies, waits for them, and re-layouts  3.15 us (6%)
  other arithmetic  1.34 us (2%)
  between operations  0.74 us (1%)
    pallas_call x2, Pallas kernels, loss_call(): pl.pallas_call(functools.partial(loss_kernel, n_parts, n_dest, split, dir...  21.7 us
    ppermute x6, starting transfers between devices, shifted(): return lax.ppermute(x, axis, [(i, (i + k) % n) for i in range(n)])  9.68 us
    ppermute x6, starting transfers between devices, swapped(): lax.ppermute(x, axis, [(i, i ^ k) for i in range(lax.axis_size(axis))])  5.36 us
    ppermute x6, waiting for transfers between devices, shifted(): return lax.ppermute(x, axis, [(i, (i + k) % n) for i in range(n)])  5.34 us
    pallas_call x2, Pallas kernels, net_call(): pl.pallas_call(functools.partial(net_kernel, first_point, len(received)),...  3.84 us
    unnamed x16, local copies, waits for them, and re-layouts  3.15 us
    pallas_call x1, Pallas kernels, body(): pl.pallas_call(panel_kernel, out_shape=jax.ShapeDtypeStruct((2, own.shape...  3.07 us
    ppermute x6, waiting for transfers between devices, swapped(): lax.ppermute(x, axis, [(i, i ^ k) for i in range(lax.axis_size(axis))])  2.43 us
  transfers between devices with their start and end apart: 12, of which 4 were waited for; matrix products, arithmetic and copies ran while one was open for 0% of the time, Pallas kernels for 28%

profile of v6, /device:TPU:0, one launch (start us, length us, event | category | flops | bytes accessed | tf_op | source)
XLA Modules:
  0.0 56.7 jit_solution(16092345335049257916)
XLA Ops:
  0.6 0.7 %pad_add_fusion.part = s32[2,2048]{1,0:T(2,128)S(1)} fusion(s32[1,2048]{1,0:T(1,128)} %bitcast.20, s32[1,2048]{1,0:T(1,128)} %bitcast.21), kind=kLoop, calls=%fused_computation | loop fusion | flops 4096 | bytes 32768 | tf_op jit(solution)/shard_map/stack | solution.py:378
  1.4 0.0 copy-start.7
  1.4 0.5 collective-permute-start
  1.9 2.6 %collective-permute-start.1 = (s32[2,2048]{1,0:T(2,128)S(1)}, s32[2,2048]{1,0:T(2,128)S(1)}, u32[]{:S(2)}, u32[]{:S(2)}) collective-permute-start(s32[2,2048]{1,0:T(2,128)S(1)} %pad_add_fusion.part), channel_id=1, source_target_pairs={{0,2},{1,3},{2,0},{3,1},{4,6},{5,7},{6,4},{7,5},{8,10},{9,11},{10,... | collective-permute-start | bytes 49160 | tf_op jit(solution)/shard_map/ppermute | solution.py:351
  4.5 0.1 collective-permute-start.2
  4.5 0.0 copy-done.7
  4.5 3.1 %panel.1.refs_0_ = bf16[2,16,128,128]{3,2,1,0:T(8,128)(2,1)} custom-call(s32[2,2048]{1,0:T(2,128)} %copy-done.7), custom_call_target="tpu_custom_call" | custom-call | tf_op jit(solution)/shard_map/panel/pallas_call | solution.py:381
  7.6 0.0 collective-permute-done.refs_1_
  7.6 0.0 copy-start.4
  7.6 0.0 collective-permute-done.1.refs_2_
  7.6 0.0 copy-start.5
  7.6 0.0 collective-permute-done.2.refs_3_
  7.6 0.0 copy-start.6
  7.6 0.6 copy-done.4
  8.2 0.0 copy-done.5
  8.2 0.0 copy-done.6
  8.2 0.0 copy-start.3
  8.2 10.8 %loss.3 = (f32[64,1024]{1,0:T(8,128)}, bf16[64,1024]{1,0:T(8,128)(2,1)}, bf16[64,1024]{1,0:T(8,128)(2,1)}, bf16[64,1024]{1,0:T(8,128)(2,1)}) custom-call(s32[4,64]{1,0:T(4,128)} %bitcast.18, bf16[2,16,128,128]{3,2,1,0:T(8,128)(2,1)} %panel.1.refs_0_, s32[2,2048]{1,0:T(2,128)} %copy-done.4, s32[2,2048]{1,0:T(2,128)} %copy-done.5, s32[2,2048]{1,0:T(2,128)} %copy-done.6, ...), custom_call_target="tpu_custom_call" | custom-call | tf_op jit(solution)/shard_map/loss/pallas_call | solution.py:317
  19.1 0.0 copy-start.2
  19.1 1.9 %collective-permute-start.6 = (bf16[64,1024]{1,0:T(8,128)(2,1)}, bf16[64,1024]{1,0:T(8,128)(2,1)S(1)}, u32[]{:S(2)}, u32[]{:S(2)}) collective-permute-start(bf16[64,1024]{1,0:T(8,128)(2,1)} %get-tuple-element.19), channel_id=1, source_target_pairs={{0,4},{4,8},{8,12},{12,0},{1,5},{5,9},{9,13},{13,1},{2,6},{6,10},{... | collective-permute-start | bytes 393224 | tf_op jit(solution)/shard_map/ppermute | solution.py:347
  20.9 2.6 %collective-permute-start.7 = (bf16[64,1024]{1,0:T(8,128)(2,1)}, bf16[64,1024]{1,0:T(8,128)(2,1)S(1)}, u32[]{:S(2)}, u32[]{:S(2)}) collective-permute-start(bf16[64,1024]{1,0:T(8,128)(2,1)} %get-tuple-element.20), channel_id=1, source_target_pairs={{0,8},{4,12},{8,0},{12,4},{1,9},{5,13},{9,1},{13,5},{2,10},{6,14},... | collective-permute-start | bytes 393224 | tf_op jit(solution)/shard_map/ppermute | solution.py:347
  23.5 1.3 %collective-permute-start.8 = (bf16[64,1024]{1,0:T(8,128)(2,1)}, bf16[64,1024]{1,0:T(8,128)(2,1)S(1)}, u32[]{:S(2)}, u32[]{:S(2)}) collective-permute-start(bf16[64,1024]{1,0:T(8,128)(2,1)} %get-tuple-element.21), channel_id=1, source_target_pairs={{0,12},{4,0},{8,4},{12,8},{1,13},{5,1},{9,5},{13,9},{2,14},{6,2},{... | collective-permute-start | bytes 393224 | tf_op jit(solution)/shard_map/ppermute | solution.py:347
  24.9 10.9 %loss.2 = (f32[64,1024]{1,0:T(8,128)}, bf16[64,1024]{1,0:T(8,128)(2,1)}, bf16[64,1024]{1,0:T(8,128)(2,1)}, bf16[64,1024]{1,0:T(8,128)(2,1)}) custom-call(s32[4,64]{1,0:T(4,128)} %bitcast.19, bf16[2,16,128,128]{3,2,1,0:T(8,128)(2,1)} %panel.1.refs_0_, s32[2,2048]{1,0:T(2,128)} %copy-done.4, s32[2,2048]{1,0:T(2,128)} %copy-done.5, s32[2,2048]{1,0:T(2,128)} %copy-done.6, ...), custom_call_target="tpu_custom_call" | custom-call | tf_op jit(solution)/shard_map/loss/pallas_call | solution.py:317
  35.8 0.7 %collective-permute-start.3 = (bf16[64,1024]{1,0:T(8,128)(2,1)}, bf16[64,1024]{1,0:T(8,128)(2,1)S(1)}, u32[]{:S(2)}, u32[]{:S(2)}) collective-permute-start(bf16[64,1024]{1,0:T(8,128)(2,1)} %get-tuple-element.15), channel_id=1, source_target_pairs={{0,4},{4,8},{8,12},{12,0},{1,5},{5,9},{9,13},{13,1},{2,6},{6,10},{... | collective-permute-start | bytes 393224 | tf_op jit(solution)/shard_map/ppermute | solution.py:347
  36.5 0.3 collective-permute-start.4
  36.9 0.0 collective-permute-done.6.refs_1_
  36.9 2.8 %collective-permute-start.5 = (bf16[64,1024]{1,0:T(8,128)(2,1)}, bf16[64,1024]{1,0:T(8,128)(2,1)S(1)}, u32[]{:S(2)}, u32[]{:S(2)}) collective-permute-start(bf16[64,1024]{1,0:T(8,128)(2,1)} %get-tuple-element.17), channel_id=1, source_target_pairs={{0,12},{4,0},{8,4},{12,8},{1,13},{5,1},{9,5},{13,9},{2,14},{6,2},{... | collective-permute-start | bytes 393224 | tf_op jit(solution)/shard_map/ppermute | solution.py:347
  39.7 0.0 collective-permute-done.7.refs_2_
  39.7 0.0 collective-permute-done.8.refs_3_
  39.7 0.0 copy-done.3
  39.7 0.0 copy-done.2
  39.7 0.0 copy-start
  39.7 1.6 %copy-done = bf16[8,8,128,128]{3,2,1,0:T(8,128)(2,1)S(1)} copy-done((bf16[8,8,128,128]{3,2,1,0:T(8,128)(2,1)S(1)}, bf16[8,8,128,128]{3,2,1,0:T(8,128)(2,1)}, u32[]{:S(2)}) %copy-start) | copy-done | bytes 2097176
  41.3 1.9 %net.2 = (f32[128,1024]{1,0:T(8,128)}, f32[2,1024]{1,0:T(2,128)S(1)}) custom-call(s32[8,8]{1,0:T(8,128)S(1)} %copy-done.3, bf16[8,1024,128]{2,1,0:T(8,128)(2,1)S(1)} %bitcast.8, f32[64,1024]{1,0:T(8,128)S(1)} %copy-done.2, bf16[64,1024]{1,0:T(8,128)(2,1)S(1)} %collective-permute-done.6.refs_1_, bf16[64,1024]{1,0:T(8,128)(2,1)S(1)} %collective-permute-done.7.refs_2_, ...), custom_call_target="tpu_custom_call" | custom-call | tf_op jit(solution)/shard_map/net/pallas_call | solution.py:280
  43.2 1.1 %collective-permute-done.3.refs_1_ = bf16[64,1024]{1,0:T(8,128)(2,1)S(1)} collective-permute-done((bf16[64,1024]{1,0:T(8,128)(2,1)}, bf16[64,1024]{1,0:T(8,128)(2,1)S(1)}, u32[]{:S(2)}, u32[]{:S(2)}) %collective-permute-start.3) | collective-permute-done | bytes 131104 | tf_op jit(solution)/shard_map/ppermute | solution.py:347
  44.3 4.2 %collective-permute-done.4.refs_2_ = bf16[64,1024]{1,0:T(8,128)(2,1)S(1)} collective-permute-done((bf16[64,1024]{1,0:T(8,128)(2,1)}, bf16[64,1024]{1,0:T(8,128)(2,1)S(1)}, u32[]{:S(2)}, u32[]{:S(2)}) %collective-permute-start.4) | collective-permute-done | bytes 131104 | tf_op jit(solution)/shard_map/ppermute | solution.py:347
  48.5 0.0 collective-permute-done.5.refs_3_
  48.5 0.0 copy-start.1
  48.5 0.9 %copy-done.1 = f32[64,1024]{1,0:T(8,128)S(1)} copy-done((f32[64,1024]{1,0:T(8,128)S(1)}, f32[64,1024]{1,0:T(8,128)}, u32[]{:S(2)}) %copy-start.1) | copy-done | bytes 262168
  49.5 1.9 %net.3 = (f32[128,1024]{1,0:T(8,128)}, f32[2,1024]{1,0:T(2,128)S(1)}) custom-call(s32[8,8]{1,0:T(8,128)S(1)} %copy-done.3, bf16[8,1024,128]{2,1,0:T(8,128)(2,1)S(1)} %bitcast.9, f32[64,1024]{1,0:T(8,128)S(1)} %copy-done.1, bf16[64,1024]{1,0:T(8,128)(2,1)S(1)} %collective-permute-done.3.refs_1_, ...), custom_call_target="tpu_custom_call", output_to_operand_aliasing={{0}: (7, {})} | custom-call | tf_op jit(solution)/shard_map/net/pallas_call | solution.py:280
  51.4 1.6 %collective-permute-start.10 = (f32[2,1024]{1,0:T(2,128)S(1)}, f32[2,1024]{1,0:T(2,128)S(1)}, u32[]{:S(2)}, u32[]{:S(2)}) collective-permute-start(f32[2,1024]{1,0:T(2,128)S(1)} %get-tuple-element.25), channel_id=1, source_target_pairs={{0,2},{1,3},{2,0},{3,1},{4,6},{5,7},{6,4},{7,5},{8,10},{9,11},{10,... | collective-permute-start | bytes 24584 | tf_op jit(solution)/shard_map/ppermute | solution.py:351
  53.0 0.0 collective-permute-start.11
  53.0 0.6 %collective-permute-start.9 = (f32[2,1024]{1,0:T(2,128)S(1)}, f32[2,1024]{1,0:T(2,128)S(1)}, u32[]{:S(2)}, u32[]{:S(2)}) collective-permute-start(f32[2,1024]{1,0:T(2,128)S(1)} %get-tuple-element.25), channel_id=1, source_target_pairs={{0,1},{1,0},{2,3},{3,2},{4,5},{5,4},{6,7},{7,6},{8,9},{9,8},{10,11... | collective-permute-start | bytes 24584 | tf_op jit(solution)/shard_map/ppermute | solution.py:351
  53.6 1.5 %collective-permute-done.10 = f32[2,1024]{1,0:T(2,128)S(1)} collective-permute-done((f32[2,1024]{1,0:T(2,128)S(1)}, f32[2,1024]{1,0:T(2,128)S(1)}, u32[]{:S(2)}, u32[]{:S(2)}) %collective-permute-start.10) | collective-permute-done | bytes 8224 | tf_op jit(solution)/shard_map/ppermute | solution.py:351
  55.1 0.9 %collective-permute-done.11 = f32[2,1024]{1,0:T(2,128)S(1)} collective-permute-done((f32[2,1024]{1,0:T(2,128)S(1)}, f32[2,1024]{1,0:T(2,128)S(1)}, u32[]{:S(2)}, u32[]{:S(2)}) %collective-permute-start.11) | collective-permute-done | bytes 8224 | tf_op jit(solution)/shard_map/ppermute | solution.py:351
  56.1 0.0 collective-permute-done.9
  56.1 0.6 %add_multiply_fusion = f32[2,1024]{1,0:T(2,128)} fusion(f32[2,1024]{1,0:T(2,128)S(1)} %collective-permute-done.10, f32[2,1024]{1,0:T(2,128)S(1)} %collective-permute-done.11, f32[2,1024]{1,0:T(2,128)S(1)} %get-tuple-element.25, f32[2,1024]{1,0:T(2,128)S(1)} %collective-permute-done.9), kind=kLoop, calls=%fused_computation.1 | loop fusion | flops 8192 | bytes 40960 | tf_op jit(solution)/shard_map/div | solution.py:421
Async XLA Ops:
  1.4 3.2 %copy-start.7 = (s32[2,2048]{1,0:T(2,128)}, s32[2,2048]{1,0:T(2,128)S(1)}, u32[]{:S(2)}) copy-start(s32[2,2048]{1,0:T(2,128)S(1)} %pad_add_fusion.part) | copy-start | bytes 49156
  1.4 6.2 %collective-permute-start = (s32[2,2048]{1,0:T(2,128)S(1)}, s32[2,2048]{1,0:T(2,128)S(1)}, u32[]{:S(2)}, u32[]{:S(2)}) collective-permute-start(s32[2,2048]{1,0:T(2,128)S(1)} %pad_add_fusion.part), channel_id=1, source_target_pairs={{0,1},{1,0},{2,3},{3,2},{4,5},{5,4},{6,7},{7,6},{8,9},{9,8},{10,11... | collective-permute-start | bytes 49160 | tf_op jit(solution)/shard_map/ppermute | solution.py:351
  1.9 5.7 %collective-permute-start.1 = (s32[2,2048]{1,0:T(2,128)S(1)}, s32[2,2048]{1,0:T(2,128)S(1)}, u32[]{:S(2)}, u32[]{:S(2)}) collective-permute-start(s32[2,2048]{1,0:T(2,128)S(1)} %pad_add_fusion.part), channel_id=1, source_target_pairs={{0,2},{1,3},{2,0},{3,1},{4,6},{5,7},{6,4},{7,5},{8,10},{9,11},{10,... | collective-permute-start | bytes 49160 | tf_op jit(solution)/shard_map/ppermute | solution.py:351
  4.5 3.2 %collective-permute-start.2 = (s32[2,2048]{1,0:T(2,128)S(1)}, s32[2,2048]{1,0:T(2,128)S(1)}, u32[]{:S(2)}, u32[]{:S(2)}) collective-permute-start(s32[2,2048]{1,0:T(2,128)S(1)} %pad_add_fusion.part), channel_id=1, source_target_pairs={{0,3},{1,2},{2,1},{3,0},{4,7},{5,6},{6,5},{7,4},{8,11},{9,10},{10,... | collective-permute-start | bytes 49160 | tf_op jit(solution)/shard_map/ppermute | solution.py:351
  7.6 0.6 %copy-start.4 = (s32[2,2048]{1,0:T(2,128)}, s32[2,2048]{1,0:T(2,128)S(1)}, u32[]{:S(2)}) copy-start(s32[2,2048]{1,0:T(2,128)S(1)} %collective-permute-done.refs_1_) | copy-start | bytes 49156
  7.6 0.6 %copy-start.5 = (s32[2,2048]{1,0:T(2,128)}, s32[2,2048]{1,0:T(2,128)S(1)}, u32[]{:S(2)}) copy-start(s32[2,2048]{1,0:T(2,128)S(1)} %collective-permute-done.1.refs_2_) | copy-start | bytes 49156
  7.6 0.6 %copy-start.6 = (s32[2,2048]{1,0:T(2,128)}, s32[2,2048]{1,0:T(2,128)S(1)}, u32[]{:S(2)}) copy-start(s32[2,2048]{1,0:T(2,128)S(1)} %collective-permute-done.2.refs_3_) | copy-start | bytes 49156
  8.2 31.5 %copy-start.3 = (s32[8,8]{1,0:T(8,128)S(1)}, s32[8,8]{1,0:T(8,128)}, u32[]{:S(2)}) copy-start(s32[8,8]{1,0:T(8,128)} %pattern.3) | copy-start | bytes 772
  19.1 20.6 %copy-start.2 = (f32[64,1024]{1,0:T(8,128)S(1)}, f32[64,1024]{1,0:T(8,128)}, u32[]{:S(2)}) copy-start(f32[64,1024]{1,0:T(8,128)} %get-tuple-element.18.refs_0_) | copy-start | bytes 786436
  19.1 17.8 %collective-permute-start.6 = (bf16[64,1024]{1,0:T(8,128)(2,1)}, bf16[64,1024]{1,0:T(8,128)(2,1)S(1)}, u32[]{:S(2)}, u32[]{:S(2)}) collective-permute-start(bf16[64,1024]{1,0:T(8,128)(2,1)} %get-tuple-element.19), channel_id=1, source_target_pairs={{0,4},{4,8},{8,12},{12,0},{1,5},{5,9},{9,13},{13,1},{2,6},{6,10},{... | collective-permute-start | bytes 393224 | tf_op jit(solution)/shard_map/ppermute | solution.py:347
  20.9 18.7 %collective-permute-start.7 = (bf16[64,1024]{1,0:T(8,128)(2,1)}, bf16[64,1024]{1,0:T(8,128)(2,1)S(1)}, u32[]{:S(2)}, u32[]{:S(2)}) collective-permute-start(bf16[64,1024]{1,0:T(8,128)(2,1)} %get-tuple-element.20), channel_id=1, source_target_pairs={{0,8},{4,12},{8,0},{12,4},{1,9},{5,13},{9,1},{13,5},{2,10},{6,14},... | collective-permute-start | bytes 393224 | tf_op jit(solution)/shard_map/ppermute | solution.py:347
  23.5 16.1 %collective-permute-start.8 = (bf16[64,1024]{1,0:T(8,128)(2,1)}, bf16[64,1024]{1,0:T(8,128)(2,1)S(1)}, u32[]{:S(2)}, u32[]{:S(2)}) collective-permute-start(bf16[64,1024]{1,0:T(8,128)(2,1)} %get-tuple-element.21), channel_id=1, source_target_pairs={{0,12},{4,0},{8,4},{12,8},{1,13},{5,1},{9,5},{13,9},{2,14},{6,2},{... | collective-permute-start | bytes 393224 | tf_op jit(solution)/shard_map/ppermute | solution.py:347
  35.8 8.5 %collective-permute-start.3 = (bf16[64,1024]{1,0:T(8,128)(2,1)}, bf16[64,1024]{1,0:T(8,128)(2,1)S(1)}, u32[]{:S(2)}, u32[]{:S(2)}) collective-permute-start(bf16[64,1024]{1,0:T(8,128)(2,1)} %get-tuple-element.15), channel_id=1, source_target_pairs={{0,4},{4,8},{8,12},{12,0},{1,5},{5,9},{9,13},{13,1},{2,6},{6,10},{... | collective-permute-start | bytes 393224 | tf_op jit(solution)/shard_map/ppermute | solution.py:347
  36.5 12.0 %collective-permute-start.4 = (bf16[64,1024]{1,0:T(8,128)(2,1)}, bf16[64,1024]{1,0:T(8,128)(2,1)S(1)}, u32[]{:S(2)}, u32[]{:S(2)}) collective-permute-start(bf16[64,1024]{1,0:T(8,128)(2,1)} %get-tuple-element.16), channel_id=1, source_target_pairs={{0,8},{4,12},{8,0},{12,4},{1,9},{5,13},{9,1},{13,5},{2,10},{6,14},... | collective-permute-start | bytes 393224 | tf_op jit(solution)/shard_map/ppermute | solution.py:347
  36.9 11.7 %collective-permute-start.5 = (bf16[64,1024]{1,0:T(8,128)(2,1)}, bf16[64,1024]{1,0:T(8,128)(2,1)S(1)}, u32[]{:S(2)}, u32[]{:S(2)}) collective-permute-start(bf16[64,1024]{1,0:T(8,128)(2,1)} %get-tuple-element.17), channel_id=1, source_target_pairs={{0,12},{4,0},{8,4},{12,8},{1,13},{5,1},{9,5},{13,9},{2,14},{6,2},{... | collective-permute-start | bytes 393224 | tf_op jit(solution)/shard_map/ppermute | solution.py:347
  39.7 1.6 %copy-start = (bf16[8,8,128,128]{3,2,1,0:T(8,128)(2,1)S(1)}, bf16[8,8,128,128]{3,2,1,0:T(8,128)(2,1)}, u32[]{:S(2)}) copy-start(bf16[8,8,128,128]{3,2,1,0:T(8,128)(2,1)} %param.16) | copy-start | bytes 6291460
  48.5 1.0 %copy-start.1 = (f32[64,1024]{1,0:T(8,128)S(1)}, f32[64,1024]{1,0:T(8,128)}, u32[]{:S(2)}) copy-start(f32[64,1024]{1,0:T(8,128)} %get-tuple-element.14.refs_0_) | copy-start | bytes 786436
  51.4 3.7 %collective-permute-start.10 = (f32[2,1024]{1,0:T(2,128)S(1)}, f32[2,1024]{1,0:T(2,128)S(1)}, u32[]{:S(2)}, u32[]{:S(2)}) collective-permute-start(f32[2,1024]{1,0:T(2,128)S(1)} %get-tuple-element.25), channel_id=1, source_target_pairs={{0,2},{1,3},{2,0},{3,1},{4,6},{5,7},{6,4},{7,5},{8,10},{9,11},{10,... | collective-permute-start | bytes 24584 | tf_op jit(solution)/shard_map/ppermute | solution.py:351
  53.0 3.1 %collective-permute-start.11 = (f32[2,1024]{1,0:T(2,128)S(1)}, f32[2,1024]{1,0:T(2,128)S(1)}, u32[]{:S(2)}, u32[]{:S(2)}) collective-permute-start(f32[2,1024]{1,0:T(2,128)S(1)} %get-tuple-element.25), channel_id=1, source_target_pairs={{0,3},{1,2},{2,1},{3,0},{4,7},{5,6},{6,5},{7,4},{8,11},{9,10},{10,... | collective-permute-start | bytes 24584 | tf_op jit(solution)/shard_map/ppermute | solution.py:351
  53.0 3.1 %collective-permute-start.9 = (f32[2,1024]{1,0:T(2,128)S(1)}, f32[2,1024]{1,0:T(2,128)S(1)}, u32[]{:S(2)}, u32[]{:S(2)}) collective-permute-start(f32[2,1024]{1,0:T(2,128)S(1)} %get-tuple-element.25), channel_id=1, source_target_pairs={{0,1},{1,0},{2,3},{3,2},{4,5},{5,4},{6,7},{7,6},{8,9},{9,8},{10,11... | collective-permute-start | bytes 24584 | tf_op jit(solution)/shard_map/ppermute | solution.py:351

commit v7 on v6

--- a/solution.py
+++ b/solution.py
@@ -12,7 +12,7 @@
 ROWS = 16
 DEST_CHUNK = 4
 MXU = 256
-CHUNKS = (64, 64)
+CHUNKS = (80, 48)
 VMEM_LIMIT = 63 << 20
 NET_VMEM = 16 << 20
 
@@ -91,23 +91,21 @@
     lax.fori_loop(0, part.shape[1] // LANES, fill, 0, unroll=part.shape[1] // LANES)
 
 
-def panel_kernel(part, panel):
-    fill_panel(panel, 0, part, lax.axis_index("narrow") * panel.shape[2])
-
-
-def loss_kernel(n_parts, n_dest, split, direct, first_point, pattern, *refs):
+def panel_kernel(all_points, part, panel):
+    fill_panel(panel, 0, part, lax.axis_index("narrow") * all_points)
+
+
+def loss_kernel(n_parts, n_dest, split, direct, has_panel, all_points, first_point, pattern, *refs):
     me = lax.axis_index("narrow")
     base = lax.axis_index("wide") if direct else 0
-    own_panel = refs[0]
-    parts = refs[1:n_parts]
+    parts = refs[:n_parts]
     sources = refs[n_parts : n_parts + 4]
     outs = refs[n_parts + 4 : -8]
     panel, load_ref, thr_ref, expo_ref, seg_ref, even, odd, sems = refs[-8:]
     masked = (even, odd)
     points = panel.shape[2]
     blocks = load_ref.shape[0]
-    columns = own_panel.shape[1]
-    all_points = own_panel.shape[2]
+    columns = parts[-1].shape[1] // LANES
     seg_dev = (outs[0] if direct else outs[0].at[0]).shape[1]
     sub = seg_dev // (2 * MXU)
     group = split * sub
@@ -117,18 +115,15 @@
         pltpu.make_async_copy(source, target, sems.at[i])
         for i, (source, target) in enumerate(zip(sources, (load_ref, thr_ref, expo_ref, seg_ref)))
     ]
-    copies.append(
-        pltpu.make_async_copy(
-            own_panel.at[:, :, pl.ds(first_point, points), :],
-            panel.at[:, pl.ds(me * columns, columns)],
-            sems.at[4],
+    if has_panel:
+        copies.append(
+            pltpu.make_async_copy(parts[0], panel.at[:, pl.ds(me * columns, columns)], sems.at[4])
         )
-    )
     for copy in copies:
         copy.start()
 
-    for k in range(1, n_parts):
-        fill_panel(panel, (me ^ k) * columns, parts[k - 1], me * all_points + first_point)
+    for k in range(int(has_panel), n_parts):
+        fill_panel(panel, (me ^ k) * columns, parts[k], me * all_points + first_point)
 
     for copy in copies:
         copy.wait()
@@ -240,10 +235,19 @@
     )
 
 
-def net_kernel(first_point, n_received, pattern, tiles_ref, *refs):
+def net_kernel(first_point, n_received, has_before, pattern, tiles_ref, *refs):
     received = refs[:n_received]
-    out_ref, sums_ref, losses, net_rows, sem = refs[-5:]
-    before = refs[n_received : -5]
+    losses, net_rows, sem, keep_sem = refs[-4:]
+    n_before = 2 if has_before else 0
+    before = refs[n_received : n_received + n_before]
+    keep = refs[n_received + n_before : -4]
+    if len(keep) == 4:
+        keep_in, out_ref, sums_ref, keep_out = keep
+        keep_copy = pltpu.make_async_copy(keep_in, keep_out, keep_sem)
+        keep_copy.start()
+    else:
+        keep_copy = None
+        out_ref, sums_ref = keep
     blocks = tiles_ref.shape[0]
     points = losses.shape[1]
     slots = tiles_ref.shape[1] // LANES
@@ -271,37 +275,42 @@
     copy = pltpu.make_async_copy(net_rows, out_ref.at[pl.ds(first_point, points), :], sem)
     copy.start()
     copy.wait()
-
-
-def net_call(net_pattern, tiles, received, first_point, chunk, points, seg_dev, before):
+    if keep_copy is not None:
+        keep_copy.wait()
+
+
+def net_call(net_pattern, tiles, received, first_point, chunk, points, seg_dev, before, keep):
     vmem = pl.BlockSpec(memory_space=pltpu.VMEM)
     hbm = pl.BlockSpec(memory_space=pltpu.HBM)
     extra = [] if before is None else [before[1], before[0]]
     return pl.pallas_call(
-        functools.partial(net_kernel, first_point, len(received)),
+        functools.partial(net_kernel, first_point, len(received), before is not None),
         out_shape=[
             jax.ShapeDtypeStruct((points, seg_dev), jnp.float32),
             jax.ShapeDtypeStruct((2, seg_dev), jnp.float32),
-        ],
+        ]
+        + [jax.ShapeDtypeStruct(k.shape, k.dtype) for k in keep],
         in_specs=[pl.BlockSpec(memory_space=pltpu.SMEM)]
         + [vmem] * (1 + len(received))
-        + [vmem, hbm][: len(extra)],
-        out_specs=[hbm, vmem],
+        + [vmem, hbm][: len(extra)]
+        + [hbm] * len(keep),
+        out_specs=[hbm, vmem] + [vmem] * len(keep),
         scratch_shapes=[
             pltpu.VMEM((seg_dev // LANES, chunk, LANES), jnp.bfloat16),
             pltpu.VMEM((chunk, seg_dev), jnp.float32),
+            pltpu.SemaphoreType.DMA,
             pltpu.SemaphoreType.DMA,
         ],
         input_output_aliases={} if before is None else {3 + len(received): 0},
         compiler_params=pltpu.CompilerParams(vmem_limit_bytes=NET_VMEM),
         name="net",
-    )(net_pattern, tiles, *received, *extra)
-
-
-def loss_call(pattern, own_panel, parts, loadings, threshold, exposure, segment_map, n_dest, first_point, points, seg_dev, direct):
+    )(net_pattern, tiles, *received, *extra, *keep)
+
+
+def loss_call(pattern, parts, has_panel, loadings, threshold, exposure, segment_map, n_dest, all_points, first_point, points, seg_dev, direct):
     blocks = loadings.shape[0]
-    n_parts = len(parts) + 1
-    columns = own_panel.shape[1] * n_parts
+    n_parts = len(parts)
+    columns = parts[-1].shape[1] // LANES * n_parts
     split = min(n_dest, DEST_CHUNK)
     if direct:
         out_shape = [
@@ -315,9 +324,9 @@
     smem = pl.BlockSpec(memory_space=pltpu.SMEM)
     hbm = pl.BlockSpec(memory_space=pltpu.HBM)
     return pl.pallas_call(
-        functools.partial(loss_kernel, n_parts, n_dest, split, direct, first_point),
+        functools.partial(loss_kernel, n_parts, n_dest, split, direct, has_panel, all_points, first_point),
         out_shape=out_shape,
-        in_specs=[smem, hbm] + [vmem] * (n_parts - 1) + [hbm] * 4,
+        in_specs=[smem, hbm if has_panel else vmem] + [vmem] * (n_parts - 1) + [hbm] * 4,
         out_specs=[vmem] * len(out_shape),
         scratch_shapes=[
             pltpu.VMEM((2, columns, points, LANES), jnp.bfloat16),
@@ -333,7 +342,6 @@
         name="loss",
     )(
         pattern,
-        own_panel,
         *parts,
         loadings.reshape(blocks, 256, LANES),
         threshold.reshape(blocks, LANES),
@@ -379,8 +387,10 @@
     parts = [swapped(own, "narrow", k) for k in range(1, n_narrow)]
     vmem = pl.BlockSpec(memory_space=pltpu.VMEM)
     own_panel = pl.pallas_call(
-        panel_kernel,
-        out_shape=jax.ShapeDtypeStruct((2, own.shape[1] // LANES, points, LANES), jnp.bfloat16),
+        functools.partial(panel_kernel, points),
+        out_shape=jax.ShapeDtypeStruct(
+            (2, own.shape[1] // LANES, CHUNKS[0] * points // sum(CHUNKS), LANES), jnp.bfloat16
+        ),
         in_specs=[vmem],
         out_specs=vmem,
         name="panel",
@@ -394,13 +404,14 @@
         chunk = chunk * points // sum(CHUNKS)
         partial = loss_call(
             pattern,
-            own_panel,
-            parts,
+            [own_panel if first == 0 else own] + parts,
+            first == 0,
             loadings,
             threshold,
             exposure,
             segment_map,
             n_dest,
+            points,
             first,
             chunk,
             seg_dev,
@@ -413,8 +424,11 @@
         chunks.append((first, chunk, received))
         first += chunk
     done = None
-    for first, chunk, received in chunks:
-        done = net_call(net_pattern, tiles, received, first, chunk, points, seg_dev, done)
+    for i, (first, chunk, received) in enumerate(chunks):
+        keep = [chunks[i + 1][2][0]] if direct and i + 1 < len(chunks) else []
+        *done, = net_call(net_pattern, tiles, received, first, chunk, points, seg_dev, done, keep)
+        if keep:
+            chunks[i + 1][2][0] = done.pop()
     net_loss, sums = done
 
     total = pair_sum([sums] + [swapped(sums, "narrow", k) for k in range(1, n_narrow)])

time: 57.1 us -> 53.3 us (0.933)
  waiting for transfers between devices: 7.77 us -> 4.01 us
    ppermute x6, waiting for transfers between devices: 5.34 us -> 1.59 us  [shifted(): return lax.ppermute(x, axis, [(i, (i + k) % n) for i in range(n)])]
    pallas_call x2, Pallas kernels: 21.7 us -> 22.5 us  [loss_call(): pl.pallas_call(functools.partial(loss_kernel, n_parts, n_dest, split, dir...]
    unnamed x16 -> x18, local copies, waits for them, and re-layouts: 3.15 us -> 3.13 us
  transfers between devices with their start and end apart: 12 -> 12, of which waited for: 4 -> 4; matrix products, arithmetic and copies ran while one was open for 0% -> 0% of each run, Pallas kernels for 28% -> 29%
where the time goes in v7:
time: 53.3 us; the launch traced here: 52.8 us
  Pallas kernels  29.1 us (55%)
  starting transfers between devices  14.5 us (27%)
  waiting for transfers between devices  4.01 us (8%)
  local copies, waits for them, and re-layouts  3.13 us (6%)
  other arithmetic  1.34 us (3%)
  between operations  0.73 us (1%)
    pallas_call x2, Pallas kernels, loss_call(): pl.pallas_call(functools.partial(loss_kernel, n_parts, n_dest, split, dir...  22.5 us
    ppermute x6, starting transfers between devices, shifted(): return lax.ppermute(x, axis, [(i, (i + k) % n) for i in range(n)])  9.45 us
    ppermute x6, starting transfers between devices, swapped(): lax.ppermute(x, axis, [(i, i ^ k) for i in range(lax.axis_size(axis))])  5.04 us
    pallas_call x2, Pallas kernels, net_call(): pl.pallas_call(functools.partial(net_kernel, first_point, len(received),...  4.07 us
    unnamed x18, local copies, waits for them, and re-layouts  3.13 us
    pallas_call x1, Pallas kernels, body(): pl.pallas_call(functools.partial(panel_kernel, points), out_shape=jax.Sha...  2.51 us
    ppermute x6, waiting for transfers between devices, swapped(): lax.ppermute(x, axis, [(i, i ^ k) for i in range(lax.axis_size(axis))])  2.42 us
    ppermute x6, waiting for transfers between devices, shifted(): return lax.ppermute(x, axis, [(i, (i + k) % n) for i in range(n)])  1.59 us
  transfers between devices with their start and end apart: 12, of which 4 were waited for; matrix products, arithmetic and copies ran while one was open for 0% of the time, Pallas kernels for 29%

profile of v7, /device:TPU:0, one launch (start us, length us, event | category | flops | bytes accessed | tf_op | source)
XLA Modules:
  0.0 52.8 jit_solution(556166331406264937)
XLA Ops:
  0.6 0.7 %pad_add_fusion.part.refs_0_ = s32[2,2048]{1,0:T(2,128)S(1)} fusion(s32[1,2048]{1,0:T(1,128)} %bitcast.20, s32[1,2048]{1,0:T(1,128)} %bitcast.21), kind=kLoop, calls=%fused_computation | loop fusion | flops 4096 | bytes 32768 | tf_op jit(solution)/shard_map/stack | solution.py:386
  1.4 0.0 copy-start.5
  1.4 2.4 %collective-permute-start.2 = (s32[2,2048]{1,0:T(2,128)S(1)}, s32[2,2048]{1,0:T(2,128)S(1)}, u32[]{:S(2)}, u32[]{:S(2)}) collective-permute-start(s32[2,2048]{1,0:T(2,128)S(1)} %pad_add_fusion.part.refs_0_), channel_id=1, source_target_pairs={{0,3},{1,2},{2,1},{3,0},{4,7},{5,6},{6,5},{7,4},{8,11},{9,10},{10,... | collective-permute-start | bytes 49160 | tf_op jit(solution)/shard_map/ppermute | solution.py:359
  3.8 0.6 %collective-permute-start.1 = (s32[2,2048]{1,0:T(2,128)S(1)}, s32[2,2048]{1,0:T(2,128)S(1)}, u32[]{:S(2)}, u32[]{:S(2)}) collective-permute-start(s32[2,2048]{1,0:T(2,128)S(1)} %pad_add_fusion.part.refs_0_), channel_id=1, source_target_pairs={{0,2},{1,3},{2,0},{3,1},{4,6},{5,7},{6,4},{7,5},{8,10},{9,11},{10,... | collective-permute-start | bytes 49160 | tf_op jit(solution)/shard_map/ppermute | solution.py:359
  4.5 0.0 collective-permute-start
  4.5 0.0 copy-done.5
  4.5 2.5 %panel.1.refs_0_ = bf16[2,16,80,128]{3,2,1,0:T(8,128)(2,1)} custom-call(s32[2,2048]{1,0:T(2,128)} %copy-done.5), custom_call_target="tpu_custom_call" | custom-call | tf_op jit(solution)/shard_map/panel/pallas_call | solution.py:389
  7.0 0.0 collective-permute-done.2.refs_3_
  7.0 0.0 copy-start.6
  7.0 0.5 %collective-permute-done.1.refs_2_ = s32[2,2048]{1,0:T(2,128)S(1)} collective-permute-done((s32[2,2048]{1,0:T(2,128)S(1)}, s32[2,2048]{1,0:T(2,128)S(1)}, u32[]{:S(2)}, u32[]{:S(2)}) %collective-permute-start.1) | collective-permute-done | bytes 16416 | tf_op jit(solution)/shard_map/ppermute | solution.py:359
  7.6 0.0 copy-start.7
  7.6 0.0 collective-permute-done.refs_1_
  7.6 0.0 copy-start.8
  7.6 0.0 copy-done.6
  7.6 0.5 %copy-done.7 = s32[2,2048]{1,0:T(2,128)} copy-done((s32[2,2048]{1,0:T(2,128)}, s32[2,2048]{1,0:T(2,128)S(1)}, u32[]{:S(2)}) %copy-start.7) | copy-done | bytes 16408
  8.2 0.0 copy-done.8
  8.2 0.0 copy-start.4
  8.2 12.2 %loss.2 = (f32[80,1024]{1,0:T(8,128)}, bf16[80,1024]{1,0:T(8,128)(2,1)}, bf16[80,1024]{1,0:T(8,128)(2,1)}, bf16[80,1024]{1,0:T(8,128)(2,1)}) custom-call(s32[4,64]{1,0:T(4,128)} %bitcast.18, bf16[2,16,80,128]{3,2,1,0:T(8,128)(2,1)} %panel.1.refs_0_, s32[2,2048]{1,0:T(2,128)} %copy-done.8, s32[2,2048]{1,0:T(2,128)} %copy-done.7, s32[2,2048]{1,0:T(2,128)} %copy-done.6, ...), custom_call_target="tpu_custom_call" | custom-call | tf_op jit(solution)/shard_map/loss/pallas_call | solution.py:326
  20.3 0.0 copy-start.2
  20.3 1.6 %collective-permute-start.3 = (bf16[80,1024]{1,0:T(8,128)(2,1)}, bf16[80,1024]{1,0:T(8,128)(2,1)S(1)}, u32[]{:S(2)}, u32[]{:S(2)}) collective-permute-start(bf16[80,1024]{1,0:T(8,128)(2,1)} %get-tuple-element.16), channel_id=1, source_target_pairs={{0,4},{4,8},{8,12},{12,0},{1,5},{5,9},{9,13},{13,1},{2,6},{6,10},{... | collective-permute-start | bytes 491528 | tf_op jit(solution)/shard_map/ppermute | solution.py:355
  22.0 2.6 %collective-permute-start.4 = (bf16[80,1024]{1,0:T(8,128)(2,1)}, bf16[80,1024]{1,0:T(8,128)(2,1)S(1)}, u32[]{:S(2)}, u32[]{:S(2)}) collective-permute-start(bf16[80,1024]{1,0:T(8,128)(2,1)} %get-tuple-element.17), channel_id=1, source_target_pairs={{0,8},{4,12},{8,0},{12,4},{1,9},{5,13},{9,1},{13,5},{2,10},{6,14},... | collective-permute-start | bytes 491528 | tf_op jit(solution)/shard_map/ppermute | solution.py:355
  24.6 1.3 %collective-permute-start.5 = (bf16[80,1024]{1,0:T(8,128)(2,1)}, bf16[80,1024]{1,0:T(8,128)(2,1)S(1)}, u32[]{:S(2)}, u32[]{:S(2)}) collective-permute-start(bf16[80,1024]{1,0:T(8,128)(2,1)} %get-tuple-element.18), channel_id=1, source_target_pairs={{0,12},{4,0},{8,4},{12,8},{1,13},{5,1},{9,5},{13,9},{2,14},{6,2},{... | collective-permute-start | bytes 491528 | tf_op jit(solution)/shard_map/ppermute | solution.py:355
  25.9 10.3 %loss.3 = (f32[48,1024]{1,0:T(8,128)}, bf16[48,1024]{1,0:T(8,128)(2,1)}, bf16[48,1024]{1,0:T(8,128)(2,1)}, bf16[48,1024]{1,0:T(8,128)(2,1)}) custom-call(s32[4,64]{1,0:T(4,128)} %bitcast.19, s32[2,2048]{1,0:T(2,128)} %copy-done.5, s32[2,2048]{1,0:T(2,128)} %copy-done.8, s32[2,2048]{1,0:T(2,128)} %copy-done.7, s32[2,2048]{1,0:T(2,128)} %copy-done.6, ...), custom_call_target="tpu_custom_call" | custom-call | tf_op jit(solution)/shard_map/loss/pallas_call | solution.py:326
  36.3 0.7 %collective-permute-start.6 = (bf16[48,1024]{1,0:T(8,128)(2,1)}, bf16[48,1024]{1,0:T(8,128)(2,1)S(1)}, u32[]{:S(2)}, u32[]{:S(2)}) collective-permute-start(bf16[48,1024]{1,0:T(8,128)(2,1)} %get-tuple-element.21), channel_id=1, source_target_pairs={{0,4},{4,8},{8,12},{12,0},{1,5},{5,9},{9,13},{13,1},{2,6},{6,10},{... | collective-permute-start | bytes 294920 | tf_op jit(solution)/shard_map/ppermute | solution.py:355
  37.0 0.3 collective-permute-start.7
  37.3 0.0 collective-permute-done.3.refs_1_
  37.3 2.8 %collective-permute-start.8 = (bf16[48,1024]{1,0:T(8,128)(2,1)}, bf16[48,1024]{1,0:T(8,128)(2,1)S(1)}, u32[]{:S(2)}, u32[]{:S(2)}) collective-permute-start(bf16[48,1024]{1,0:T(8,128)(2,1)} %get-tuple-element.23), channel_id=1, source_target_pairs={{0,12},{4,0},{8,4},{12,8},{1,13},{5,1},{9,5},{13,9},{2,14},{6,2},{... | collective-permute-start | bytes 294920 | tf_op jit(solution)/shard_map/ppermute | solution.py:355
  40.1 0.0 collective-permute-done.4.refs_2_
  40.2 0.0 collective-permute-done.5.refs_3_
  40.2 0.0 copy-done.4
  40.2 0.0 copy-done.2
  40.2 0.0 copy-start
  40.2 1.6 %copy-done = bf16[8,8,128,128]{3,2,1,0:T(8,128)(2,1)S(1)} copy-done((bf16[8,8,128,128]{3,2,1,0:T(8,128)(2,1)S(1)}, bf16[8,8,128,128]{3,2,1,0:T(8,128)(2,1)}, u32[]{:S(2)}) %copy-start) | copy-done | bytes 2097176
  41.8 0.0 copy-start.3
  41.8 0.9 %copy-done.3 = f32[48,1024]{1,0:T(8,128)S(1)} copy-done((f32[48,1024]{1,0:T(8,128)S(1)}, f32[48,1024]{1,0:T(8,128)}, u32[]{:S(2)}) %copy-start.3) | copy-done | bytes 196632
  42.7 2.2 %net.2 = (f32[128,1024]{1,0:T(8,128)}, f32[2,1024]{1,0:T(2,128)S(1)}, f32[48,1024]{1,0:T(8,128)S(1)}) custom-call(s32[8,8]{1,0:T(8,128)S(1)} %copy-done.4, bf16[8,1024,128]{2,1,0:T(8,128)(2,1)S(1)} %bitcast.8, f32[80,1024]{1,0:T(8,128)S(1)} %copy-done.2, bf16[80,1024]{1,0:T(8,128)(2,1)S(1)} %collective-permute-done.3.refs_1_, ...), custom_call_target="tpu_custom_call" | custom-call | tf_op jit(solution)/shard_map/net/pallas_call | solution.py:286
  44.9 0.0 collective-permute-done.6.refs_1_
  45.0 1.6 %collective-permute-done.7.refs_2_ = bf16[48,1024]{1,0:T(8,128)(2,1)S(1)} collective-permute-done((bf16[48,1024]{1,0:T(8,128)(2,1)}, bf16[48,1024]{1,0:T(8,128)(2,1)S(1)}, u32[]{:S(2)}, u32[]{:S(2)}) %collective-permute-start.7) | collective-permute-done | bytes 98336 | tf_op jit(solution)/shard_map/ppermute | solution.py:355
  46.5 0.0 collective-permute-done.8.refs_3_
  46.5 0.0 copy-done.1
  46.5 1.8 %net.3 = (f32[128,1024]{1,0:T(8,128)}, f32[2,1024]{1,0:T(2,128)S(1)}) custom-call(s32[8,8]{1,0:T(8,128)S(1)} %copy-done.4, bf16[8,1024,128]{2,1,0:T(8,128)(2,1)S(1)} %bitcast.9, f32[48,1024]{1,0:T(8,128)S(1)} %get-tuple-element.20.refs_0_, bf16[48,1024]{1,0:T(8,128)(2,1)S(1)} %collective-permute-done.6.refs_1_, ...), custom_call_target="tpu_custom_call", output_to_operand_aliasing={{0}: (7, {})} | custom-call | tf_op jit(solution)/shard_map/net/pallas_call | solution.py:286
  48.4 0.1 collective-permute-start.11
  48.5 1.5 %collective-permute-start.10 = (f32[2,1024]{1,0:T(2,128)S(1)}, f32[2,1024]{1,0:T(2,128)S(1)}, u32[]{:S(2)}, u32[]{:S(2)}) collective-permute-start(f32[2,1024]{1,0:T(2,128)S(1)} %get-tuple-element.27), channel_id=1, source_target_pairs={{0,2},{1,3},{2,0},{3,1},{4,6},{5,7},{6,4},{7,5},{8,10},{9,11},{10,... | collective-permute-start | bytes 24584 | tf_op jit(solution)/shard_map/ppermute | solution.py:359
  50.0 0.3 collective-permute-start.9
  50.3 1.3 %collective-permute-done.11 = f32[2,1024]{1,0:T(2,128)S(1)} collective-permute-done((f32[2,1024]{1,0:T(2,128)S(1)}, f32[2,1024]{1,0:T(2,128)S(1)}, u32[]{:S(2)}, u32[]{:S(2)}) %collective-permute-start.11) | collective-permute-done | bytes 8224 | tf_op jit(solution)/shard_map/ppermute | solution.py:359
  51.6 0.6 %collective-permute-done.10 = f32[2,1024]{1,0:T(2,128)S(1)} collective-permute-done((f32[2,1024]{1,0:T(2,128)S(1)}, f32[2,1024]{1,0:T(2,128)S(1)}, u32[]{:S(2)}, u32[]{:S(2)}) %collective-permute-start.10) | collective-permute-done | bytes 8224 | tf_op jit(solution)/shard_map/ppermute | solution.py:359
  52.2 0.0 collective-permute-done.9
  52.2 0.6 %add_multiply_fusion = f32[2,1024]{1,0:T(2,128)} fusion(f32[2,1024]{1,0:T(2,128)S(1)} %collective-permute-done.10, f32[2,1024]{1,0:T(2,128)S(1)} %collective-permute-done.11, f32[2,1024]{1,0:T(2,128)S(1)} %get-tuple-element.27, f32[2,1024]{1,0:T(2,128)S(1)} %collective-permute-done.9), kind=kLoop, calls=%fused_computation.1 | loop fusion | flops 8192 | bytes 40960 | tf_op jit(solution)/shard_map/div | solution.py:435
  (1 shorter events, 0.0 us)
Async XLA Ops:
  1.4 3.1 %copy-start.5 = (s32[2,2048]{1,0:T(2,128)}, s32[2,2048]{1,0:T(2,128)S(1)}, u32[]{:S(2)}) copy-start(s32[2,2048]{1,0:T(2,128)S(1)} %pad_add_fusion.part.refs_0_) | copy-start | bytes 49156
  1.4 5.6 %collective-permute-start.2 = (s32[2,2048]{1,0:T(2,128)S(1)}, s32[2,2048]{1,0:T(2,128)S(1)}, u32[]{:S(2)}, u32[]{:S(2)}) collective-permute-start(s32[2,2048]{1,0:T(2,128)S(1)} %pad_add_fusion.part.refs_0_), channel_id=1, source_target_pairs={{0,3},{1,2},{2,1},{3,0},{4,7},{5,6},{6,5},{7,4},{8,11},{9,10},{10,... | collective-permute-start | bytes 49160 | tf_op jit(solution)/shard_map/ppermute | solution.py:359
  3.8 3.7 %collective-permute-start.1 = (s32[2,2048]{1,0:T(2,128)S(1)}, s32[2,2048]{1,0:T(2,128)S(1)}, u32[]{:S(2)}, u32[]{:S(2)}) collective-permute-start(s32[2,2048]{1,0:T(2,128)S(1)} %pad_add_fusion.part.refs_0_), channel_id=1, source_target_pairs={{0,2},{1,3},{2,0},{3,1},{4,6},{5,7},{6,4},{7,5},{8,10},{9,11},{10,... | collective-permute-start | bytes 49160 | tf_op jit(solution)/shard_map/ppermute | solution.py:359
  4.5 3.1 %collective-permute-start = (s32[2,2048]{1,0:T(2,128)S(1)}, s32[2,2048]{1,0:T(2,128)S(1)}, u32[]{:S(2)}, u32[]{:S(2)}) collective-permute-start(s32[2,2048]{1,0:T(2,128)S(1)} %pad_add_fusion.part.refs_0_), channel_id=1, source_target_pairs={{0,1},{1,0},{2,3},{3,2},{4,5},{5,4},{6,7},{7,6},{8,9},{9,8},{10,11... | collective-permute-start | bytes 49160 | tf_op jit(solution)/shard_map/ppermute | solution.py:359
  7.0 0.6 %copy-start.6 = (s32[2,2048]{1,0:T(2,128)}, s32[2,2048]{1,0:T(2,128)S(1)}, u32[]{:S(2)}) copy-start(s32[2,2048]{1,0:T(2,128)S(1)} %collective-permute-done.2.refs_3_) | copy-start | bytes 49156
  7.6 0.6 %copy-start.7 = (s32[2,2048]{1,0:T(2,128)}, s32[2,2048]{1,0:T(2,128)S(1)}, u32[]{:S(2)}) copy-start(s32[2,2048]{1,0:T(2,128)S(1)} %collective-permute-done.1.refs_2_) | copy-start | bytes 49156
  7.6 0.6 %copy-start.8 = (s32[2,2048]{1,0:T(2,128)}, s32[2,2048]{1,0:T(2,128)S(1)}, u32[]{:S(2)}) copy-start(s32[2,2048]{1,0:T(2,128)S(1)} %collective-permute-done.refs_1_) | copy-start | bytes 49156
  8.2 32.0 %copy-start.4 = (s32[8,8]{1,0:T(8,128)S(1)}, s32[8,8]{1,0:T(8,128)}, u32[]{:S(2)}) copy-start(s32[8,8]{1,0:T(8,128)} %pattern.3) | copy-start | bytes 772
  20.3 19.8 %copy-start.2 = (f32[80,1024]{1,0:T(8,128)S(1)}, f32[80,1024]{1,0:T(8,128)}, u32[]{:S(2)}) copy-start(f32[80,1024]{1,0:T(8,128)} %get-tuple-element.15.refs_0_) | copy-start | bytes 983044
  20.3 17.0 %collective-permute-start.3 = (bf16[80,1024]{1,0:T(8,128)(2,1)}, bf16[80,1024]{1,0:T(8,128)(2,1)S(1)}, u32[]{:S(2)}, u32[]{:S(2)}) collective-permute-start(bf16[80,1024]{1,0:T(8,128)(2,1)} %get-tuple-element.16), channel_id=1, source_target_pairs={{0,4},{4,8},{8,12},{12,0},{1,5},{5,9},{9,13},{13,1},{2,6},{6,10},{... | collective-permute-start | bytes 491528 | tf_op jit(solution)/shard_map/ppermute | solution.py:355
  22.0 18.2 %collective-permute-start.4 = (bf16[80,1024]{1,0:T(8,128)(2,1)}, bf16[80,1024]{1,0:T(8,128)(2,1)S(1)}, u32[]{:S(2)}, u32[]{:S(2)}) collective-permute-start(bf16[80,1024]{1,0:T(8,128)(2,1)} %get-tuple-element.17), channel_id=1, source_target_pairs={{0,8},{4,12},{8,0},{12,4},{1,9},{5,13},{9,1},{13,5},{2,10},{6,14},... | collective-permute-start | bytes 491528 | tf_op jit(solution)/shard_map/ppermute | solution.py:355
  24.6 15.6 %collective-permute-start.5 = (bf16[80,1024]{1,0:T(8,128)(2,1)}, bf16[80,1024]{1,0:T(8,128)(2,1)S(1)}, u32[]{:S(2)}, u32[]{:S(2)}) collective-permute-start(bf16[80,1024]{1,0:T(8,128)(2,1)} %get-tuple-element.18), channel_id=1, source_target_pairs={{0,12},{4,0},{8,4},{12,8},{1,13},{5,1},{9,5},{13,9},{2,14},{6,2},{... | collective-permute-start | bytes 491528 | tf_op jit(solution)/shard_map/ppermute | solution.py:355
  36.3 8.7 %collective-permute-start.6 = (bf16[48,1024]{1,0:T(8,128)(2,1)}, bf16[48,1024]{1,0:T(8,128)(2,1)S(1)}, u32[]{:S(2)}, u32[]{:S(2)}) collective-permute-start(bf16[48,1024]{1,0:T(8,128)(2,1)} %get-tuple-element.21), channel_id=1, source_target_pairs={{0,4},{4,8},{8,12},{12,0},{1,5},{5,9},{9,13},{13,1},{2,6},{6,10},{... | collective-permute-start | bytes 294920 | tf_op jit(solution)/shard_map/ppermute | solution.py:355
  37.0 9.5 %collective-permute-start.7 = (bf16[48,1024]{1,0:T(8,128)(2,1)}, bf16[48,1024]{1,0:T(8,128)(2,1)S(1)}, u32[]{:S(2)}, u32[]{:S(2)}) collective-permute-start(bf16[48,1024]{1,0:T(8,128)(2,1)} %get-tuple-element.22), channel_id=1, source_target_pairs={{0,8},{4,12},{8,0},{12,4},{1,9},{5,13},{9,1},{13,5},{2,10},{6,14},... | collective-permute-start | bytes 294920 | tf_op jit(solution)/shard_map/ppermute | solution.py:355
  37.3 9.2 %collective-permute-start.8 = (bf16[48,1024]{1,0:T(8,128)(2,1)}, bf16[48,1024]{1,0:T(8,128)(2,1)S(1)}, u32[]{:S(2)}, u32[]{:S(2)}) collective-permute-start(bf16[48,1024]{1,0:T(8,128)(2,1)} %get-tuple-element.23), channel_id=1, source_target_pairs={{0,12},{4,0},{8,4},{12,8},{1,13},{5,1},{9,5},{13,9},{2,14},{6,2},{... | collective-permute-start | bytes 294920 | tf_op jit(solution)/shard_map/ppermute | solution.py:355
  40.2 1.6 %copy-start = (bf16[8,8,128,128]{3,2,1,0:T(8,128)(2,1)S(1)}, bf16[8,8,128,128]{3,2,1,0:T(8,128)(2,1)}, u32[]{:S(2)}) copy-start(bf16[8,8,128,128]{3,2,1,0:T(8,128)(2,1)} %param.16) | copy-start | bytes 6291460
  41.8 0.9 %copy-start.3 = (f32[48,1024]{1,0:T(8,128)S(1)}, f32[48,1024]{1,0:T(8,128)}, u32[]{:S(2)}) copy-start(f32[48,1024]{1,0:T(8,128)} %get-tuple-element.19.refs_4_) | copy-start | bytes 589828
  42.7 3.8 %copy-start.1 = (bf16[8,8,128,128]{3,2,1,0:T(8,128)(2,1)S(1)}, bf16[8,8,128,128]{3,2,1,0:T(8,128)(2,1)}, u32[]{:S(2)}) copy-start(bf16[8,8,128,128]{3,2,1,0:T(8,128)(2,1)} %param.16) | copy-start | bytes 6291460
  48.4 3.2 %collective-permute-start.11 = (f32[2,1024]{1,0:T(2,128)S(1)}, f32[2,1024]{1,0:T(2,128)S(1)}, u32[]{:S(2)}, u32[]{:S(2)}) collective-permute-start(f32[2,1024]{1,0:T(2,128)S(1)} %get-tuple-element.27), channel_id=1, source_target_pairs={{0,3},{1,2},{2,1},{3,0},{4,7},{5,6},{6,5},{7,4},{8,11},{9,10},{10,... | collective-permute-start | bytes 24584 | tf_op jit(solution)/shard_map/ppermute | solution.py:359
  48.5 3.7 %collective-permute-start.10 = (f32[2,1024]{1,0:T(2,128)S(1)}, f32[2,1024]{1,0:T(2,128)S(1)}, u32[]{:S(2)}, u32[]{:S(2)}) collective-permute-start(f32[2,1024]{1,0:T(2,128)S(1)} %get-tuple-element.27), channel_id=1, source_target_pairs={{0,2},{1,3},{2,0},{3,1},{4,6},{5,7},{6,4},{7,5},{8,10},{9,11},{10,... | collective-permute-start | bytes 24584 | tf_op jit(solution)/shard_map/ppermute | solution.py:359
  50.0 2.2 %collective-permute-start.9 = (f32[2,1024]{1,0:T(2,128)S(1)}, f32[2,1024]{1,0:T(2,128)S(1)}, u32[]{:S(2)}, u32[]{:S(2)}) collective-permute-start(f32[2,1024]{1,0:T(2,128)S(1)} %get-tuple-element.27), channel_id=1, source_target_pairs={{0,1},{1,0},{2,3},{3,2},{4,5},{5,4},{6,7},{7,6},{8,9},{9,8},{10,11... | collective-permute-start | bytes 24584 | tf_op jit(solution)/shard_map/ppermute | solution.py:359

commit v8 on v7

--- a/solution.py
+++ b/solution.py
@@ -174,15 +174,14 @@
             for n in range(2):
                 pltpu.matmul_acc_lhs(sums[n], masked[parity][...], parity)
 
-        def weigh(step, parity):
-            latent = pltpu.matmul_pop(latents[parity])
+        def weigh(step, parity, latent):
             for j in range(2):
                 one = pl.ds(2 * step + j, 1)
                 here = slice(j * LANES, (j + 1) * LANES)
                 t = thr_ref[one, :] - latent[j * points : (j + 1) * points, here]
                 prob = weighted_prob(t, expo_ref[one, :]).astype(jnp.bfloat16)
-                part = lax.shift_right_logical(seg_ref[one, :], (2 * MXU).bit_length() - 1) - base * sub
-                part = jnp.where(part < 0, part + n_dest * sub, part) - chunk * group
+                part = lax.shift_right_logical(seg_ref[one, :], (2 * MXU).bit_length() - 1)
+                part = (part ^ (base * sub)) - chunk * group
                 part = jnp.broadcast_to(part, (ROWS, LANES)).astype(jnp.int16)
                 for d in range(group):
                     mine = part == jnp.int16(d)
@@ -192,12 +191,13 @@
                         )
 
         def stage(step, parity, ahead=True, behind=True):
+            latent = pltpu.matmul_pop(latents[parity])
             push_onehot(step, parity)
             if behind:
                 add_up(1 - parity)
             if ahead:
                 project(step + 1, 1 - parity)
-            weigh(step, parity)
+            weigh(step, parity, latent)
 
         project(0, 0)
         stage(0, 0, behind=False)
@@ -418,7 +418,7 @@
             direct,
         )
         if direct:
-            received = [partial[0]] + [shifted(partial[k], "wide", k) for k in range(1, n_dest)]
+            received = [partial[0]] + [swapped(partial[k], "wide", k) for k in [*range(2, n_dest), *range(1, min(2, n_dest))]]
         else:
             received = [lax.all_to_all(partial[0], "wide", split_axis=0, concat_axis=0, tiled=True)]
         chunks.append((first, chunk, received))

time: 53.3 us -> 52.8 us (level)
  starting transfers between devices: 14.5 us -> 13.5 us
    ppermute x6 -> x0, starting transfers between devices: 9.45 us -> none  [shifted(): return lax.ppermute(x, axis, [(i, (i + k) % n) for i in range(n)])]
    ppermute x6 -> x12, starting transfers between devices: 5.04 us -> 13.5 us  [swapped(): lax.ppermute(x, axis, [(i, i ^ k) for i in range(lax.axis_size(axis))])]
    ppermute x6 -> x12, waiting for transfers between devices: 2.42 us -> 4.36 us  [swapped(): lax.ppermute(x, axis, [(i, i ^ k) for i in range(lax.axis_size(axis))])]
    ppermute x6 -> x0, waiting for transfers between devices: 1.59 us -> none  [shifted(): return lax.ppermute(x, axis, [(i, (i + k) % n) for i in range(n)])]
  transfers between devices with their start and end apart: 12 -> 12, of which waited for: 4 -> 5; matrix products, arithmetic and copies ran while one was open for 0% -> 0% of each run, Pallas kernels for 29% -> 29%
where the time goes in v8:
time: 52.8 us; the launch traced here: 52.1 us
  Pallas kernels  29.1 us (55%)
  starting transfers between devices  13.5 us (26%)
  waiting for transfers between devices  4.36 us (8%)
  local copies, waits for them, and re-layouts  3.13 us (6%)
  other arithmetic  1.34 us (3%)
  between operations  0.74 us (1%)
    pallas_call x2, Pallas kernels, loss_call(): pl.pallas_call(functools.partial(loss_kernel, n_parts, n_dest, split, dir...  22.5 us
    ppermute x12, starting transfers between devices, swapped(): lax.ppermute(x, axis, [(i, i ^ k) for i in range(lax.axis_size(axis))])  13.5 us
    ppermute x12, waiting for transfers between devices, swapped(): lax.ppermute(x, axis, [(i, i ^ k) for i in range(lax.axis_size(axis))])  4.36 us
    pallas_call x2, Pallas kernels, net_call(): pl.pallas_call(functools.partial(net_kernel, first_point, len(received),...  4.07 us
    unnamed x18, local copies, waits for them, and re-layouts  3.13 us
    pallas_call x1, Pallas kernels, body(): pl.pallas_call(functools.partial(panel_kernel, points), out_shape=jax.Sha...  2.51 us
  transfers between devices with their start and end apart: 12, of which 5 were waited for; matrix products, arithmetic and copies ran while one was open for 0% of the time, Pallas kernels for 29%

profile of v8, /device:TPU:0, one launch (start us, length us, event | category | flops | bytes accessed | tf_op | source)
XLA Modules:
  0.0 52.1 jit_solution(9656878071887866703)
XLA Ops:
  0.6 0.7 %pad_add_fusion.part.refs_0_ = s32[2,2048]{1,0:T(2,128)S(1)} fusion(s32[1,2048]{1,0:T(1,128)} %bitcast.20, s32[1,2048]{1,0:T(1,128)} %bitcast.21), kind=kLoop, calls=%fused_computation | loop fusion | flops 4096 | bytes 32768 | tf_op jit(solution)/shard_map/stack | solution.py:386
  1.4 0.0 copy-start.5
  1.4 2.4 %collective-permute-start.2 = (s32[2,2048]{1,0:T(2,128)S(1)}, s32[2,2048]{1,0:T(2,128)S(1)}, u32[]{:S(2)}, u32[]{:S(2)}) collective-permute-start(s32[2,2048]{1,0:T(2,128)S(1)} %pad_add_fusion.part.refs_0_), channel_id=1, source_target_pairs={{0,3},{1,2},{2,1},{3,0},{4,7},{5,6},{6,5},{7,4},{8,11},{9,10},{10,... | collective-permute-start | bytes 49160 | tf_op jit(solution)/shard_map/ppermute | solution.py:359
  3.8 0.6 %collective-permute-start.1 = (s32[2,2048]{1,0:T(2,128)S(1)}, s32[2,2048]{1,0:T(2,128)S(1)}, u32[]{:S(2)}, u32[]{:S(2)}) collective-permute-start(s32[2,2048]{1,0:T(2,128)S(1)} %pad_add_fusion.part.refs_0_), channel_id=1, source_target_pairs={{0,2},{1,3},{2,0},{3,1},{4,6},{5,7},{6,4},{7,5},{8,10},{9,11},{10,... | collective-permute-start | bytes 49160 | tf_op jit(solution)/shard_map/ppermute | solution.py:359
  4.5 0.0 collective-permute-start
  4.5 0.0 copy-done.5
  4.5 2.5 %panel.1.refs_0_ = bf16[2,16,80,128]{3,2,1,0:T(8,128)(2,1)} custom-call(s32[2,2048]{1,0:T(2,128)} %copy-done.5), custom_call_target="tpu_custom_call" | custom-call | tf_op jit(solution)/shard_map/panel/pallas_call | solution.py:389
  7.0 0.0 collective-permute-done.2.refs_3_
  7.0 0.0 copy-start.6
  7.0 0.5 %collective-permute-done.1.refs_2_ = s32[2,2048]{1,0:T(2,128)S(1)} collective-permute-done((s32[2,2048]{1,0:T(2,128)S(1)}, s32[2,2048]{1,0:T(2,128)S(1)}, u32[]{:S(2)}, u32[]{:S(2)}) %collective-permute-start.1) | collective-permute-done | bytes 16416 | tf_op jit(solution)/shard_map/ppermute | solution.py:359
  7.6 0.0 copy-start.7
  7.6 0.0 collective-permute-done.refs_1_
  7.6 0.0 copy-start.8
  7.6 0.0 copy-done.6
  7.6 0.5 %copy-done.7 = s32[2,2048]{1,0:T(2,128)} copy-done((s32[2,2048]{1,0:T(2,128)}, s32[2,2048]{1,0:T(2,128)S(1)}, u32[]{:S(2)}) %copy-start.7) | copy-done | bytes 16408
  8.2 0.0 copy-done.8
  8.2 0.0 copy-start.4
  8.2 12.2 %loss.2 = (f32[80,1024]{1,0:T(8,128)}, bf16[80,1024]{1,0:T(8,128)(2,1)}, bf16[80,1024]{1,0:T(8,128)(2,1)}, bf16[80,1024]{1,0:T(8,128)(2,1)}) custom-call(s32[4,64]{1,0:T(4,128)} %bitcast.18, bf16[2,16,80,128]{3,2,1,0:T(8,128)(2,1)} %panel.1.refs_0_, s32[2,2048]{1,0:T(2,128)} %copy-done.8, s32[2,2048]{1,0:T(2,128)} %copy-done.7, s32[2,2048]{1,0:T(2,128)} %copy-done.6, ...), custom_call_target="tpu_custom_call" | custom-call | tf_op jit(solution)/shard_map/loss/pallas_call | solution.py:326
  20.3 0.0 copy-start.2
  20.4 2.6 %collective-permute-start.3 = (bf16[80,1024]{1,0:T(8,128)(2,1)}, bf16[80,1024]{1,0:T(8,128)(2,1)S(1)}, u32[]{:S(2)}, u32[]{:S(2)}) collective-permute-start(bf16[80,1024]{1,0:T(8,128)(2,1)} %get-tuple-element.16), channel_id=1, source_target_pairs={{0,8},{4,12},{8,0},{12,4},{1,9},{5,13},{9,1},{13,5},{2,10},{6,14},... | collective-permute-start | bytes 491528 | tf_op jit(solution)/shard_map/ppermute | solution.py:359
  23.0 1.3 %collective-permute-start.4 = (bf16[80,1024]{1,0:T(8,128)(2,1)}, bf16[80,1024]{1,0:T(8,128)(2,1)S(1)}, u32[]{:S(2)}, u32[]{:S(2)}) collective-permute-start(bf16[80,1024]{1,0:T(8,128)(2,1)} %get-tuple-element.17), channel_id=1, source_target_pairs={{0,12},{4,8},{8,4},{12,0},{1,13},{5,9},{9,5},{13,1},{2,14},{6,10},... | collective-permute-start | bytes 491528 | tf_op jit(solution)/shard_map/ppermute | solution.py:359
  24.3 0.2 collective-permute-start.5
  24.6 10.3 %loss.3 = (f32[48,1024]{1,0:T(8,128)}, bf16[48,1024]{1,0:T(8,128)(2,1)}, bf16[48,1024]{1,0:T(8,128)(2,1)}, bf16[48,1024]{1,0:T(8,128)(2,1)}) custom-call(s32[4,64]{1,0:T(4,128)} %bitcast.19, s32[2,2048]{1,0:T(2,128)} %copy-done.5, s32[2,2048]{1,0:T(2,128)} %copy-done.8, s32[2,2048]{1,0:T(2,128)} %copy-done.7, s32[2,2048]{1,0:T(2,128)} %copy-done.6, ...), custom_call_target="tpu_custom_call" | custom-call | tf_op jit(solution)/shard_map/loss/pallas_call | solution.py:326
  34.9 2.9 %collective-permute-start.6 = (bf16[48,1024]{1,0:T(8,128)(2,1)}, bf16[48,1024]{1,0:T(8,128)(2,1)S(1)}, u32[]{:S(2)}, u32[]{:S(2)}) collective-permute-start(bf16[48,1024]{1,0:T(8,128)(2,1)} %get-tuple-element.21), channel_id=1, source_target_pairs={{0,8},{4,12},{8,0},{12,4},{1,9},{5,13},{9,1},{13,5},{2,10},{6,14},... | collective-permute-start | bytes 294920 | tf_op jit(solution)/shard_map/ppermute | solution.py:359
  37.8 1.3 %collective-permute-start.7 = (bf16[48,1024]{1,0:T(8,128)(2,1)}, bf16[48,1024]{1,0:T(8,128)(2,1)S(1)}, u32[]{:S(2)}, u32[]{:S(2)}) collective-permute-start(bf16[48,1024]{1,0:T(8,128)(2,1)} %get-tuple-element.22), channel_id=1, source_target_pairs={{0,12},{4,8},{8,4},{12,0},{1,13},{5,9},{9,5},{13,1},{2,14},{6,10},... | collective-permute-start | bytes 294920 | tf_op jit(solution)/shard_map/ppermute | solution.py:359
  39.1 0.0 collective-permute-done.3.refs_1_
  39.1 0.0 collective-permute-start.8
  39.1 0.0 collective-permute-done.4.refs_2_
  39.1 0.0 collective-permute-done.5.refs_3_
  39.1 0.0 copy-done.4
  39.2 0.0 copy-done.2
  39.2 0.0 copy-start
  39.2 1.6 %copy-done = bf16[8,8,128,128]{3,2,1,0:T(8,128)(2,1)S(1)} copy-done((bf16[8,8,128,128]{3,2,1,0:T(8,128)(2,1)S(1)}, bf16[8,8,128,128]{3,2,1,0:T(8,128)(2,1)}, u32[]{:S(2)}) %copy-start) | copy-done | bytes 2097176
  40.8 0.0 copy-start.3
  40.8 0.9 %copy-done.3 = f32[48,1024]{1,0:T(8,128)S(1)} copy-done((f32[48,1024]{1,0:T(8,128)S(1)}, f32[48,1024]{1,0:T(8,128)}, u32[]{:S(2)}) %copy-start.3) | copy-done | bytes 196632
  41.7 2.2 %net.2 = (f32[128,1024]{1,0:T(8,128)}, f32[2,1024]{1,0:T(2,128)S(1)}, f32[48,1024]{1,0:T(8,128)S(1)}) custom-call(s32[8,8]{1,0:T(8,128)S(1)} %copy-done.4, bf16[8,1024,128]{2,1,0:T(8,128)(2,1)S(1)} %bitcast.8, f32[80,1024]{1,0:T(8,128)S(1)} %copy-done.2, bf16[80,1024]{1,0:T(8,128)(2,1)S(1)} %collective-permute-done.3.refs_1_, ...), custom_call_target="tpu_custom_call" | custom-call | tf_op jit(solution)/shard_map/net/pallas_call | solution.py:286
  43.9 1.6 %collective-permute-done.6.refs_1_ = bf16[48,1024]{1,0:T(8,128)(2,1)S(1)} collective-permute-done((bf16[48,1024]{1,0:T(8,128)(2,1)}, bf16[48,1024]{1,0:T(8,128)(2,1)S(1)}, u32[]{:S(2)}, u32[]{:S(2)}) %collective-permute-start.6) | collective-permute-done | bytes 98336 | tf_op jit(solution)/shard_map/ppermute | solution.py:359
  45.5 0.0 collective-permute-done.7.refs_2_
  45.5 0.4 collective-permute-done.8.refs_3_
  45.9 0.0 copy-done.1
  45.9 1.8 %net.3 = (f32[128,1024]{1,0:T(8,128)}, f32[2,1024]{1,0:T(2,128)S(1)}) custom-call(s32[8,8]{1,0:T(8,128)S(1)} %copy-done.4, bf16[8,1024,128]{2,1,0:T(8,128)(2,1)S(1)} %bitcast.9, f32[48,1024]{1,0:T(8,128)S(1)} %get-tuple-element.20.refs_0_, bf16[48,1024]{1,0:T(8,128)(2,1)S(1)} %collective-permute-done.6.refs_1_, ...), custom_call_target="tpu_custom_call", output_to_operand_aliasing={{0}: (7, {})} | custom-call | tf_op jit(solution)/shard_map/net/pallas_call | solution.py:286
  47.7 0.1 collective-permute-start.11
  47.8 1.4 %collective-permute-start.10 = (f32[2,1024]{1,0:T(2,128)S(1)}, f32[2,1024]{1,0:T(2,128)S(1)}, u32[]{:S(2)}, u32[]{:S(2)}) collective-permute-start(f32[2,1024]{1,0:T(2,128)S(1)} %get-tuple-element.27), channel_id=1, source_target_pairs={{0,2},{1,3},{2,0},{3,1},{4,6},{5,7},{6,4},{7,5},{8,10},{9,11},{10,... | collective-permute-start | bytes 24584 | tf_op jit(solution)/shard_map/ppermute | solution.py:359
  49.2 0.5 collective-permute-start.9
  49.6 1.2 %collective-permute-done.11 = f32[2,1024]{1,0:T(2,128)S(1)} collective-permute-done((f32[2,1024]{1,0:T(2,128)S(1)}, f32[2,1024]{1,0:T(2,128)S(1)}, u32[]{:S(2)}, u32[]{:S(2)}) %collective-permute-start.11) | collective-permute-done | bytes 8224 | tf_op jit(solution)/shard_map/ppermute | solution.py:359
  50.8 0.7 %collective-permute-done.10 = f32[2,1024]{1,0:T(2,128)S(1)} collective-permute-done((f32[2,1024]{1,0:T(2,128)S(1)}, f32[2,1024]{1,0:T(2,128)S(1)}, u32[]{:S(2)}, u32[]{:S(2)}) %collective-permute-start.10) | collective-permute-done | bytes 8224 | tf_op jit(solution)/shard_map/ppermute | solution.py:359
  51.5 0.0 collective-permute-done.9
  51.5 0.6 %add_multiply_fusion = f32[2,1024]{1,0:T(2,128)} fusion(f32[2,1024]{1,0:T(2,128)S(1)} %collective-permute-done.10, f32[2,1024]{1,0:T(2,128)S(1)} %collective-permute-done.11, f32[2,1024]{1,0:T(2,128)S(1)} %get-tuple-element.27, f32[2,1024]{1,0:T(2,128)S(1)} %collective-permute-done.9), kind=kLoop, calls=%fused_computation.1 | loop fusion | flops 8192 | bytes 40960 | tf_op jit(solution)/shard_map/div | solution.py:435
  (1 shorter events, 0.0 us)
Async XLA Ops:
  1.4 3.1 %copy-start.5 = (s32[2,2048]{1,0:T(2,128)}, s32[2,2048]{1,0:T(2,128)S(1)}, u32[]{:S(2)}) copy-start(s32[2,2048]{1,0:T(2,128)S(1)} %pad_add_fusion.part.refs_0_) | copy-start | bytes 49156
  1.4 5.6 %collective-permute-start.2 = (s32[2,2048]{1,0:T(2,128)S(1)}, s32[2,2048]{1,0:T(2,128)S(1)}, u32[]{:S(2)}, u32[]{:S(2)}) collective-permute-start(s32[2,2048]{1,0:T(2,128)S(1)} %pad_add_fusion.part.refs_0_), channel_id=1, source_target_pairs={{0,3},{1,2},{2,1},{3,0},{4,7},{5,6},{6,5},{7,4},{8,11},{9,10},{10,... | collective-permute-start | bytes 49160 | tf_op jit(solution)/shard_map/ppermute | solution.py:359
  3.8 3.7 %collective-permute-start.1 = (s32[2,2048]{1,0:T(2,128)S(1)}, s32[2,2048]{1,0:T(2,128)S(1)}, u32[]{:S(2)}, u32[]{:S(2)}) collective-permute-start(s32[2,2048]{1,0:T(2,128)S(1)} %pad_add_fusion.part.refs_0_), channel_id=1, source_target_pairs={{0,2},{1,3},{2,0},{3,1},{4,6},{5,7},{6,4},{7,5},{8,10},{9,11},{10,... | collective-permute-start | bytes 49160 | tf_op jit(solution)/shard_map/ppermute | solution.py:359
  4.5 3.1 %collective-permute-start = (s32[2,2048]{1,0:T(2,128)S(1)}, s32[2,2048]{1,0:T(2,128)S(1)}, u32[]{:S(2)}, u32[]{:S(2)}) collective-permute-start(s32[2,2048]{1,0:T(2,128)S(1)} %pad_add_fusion.part.refs_0_), channel_id=1, source_target_pairs={{0,1},{1,0},{2,3},{3,2},{4,5},{5,4},{6,7},{7,6},{8,9},{9,8},{10,11... | collective-permute-start | bytes 49160 | tf_op jit(solution)/shard_map/ppermute | solution.py:359
  7.0 0.6 %copy-start.6 = (s32[2,2048]{1,0:T(2,128)}, s32[2,2048]{1,0:T(2,128)S(1)}, u32[]{:S(2)}) copy-start(s32[2,2048]{1,0:T(2,128)S(1)} %collective-permute-done.2.refs_3_) | copy-start | bytes 49156
  7.6 0.6 %copy-start.7 = (s32[2,2048]{1,0:T(2,128)}, s32[2,2048]{1,0:T(2,128)S(1)}, u32[]{:S(2)}) copy-start(s32[2,2048]{1,0:T(2,128)S(1)} %collective-permute-done.1.refs_2_) | copy-start | bytes 49156
  7.6 0.6 %copy-start.8 = (s32[2,2048]{1,0:T(2,128)}, s32[2,2048]{1,0:T(2,128)S(1)}, u32[]{:S(2)}) copy-start(s32[2,2048]{1,0:T(2,128)S(1)} %collective-permute-done.refs_1_) | copy-start | bytes 49156
  8.2 31.0 %copy-start.4 = (s32[8,8]{1,0:T(8,128)S(1)}, s32[8,8]{1,0:T(8,128)}, u32[]{:S(2)}) copy-start(s32[8,8]{1,0:T(8,128)} %pattern.3) | copy-start | bytes 772
  20.3 18.8 %copy-start.2 = (f32[80,1024]{1,0:T(8,128)S(1)}, f32[80,1024]{1,0:T(8,128)}, u32[]{:S(2)}) copy-start(f32[80,1024]{1,0:T(8,128)} %get-tuple-element.15.refs_0_) | copy-start | bytes 983044
  20.4 18.8 %collective-permute-start.3 = (bf16[80,1024]{1,0:T(8,128)(2,1)}, bf16[80,1024]{1,0:T(8,128)(2,1)S(1)}, u32[]{:S(2)}, u32[]{:S(2)}) collective-permute-start(bf16[80,1024]{1,0:T(8,128)(2,1)} %get-tuple-element.16), channel_id=1, source_target_pairs={{0,8},{4,12},{8,0},{12,4},{1,9},{5,13},{9,1},{13,5},{2,10},{6,14},... | collective-permute-start | bytes 491528 | tf_op jit(solution)/shard_map/ppermute | solution.py:359
  23.0 16.1 %collective-permute-start.4 = (bf16[80,1024]{1,0:T(8,128)(2,1)}, bf16[80,1024]{1,0:T(8,128)(2,1)S(1)}, u32[]{:S(2)}, u32[]{:S(2)}) collective-permute-start(bf16[80,1024]{1,0:T(8,128)(2,1)} %get-tuple-element.17), channel_id=1, source_target_pairs={{0,12},{4,8},{8,4},{12,0},{1,13},{5,9},{9,5},{13,1},{2,14},{6,10},... | collective-permute-start | bytes 491528 | tf_op jit(solution)/shard_map/ppermute | solution.py:359
  24.3 14.8 %collective-permute-start.5 = (bf16[80,1024]{1,0:T(8,128)(2,1)}, bf16[80,1024]{1,0:T(8,128)(2,1)S(1)}, u32[]{:S(2)}, u32[]{:S(2)}) collective-permute-start(bf16[80,1024]{1,0:T(8,128)(2,1)} %get-tuple-element.18), channel_id=1, source_target_pairs={{0,4},{4,0},{8,12},{12,8},{1,5},{5,1},{9,13},{13,9},{2,6},{6,2},{1... | collective-permute-start | bytes 491528 | tf_op jit(solution)/shard_map/ppermute | solution.py:359
  34.9 10.6 %collective-permute-start.6 = (bf16[48,1024]{1,0:T(8,128)(2,1)}, bf16[48,1024]{1,0:T(8,128)(2,1)S(1)}, u32[]{:S(2)}, u32[]{:S(2)}) collective-permute-start(bf16[48,1024]{1,0:T(8,128)(2,1)} %get-tuple-element.21), channel_id=1, source_target_pairs={{0,8},{4,12},{8,0},{12,4},{1,9},{5,13},{9,1},{13,5},{2,10},{6,14},... | collective-permute-start | bytes 294920 | tf_op jit(solution)/shard_map/ppermute | solution.py:359
  37.8 7.7 %collective-permute-start.7 = (bf16[48,1024]{1,0:T(8,128)(2,1)}, bf16[48,1024]{1,0:T(8,128)(2,1)S(1)}, u32[]{:S(2)}, u32[]{:S(2)}) collective-permute-start(bf16[48,1024]{1,0:T(8,128)(2,1)} %get-tuple-element.22), channel_id=1, source_target_pairs={{0,12},{4,8},{8,4},{12,0},{1,13},{5,9},{9,5},{13,1},{2,14},{6,10},... | collective-permute-start | bytes 294920 | tf_op jit(solution)/shard_map/ppermute | solution.py:359
  39.1 6.7 %collective-permute-start.8 = (bf16[48,1024]{1,0:T(8,128)(2,1)}, bf16[48,1024]{1,0:T(8,128)(2,1)S(1)}, u32[]{:S(2)}, u32[]{:S(2)}) collective-permute-start(bf16[48,1024]{1,0:T(8,128)(2,1)} %get-tuple-element.23), channel_id=1, source_target_pairs={{0,4},{4,0},{8,12},{12,8},{1,5},{5,1},{9,13},{13,9},{2,6},{6,2},{1... | collective-permute-start | bytes 294920 | tf_op jit(solution)/shard_map/ppermute | solution.py:359
  39.2 1.6 %copy-start = (bf16[8,8,128,128]{3,2,1,0:T(8,128)(2,1)S(1)}, bf16[8,8,128,128]{3,2,1,0:T(8,128)(2,1)}, u32[]{:S(2)}) copy-start(bf16[8,8,128,128]{3,2,1,0:T(8,128)(2,1)} %param.16) | copy-start | bytes 6291460
  40.8 0.9 %copy-start.3 = (f32[48,1024]{1,0:T(8,128)S(1)}, f32[48,1024]{1,0:T(8,128)}, u32[]{:S(2)}) copy-start(f32[48,1024]{1,0:T(8,128)} %get-tuple-element.19.refs_4_) | copy-start | bytes 589828
  41.7 4.2 %copy-start.1 = (bf16[8,8,128,128]{3,2,1,0:T(8,128)(2,1)S(1)}, bf16[8,8,128,128]{3,2,1,0:T(8,128)(2,1)}, u32[]{:S(2)}) copy-start(bf16[8,8,128,128]{3,2,1,0:T(8,128)(2,1)} %param.16) | copy-start | bytes 6291460
  47.7 3.1 %collective-permute-start.11 = (f32[2,1024]{1,0:T(2,128)S(1)}, f32[2,1024]{1,0:T(2,128)S(1)}, u32[]{:S(2)}, u32[]{:S(2)}) collective-permute-start(f32[2,1024]{1,0:T(2,128)S(1)} %get-tuple-element.27), channel_id=1, source_target_pairs={{0,3},{1,2},{2,1},{3,0},{4,7},{5,6},{6,5},{7,4},{8,11},{9,10},{10,... | collective-permute-start | bytes 24584 | tf_op jit(solution)/shard_map/ppermute | solution.py:359
  47.8 3.7 %collective-permute-start.10 = (f32[2,1024]{1,0:T(2,128)S(1)}, f32[2,1024]{1,0:T(2,128)S(1)}, u32[]{:S(2)}, u32[]{:S(2)}) collective-permute-start(f32[2,1024]{1,0:T(2,128)S(1)} %get-tuple-element.27), channel_id=1, source_target_pairs={{0,2},{1,3},{2,0},{3,1},{4,6},{5,7},{6,4},{7,5},{8,10},{9,11},{10,... | collective-permute-start | bytes 24584 | tf_op jit(solution)/shard_map/ppermute | solution.py:359
  49.2 2.3 %collective-permute-start.9 = (f32[2,1024]{1,0:T(2,128)S(1)}, f32[2,1024]{1,0:T(2,128)S(1)}, u32[]{:S(2)}, u32[]{:S(2)}) collective-permute-start(f32[2,1024]{1,0:T(2,128)S(1)} %get-tuple-element.27), channel_id=1, source_target_pairs={{0,1},{1,0},{2,3},{3,2},{4,5},{5,4},{6,7},{7,6},{8,9},{9,8},{10,11... | collective-permute-start | bytes 24584 | tf_op jit(solution)/shard_map/ppermute | solution.py:359
